TPU v7x, 32 devices: a whole 2x2x4 slice. The times are simulated.
32 devices in a mesh: dp: 16 (over z, y, core), mp: 2 (over x).
Axes of the slice: x: 2, y: 2, z: 4, core: 2. Of those that a mesh axis runs over, the one named last changes fastest.
Arguments:
- tokens: bfloat16 [4, 16, 1024, 1024], P(None, 'dp', 'mp'), may hold values from -6 to 6
- lengths: int32 [4, 16], P(None, 'dp'), may hold values from 128 to 1024, as said below
- timesteps: int32 [4, 16], P(None, 'dp'), may hold values from 0 to 999
- norm_gains: float32 [2, 1024], replicated, may hold values from 0.5 to 1.5
- time_weight: float32 [256, 2048], replicated, may hold values from -0.375 to 0.375
- qkv_weight: bfloat16 [3, 1024, 1024], P(None, None, 'mp'), may hold values from -0.1875 to 0.1875
- out_weight: bfloat16 [1024, 1024], P('mp'), may hold values from -1.5 to 1.5
- up_weight: bfloat16 [1024, 4096], P(None, 'mp'), may hold values from -0.1875 to 0.1875
- down_weight: bfloat16 [4096, 1024], P('mp'), may hold values from -0.09375 to 0.09375
- cotangent: bfloat16 [4, 16, 1024, 1024], P(None, 'dp', 'mp'), may hold values from -6 to 6
Outputs:
- output: bfloat16 [4, 16, 1024, 1024], P(None, 'dp', 'mp')
- input_grad: bfloat16 [4, 16, 1024, 1024], P(None, 'dp', 'mp')
- qkv_grad: float32 [3, 1024, 1024], P(None, 'dp', 'mp')
- out_grad: float32 [1024, 1024], P('mp', 'dp')
- up_grad: float32 [1024, 4096], P('dp', 'mp')
- down_grad: float32 [4096, 1024], P('mp', 'dp')
- gains_grad: float32 [2, 1024], P(None, ('dp', 'mp'))
- time_grad: float32 [256, 2048], P(None, ('dp', 'mp'))
Inputs may be any that keep to these rules, and one draw needn't show every extreme that they name: `lengths`: in every micro-batch some sequence has all 1024 positions live.
All inputs are finite; a program needn't handle non-finite values.
Results may differ from a plain program's by a relative error of at most 0.02.
Values may be sent and summed in bfloat16 or wider, within the bound.
No kernel may reach another device: no remote copies, remote signals or barrier semaphores. Data moves between devices by JAX's collectives and lax.ppermute only.
A program may use at most 256 MiB of HBM per device.

v0:
```python
import math

import jax
import jax.numpy as jnp
from jax import lax
from jax.sharding import PartitionSpec as P

HEAD = 64
TEMB = 256


def sinusoid(step_ids):
    half_width = TEMB // 2
    freqs = jnp.exp(-math.log(10000.0) * jnp.arange(half_width, dtype=jnp.float32) / half_width)
    angles = step_ids.astype(jnp.float32)[:, None] * freqs[None, :]
    return jnp.concatenate([jnp.sin(angles), jnp.cos(angles)], axis=1)


def normed(values, gain, scale):
    center = values - jnp.mean(values, axis=-1, keepdims=True)
    spread = jnp.mean(center * center, axis=-1, keepdims=True)
    return center * lax.rsqrt(spread + 1e-05) * gain * (1.0 + scale)


def exact_gelu(values):
    return jax.nn.gelu(values, approximate=False)


def per_device(
    tokens,
    lengths,
    timesteps,
    norm_gains,
    time_weight,
    qkv_weight,
    out_weight,
    up_weight,
    down_weight,
    cotangent,
):
    micro_count, seq_dev, row_count, model_width = tokens.shape
    item_count = micro_count * seq_dev
    seq_len = row_count * lax.axis_size("mp")
    heads_dev = qkv_weight.shape[2] // HEAD
    block_rows = min(512, seq_len)
    block_count = seq_len // block_rows
    key_pos = jnp.arange(seq_len)
    feats = sinusoid(timesteps.reshape(item_count))
    pairs = jnp.dot(feats, time_weight, precision=lax.Precision.HIGHEST)
    token_items = tokens.reshape(item_count, row_count, model_width)
    cot_items = cotangent.reshape(item_count, row_count, model_width)
    len_items = lengths.reshape(item_count)

    def masked_scores(query_block, key_rows, key_valid):
        raw_scores = (
            jnp.einsum("qhd,khd->hqk", query_block, key_rows, preferred_element_type=jnp.float32)
            * 0.125
        )
        return jnp.where(key_valid[None, None, :], raw_scores, -1e30)

    def step_item(totals, packed):
        tok_rows, cot_rows, seq_length, seq_pair = packed
        scale_a = seq_pair[:model_width]
        scale_b = seq_pair[model_width:]
        key_valid = key_pos < seq_length
        inputs_f = tok_rows.astype(jnp.float32)
        norm_a = normed(inputs_f, norm_gains[0], scale_a)
        hidden_a = lax.all_gather(norm_a.astype(jnp.bfloat16), "mp", axis=0, tiled=True)
        qkv_all = jnp.einsum(
            "td,cde->cte", hidden_a, qkv_weight, preferred_element_type=jnp.float32
        ).astype(jnp.bfloat16)
        queries = qkv_all[0].reshape(seq_len, heads_dev, HEAD)
        key_rows = qkv_all[1].reshape(seq_len, heads_dev, HEAD)
        values = qkv_all[2].reshape(seq_len, heads_dev, HEAD)
        query_blocks = queries.reshape(block_count, block_rows, heads_dev, HEAD)

        def attend(query_block):
            scores = masked_scores(query_block, key_rows, key_valid)
            row_max = jnp.max(scores, axis=-1, keepdims=True)
            expo = jnp.exp(scores - row_max)
            row_sum = jnp.sum(expo, axis=-1, keepdims=True)
            probs = (expo / row_sum).astype(jnp.bfloat16)
            mixed = jnp.einsum("hqk,khd->qhd", probs, values, preferred_element_type=jnp.float32)
            return (mixed.astype(jnp.bfloat16), row_max[..., 0] + jnp.log(row_sum[..., 0]))

        mixed_blocks, log_sums = lax.map(attend, query_blocks)
        mixed_heads = mixed_blocks.reshape(seq_len, heads_dev * HEAD)
        attn_branch = lax.psum_scatter(
            jnp.dot(mixed_heads, out_weight, preferred_element_type=jnp.float32).astype(
                jnp.bfloat16
            ),
            "mp",
            scatter_dimension=0,
            tiled=True,
        ).astype(jnp.float32)
        resid = inputs_f + attn_branch
        norm_b = normed(resid, norm_gains[1], scale_b)
        hidden_b = lax.all_gather(norm_b.astype(jnp.bfloat16), "mp", axis=0, tiled=True)
        up_proj = jnp.dot(hidden_b, up_weight, preferred_element_type=jnp.float32)
        activated = exact_gelu(up_proj).astype(jnp.bfloat16)
        mlp_branch = lax.psum_scatter(
            jnp.dot(activated, down_weight, preferred_element_type=jnp.float32).astype(
                jnp.bfloat16
            ),
            "mp",
            scatter_dimension=0,
            tiled=True,
        ).astype(jnp.float32)
        layer_out = (resid + mlp_branch).astype(jnp.bfloat16)
        cot_all = lax.all_gather(cot_rows, "mp", axis=0, tiled=True)
        d_act = jnp.einsum("td,fd->tf", cot_all, down_weight, preferred_element_type=jnp.float32)
        grad_down = jnp.einsum("tf,td->fd", activated, cot_all, preferred_element_type=jnp.float32)
        gelu_out, gelu_pull = jax.vjp(exact_gelu, up_proj)
        d_up = gelu_pull(d_act)[0].astype(jnp.bfloat16)
        grad_up = jnp.einsum("td,tf->df", hidden_b, d_up, preferred_element_type=jnp.float32)
        d_norm_b = lax.psum_scatter(
            jnp.einsum("tf,df->td", d_up, up_weight, preferred_element_type=jnp.float32).astype(
                jnp.bfloat16
            ),
            "mp",
            scatter_dimension=0,
            tiled=True,
        ).astype(jnp.float32)
        norm_out_b, norm_pull_b = jax.vjp(normed, resid, norm_gains[1], scale_b)
        d_resid_ln, d_gain_b, d_scale_b = norm_pull_b(d_norm_b)
        d_resid = cot_rows.astype(jnp.float32) + d_resid_ln
        d_branch = lax.all_gather(d_resid.astype(jnp.bfloat16), "mp", axis=0, tiled=True)
        d_mixed = jnp.einsum(
            "td,ed->te", d_branch, out_weight, preferred_element_type=jnp.float32
        ).astype(jnp.bfloat16)
        grad_out = jnp.einsum(
            "te,td->ed", mixed_heads, d_branch, preferred_element_type=jnp.float32
        )
        d_mixed_blocks = d_mixed.reshape(block_count, block_rows, heads_dev, HEAD)

        def attend_back(sums, block_in):
            query_block, d_mix_block, log_block = block_in
            scores = masked_scores(query_block, key_rows, key_valid)
            probs_f = jnp.exp(scores - log_block[..., None])
            d_probs = jnp.einsum(
                "qhd,khd->hqk", d_mix_block, values, preferred_element_type=jnp.float32
            )
            inner = jnp.sum(probs_f * d_probs, axis=-1, keepdims=True)
            d_raw = (probs_f * (d_probs - inner) * 0.125).astype(jnp.bfloat16)
            d_query = jnp.einsum(
                "hqk,khd->qhd", d_raw, key_rows, preferred_element_type=jnp.float32
            )
            d_key = sums[0] + jnp.einsum(
                "hqk,qhd->khd", d_raw, query_block, preferred_element_type=jnp.float32
            )
            d_value = sums[1] + jnp.einsum(
                "hqk,qhd->khd",
                probs_f.astype(jnp.bfloat16),
                d_mix_block,
                preferred_element_type=jnp.float32,
            )
            return ((d_key, d_value), d_query)

        zero_keys = jnp.zeros((seq_len, heads_dev, HEAD), jnp.float32)
        kv_sums, d_query_blocks = lax.scan(
            attend_back, (zero_keys, zero_keys), (query_blocks, d_mixed_blocks, log_sums)
        )
        d_qkv = jnp.stack(
            [
                d_query_blocks.reshape(seq_len, heads_dev * HEAD),
                kv_sums[0].reshape(seq_len, heads_dev * HEAD),
                kv_sums[1].reshape(seq_len, heads_dev * HEAD),
            ]
        ).astype(jnp.bfloat16)
        grad_qkv = jnp.einsum("td,cte->cde", hidden_a, d_qkv, preferred_element_type=jnp.float32)
        d_norm_a = lax.psum_scatter(
            jnp.einsum("cte,cde->td", d_qkv, qkv_weight, preferred_element_type=jnp.float32).astype(
                jnp.bfloat16
            ),
            "mp",
            scatter_dimension=0,
            tiled=True,
        ).astype(jnp.float32)
        norm_out_a, norm_pull_a = jax.vjp(normed, inputs_f, norm_gains[0], scale_a)
        d_input_ln, d_gain_a, d_scale_a = norm_pull_a(d_norm_a)
        input_grad = (d_resid + d_input_ln).astype(jnp.bfloat16)
        weight_terms = (grad_qkv, grad_out, grad_up, grad_down)
        new_weights = jax.tree.map(lambda held, fresh: held + fresh, totals[0], weight_terms)
        new_gains = totals[1] + jnp.stack([d_gain_a, d_gain_b])
        d_pair = jnp.concatenate([d_scale_a, d_scale_b])
        return ((new_weights, new_gains), (layer_out, input_grad, d_pair))

    start_weights = (
        jnp.zeros(qkv_weight.shape, jnp.float32),
        jnp.zeros(out_weight.shape, jnp.float32),
        jnp.zeros(up_weight.shape, jnp.float32),
        jnp.zeros(down_weight.shape, jnp.float32),
    )
    start_gains = jnp.zeros(norm_gains.shape, jnp.float32)
    final_totals, per_item = lax.scan(
        step_item, (start_weights, start_gains), (token_items, cot_items, len_items, pairs)
    )
    weight_totals, gain_totals = final_totals
    layer_outs, input_grads, d_pairs = per_item
    weight_totals = (
        lax.psum_scatter(
            weight_totals[0].astype(jnp.bfloat16), "dp", scatter_dimension=1, tiled=True
        ).astype(jnp.float32),
        lax.psum_scatter(
            weight_totals[1].astype(jnp.bfloat16), "dp", scatter_dimension=1, tiled=True
        ).astype(jnp.float32),
        lax.psum_scatter(
            weight_totals[2].astype(jnp.bfloat16), "dp", scatter_dimension=0, tiled=True
        ).astype(jnp.float32),
        lax.psum_scatter(
            weight_totals[3].astype(jnp.bfloat16), "dp", scatter_dimension=1, tiled=True
        ).astype(jnp.float32),
    )
    time_part = jnp.dot(feats.T, d_pairs, precision=lax.Precision.HIGHEST)
    gains_grad, time_grad = (
        lax.psum_scatter(gain_totals, ("dp", "mp"), scatter_dimension=1, tiled=True),
        lax.psum_scatter(time_part, ("dp", "mp"), scatter_dimension=1, tiled=True),
    )
    return (
        layer_outs.reshape(tokens.shape),
        input_grads.reshape(tokens.shape),
        weight_totals[0],
        weight_totals[1],
        weight_totals[2],
        weight_totals[3],
        gains_grad,
        time_grad,
    )


def solution(mesh):
    in_specs = (
        P(None, "dp", "mp", None),
        P(None, "dp"),
        P(None, "dp"),
        P(),
        P(),
        P(None, None, "mp"),
        P("mp", None),
        P(None, "mp"),
        P("mp", None),
        P(None, "dp", "mp", None),
    )
    out_specs = (
        P(None, "dp", "mp", None),
        P(None, "dp", "mp", None),
        P(None, "dp", "mp"),
        P("mp", "dp"),
        P("dp", "mp"),
        P("mp", "dp"),
        P(None, ("dp", "mp")),
        P(None, ("dp", "mp")),
    )
    return jax.shard_map(
        per_device, mesh=mesh, in_specs=in_specs, out_specs=out_specs, check_vma=False
    )
```

profile of v0, /device:TPU:0, one launch (start us, length us, event | category | flops | bytes accessed | tf_op | source)
XLA Modules:
  0.0 2625.4 jit_solution(2291842111236679566)
XLA Ops:
  11.3 2053.0 %while.56 = (s32[]{:T(128)}, f32[3,1024,512]{1,2,0:T(8,128)}, f32[512,1024]{1,0:T(8,128)}, f32[1024,2048]{1,0:T(8,128)}, f32[2048,1024]{1,0:T(8,128)}, /*index=5...) while((s32[]{:T(128)}, f32[3,1024,512]{1,2,0:T(8,128)}, ...), condition=%wide.region_24.25_spmd.clone, body=%wide.region_0.24_spmd.clone.sunk | while | flops 42770644992 | bytes 788189504 | solution.py:195
  20.4 34.7 %all-gather.9.cloned.1.call-done = bf16[1024,1024]{1,0:T(8,128)(2,1)} async-done(((bf16[512,1024]{1,0:T(8,128)(2,1)}), bf16[1024,1024]{1,0:T(8,128)(2,1)}) %all-gather.9.cloned.1.call-update) | async-done | bytes 2097168 | tf_op jit(solution)/shard_map/while/body/eval_jaxpr/all_gather | solution.py:68
  64.5 24.4 while.57
  96.2 31.4 %reduce-scatter.25.cloned.1.call-done = bf16[512,1024]{1,0:T(8,128)(2,1)} async-done(((bf16[1024,1024]{1,0:T(8,128)(2,1)}), bf16[512,1024]{1,0:T(8,128)(2,1)}) %reduce-scatter.25.cloned.1.call-update) | async-done | bytes 1048592 | tf_op jit(solution)/shard_map/while/body/eval_jaxpr/reduce_scatter | solution.py:88
  136.8 30.9 %all-gather.11.cloned.1.call-done = bf16[1024,1024]{1,0:T(8,128)(2,1)} async-done(((bf16[512,1024]{1,0:T(8,128)(2,1)}), bf16[1024,1024]{1,0:T(8,128)(2,1)}) %all-gather.11.cloned.1.call-update) | async-done | bytes 2097168 | tf_op jit(solution)/shard_map/while/body/eval_jaxpr/all_gather | solution.py:98
  167.7 26.0 multiply_convert_fusion.6
  202.3 12.9 add_convert_fusion.4
  223.3 31.8 %reduce-scatter.27.cloned.1.call-done = bf16[512,1024]{1,0:T(8,128)(2,1)} async-done(((bf16[1024,1024]{1,0:T(8,128)(2,1)}), bf16[512,1024]{1,0:T(8,128)(2,1)}) %reduce-scatter.27.cloned.1.call-update) | async-done | bytes 1048592 | tf_op jit(solution)/shard_map/while/body/eval_jaxpr/reduce_scatter | solution.py:116
  265.0 33.2 %all-gather.15.cloned.1.call-done = bf16[1024,1024]{1,0:T(8,128)(2,1)} async-done(((bf16[512,1024]{1,0:T(8,128)(2,1)}), bf16[1024,1024]{1,0:T(8,128)(2,1)}) %all-gather.15.cloned.1.call-update) | async-done | bytes 2097168 | tf_op jit(solution)/shard_map/while/body/eval_jaxpr/all_gather | solution.py:127
  306.0 137.9 %while.58 = (s32[]{:T(128)}, f32[1024,8,64]{0,2,1:T(8,128)}, f32[1024,8,64]{0,2,1:T(8,128)}, bf16[2,512,8,64]{1,3,2,0:T(8,128)(2,1)}, bf16[2,512,8,64]{1,3,2,0:T...) while((s32[]{:T(128)}, f32[1024,8,64]{0,2,1:T(8,128)}, ...), condition=%wide.region_15.15_spmd.clone, body=%wide.region_13.14_spmd.clone.sunk | while | flops 2745182208 | bytes 266388672 | solution.py:160
  325.6 25.4 fusion.233
  351.0 23.4 bitcast_add_fusion.7
  394.6 25.4 fusion.233
  419.9 24.0 bitcast_add_fusion.7
  498.3 23.2 reduce-scatter.31.cloned.1.call-done
  534.9 32.0 %all-gather.9.cloned.1.call-done = bf16[1024,1024]{1,0:T(8,128)(2,1)} async-done(((bf16[512,1024]{1,0:T(8,128)(2,1)}), bf16[1024,1024]{1,0:T(8,128)(2,1)}) %all-gather.9.cloned.1.call-update) | async-done | bytes 2097168 | tf_op jit(solution)/shard_map/while/body/eval_jaxpr/all_gather | solution.py:68
  576.3 24.4 while.57
  607.8 31.5 %reduce-scatter.25.cloned.1.call-done = bf16[512,1024]{1,0:T(8,128)(2,1)} async-done(((bf16[1024,1024]{1,0:T(8,128)(2,1)}), bf16[512,1024]{1,0:T(8,128)(2,1)}) %reduce-scatter.25.cloned.1.call-update) | async-done | bytes 1048592 | tf_op jit(solution)/shard_map/while/body/eval_jaxpr/reduce_scatter | solution.py:88
  648.6 30.9 %all-gather.11.cloned.1.call-done = bf16[1024,1024]{1,0:T(8,128)(2,1)} async-done(((bf16[512,1024]{1,0:T(8,128)(2,1)}), bf16[1024,1024]{1,0:T(8,128)(2,1)}) %all-gather.11.cloned.1.call-update) | async-done | bytes 2097168 | tf_op jit(solution)/shard_map/while/body/eval_jaxpr/all_gather | solution.py:98
  679.5 25.9 multiply_convert_fusion.6
  735.1 31.8 %reduce-scatter.27.cloned.1.call-done = bf16[512,1024]{1,0:T(8,128)(2,1)} async-done(((bf16[1024,1024]{1,0:T(8,128)(2,1)}), bf16[512,1024]{1,0:T(8,128)(2,1)}) %reduce-scatter.27.cloned.1.call-update) | async-done | bytes 1048592 | tf_op jit(solution)/shard_map/while/body/eval_jaxpr/reduce_scatter | solution.py:116
  776.8 33.2 %all-gather.15.cloned.1.call-done = bf16[1024,1024]{1,0:T(8,128)(2,1)} async-done(((bf16[512,1024]{1,0:T(8,128)(2,1)}), bf16[1024,1024]{1,0:T(8,128)(2,1)}) %all-gather.15.cloned.1.call-update) | async-done | bytes 2097168 | tf_op jit(solution)/shard_map/while/body/eval_jaxpr/all_gather | solution.py:127
  817.7 137.9 %while.58 = (s32[]{:T(128)}, f32[1024,8,64]{0,2,1:T(8,128)}, f32[1024,8,64]{0,2,1:T(8,128)}, bf16[2,512,8,64]{1,3,2,0:T(8,128)(2,1)}, bf16[2,512,8,64]{1,3,2,0:T...) while((s32[]{:T(128)}, f32[1024,8,64]{0,2,1:T(8,128)}, ...), condition=%wide.region_15.15_spmd.clone, body=%wide.region_13.14_spmd.clone.sunk | while | flops 2745182208 | bytes 266388672 | solution.py:160
  837.4 25.4 fusion.233
  862.7 23.4 bitcast_add_fusion.7
  906.3 25.4 fusion.233
  931.7 24.0 bitcast_add_fusion.7
  976.7 13.2 select_add_fusion.7
  1016.7 16.4 reduce-scatter.31.cloned.1.call-done
  1046.5 32.0 %all-gather.9.cloned.1.call-done = bf16[1024,1024]{1,0:T(8,128)(2,1)} async-done(((bf16[512,1024]{1,0:T(8,128)(2,1)}), bf16[1024,1024]{1,0:T(8,128)(2,1)}) %all-gather.9.cloned.1.call-update) | async-done | bytes 2097168 | tf_op jit(solution)/shard_map/while/body/eval_jaxpr/all_gather | solution.py:68
  1087.9 24.4 while.57
  1119.4 31.5 %reduce-scatter.25.cloned.1.call-done = bf16[512,1024]{1,0:T(8,128)(2,1)} async-done(((bf16[1024,1024]{1,0:T(8,128)(2,1)}), bf16[512,1024]{1,0:T(8,128)(2,1)}) %reduce-scatter.25.cloned.1.call-update) | async-done | bytes 1048592 | tf_op jit(solution)/shard_map/while/body/eval_jaxpr/reduce_scatter | solution.py:88
  1160.2 30.9 %all-gather.11.cloned.1.call-done = bf16[1024,1024]{1,0:T(8,128)(2,1)} async-done(((bf16[512,1024]{1,0:T(8,128)(2,1)}), bf16[1024,1024]{1,0:T(8,128)(2,1)}) %all-gather.11.cloned.1.call-update) | async-done | bytes 2097168 | tf_op jit(solution)/shard_map/while/body/eval_jaxpr/all_gather | solution.py:98
  1191.1 25.9 multiply_convert_fusion.6
  1246.7 31.8 %reduce-scatter.27.cloned.1.call-done = bf16[512,1024]{1,0:T(8,128)(2,1)} async-done(((bf16[1024,1024]{1,0:T(8,128)(2,1)}), bf16[512,1024]{1,0:T(8,128)(2,1)}) %reduce-scatter.27.cloned.1.call-update) | async-done | bytes 1048592 | tf_op jit(solution)/shard_map/while/body/eval_jaxpr/reduce_scatter | solution.py:116
  1288.4 33.2 %all-gather.15.cloned.1.call-done = bf16[1024,1024]{1,0:T(8,128)(2,1)} async-done(((bf16[512,1024]{1,0:T(8,128)(2,1)}), bf16[1024,1024]{1,0:T(8,128)(2,1)}) %all-gather.15.cloned.1.call-update) | async-done | bytes 2097168 | tf_op jit(solution)/shard_map/while/body/eval_jaxpr/all_gather | solution.py:127
  1329.3 137.9 %while.58 = (s32[]{:T(128)}, f32[1024,8,64]{0,2,1:T(8,128)}, f32[1024,8,64]{0,2,1:T(8,128)}, bf16[2,512,8,64]{1,3,2,0:T(8,128)(2,1)}, bf16[2,512,8,64]{1,3,2,0:T...) while((s32[]{:T(128)}, f32[1024,8,64]{0,2,1:T(8,128)}, ...), condition=%wide.region_15.15_spmd.clone, body=%wide.region_13.14_spmd.clone.sunk | while | flops 2745182208 | bytes 266388672 | solution.py:160
  1349.0 25.4 fusion.233
  1374.4 23.4 bitcast_add_fusion.7
  1417.9 25.4 fusion.233
  1443.3 24.0 bitcast_add_fusion.7
  1488.4 13.2 select_add_fusion.7
  1528.3 16.4 reduce-scatter.31.cloned.1.call-done
  1558.1 32.0 %all-gather.9.cloned.1.call-done = bf16[1024,1024]{1,0:T(8,128)(2,1)} async-done(((bf16[512,1024]{1,0:T(8,128)(2,1)}), bf16[1024,1024]{1,0:T(8,128)(2,1)}) %all-gather.9.cloned.1.call-update) | async-done | bytes 2097168 | tf_op jit(solution)/shard_map/while/body/eval_jaxpr/all_gather | solution.py:68
  1599.5 24.4 while.57
  1631.0 31.5 %reduce-scatter.25.cloned.1.call-done = bf16[512,1024]{1,0:T(8,128)(2,1)} async-done(((bf16[1024,1024]{1,0:T(8,128)(2,1)}), bf16[512,1024]{1,0:T(8,128)(2,1)}) %reduce-scatter.25.cloned.1.call-update) | async-done | bytes 1048592 | tf_op jit(solution)/shard_map/while/body/eval_jaxpr/reduce_scatter | solution.py:88
  1671.8 30.9 %all-gather.11.cloned.1.call-done = bf16[1024,1024]{1,0:T(8,128)(2,1)} async-done(((bf16[512,1024]{1,0:T(8,128)(2,1)}), bf16[1024,1024]{1,0:T(8,128)(2,1)}) %all-gather.11.cloned.1.call-update) | async-done | bytes 2097168 | tf_op jit(solution)/shard_map/while/body/eval_jaxpr/all_gather | solution.py:98
  1702.7 25.9 multiply_convert_fusion.6
  1737.4 12.9 add_convert_fusion.4
  1758.4 31.8 %reduce-scatter.27.cloned.1.call-done = bf16[512,1024]{1,0:T(8,128)(2,1)} async-done(((bf16[1024,1024]{1,0:T(8,128)(2,1)}), bf16[512,1024]{1,0:T(8,128)(2,1)}) %reduce-scatter.27.cloned.1.call-update) | async-done | bytes 1048592 | tf_op jit(solution)/shard_map/while/body/eval_jaxpr/reduce_scatter | solution.py:116
  1800.2 33.2 %all-gather.15.cloned.1.call-done = bf16[1024,1024]{1,0:T(8,128)(2,1)} async-done(((bf16[512,1024]{1,0:T(8,128)(2,1)}), bf16[1024,1024]{1,0:T(8,128)(2,1)}) %all-gather.15.cloned.1.call-update) | async-done | bytes 2097168 | tf_op jit(solution)/shard_map/while/body/eval_jaxpr/all_gather | solution.py:127
  1841.1 137.9 %while.58 = (s32[]{:T(128)}, f32[1024,8,64]{0,2,1:T(8,128)}, f32[1024,8,64]{0,2,1:T(8,128)}, bf16[2,512,8,64]{1,3,2,0:T(8,128)(2,1)}, bf16[2,512,8,64]{1,3,2,0:T...) while((s32[]{:T(128)}, f32[1024,8,64]{0,2,1:T(8,128)}, ...), condition=%wide.region_15.15_spmd.clone, body=%wide.region_13.14_spmd.clone.sunk | while | flops 2745182208 | bytes 266388672 | solution.py:160
  1860.7 25.4 fusion.233
  1886.1 23.4 bitcast_add_fusion.7
  1929.7 25.4 fusion.233
  1955.0 24.0 bitcast_add_fusion.7
  2000.1 13.2 select_add_fusion.7
  2040.0 16.6 reduce-scatter.31.cloned.1.call-done
  2091.8 109.7 %reduce-scatter.23.cloned.1.call-done = f32[32,2]{1,0:T(8,128)} async-done(((f32[1024,2]{1,0:T(8,128)}), f32[32,2]{1,0:T(8,128)}) %reduce-scatter.23.cloned.1.call-update) | async-done | bytes 272
  2202.9 55.9 %reduce-scatter.15.cloned.1.call-done = bf16[512,64]{0,1:T(8,128)(2,1)} async-done(((bf16[512,1024]{0,1:T(8,128)(2,1)}), bf16[512,64]{0,1:T(8,128)(2,1)}) %reduce-scatter.15.cloned.1.call-update) | async-done | bytes 65552 | tf_op jit(solution)/shard_map/reduce_scatter | solution.py:204
  2260.3 67.3 %reduce-scatter.13.cloned.1.call-done = bf16[3,64,512]{2,1,0:T(8,128)(2,1)} async-done(((bf16[3,1024,512]{2,1,0:T(8,128)(2,1)}), bf16[3,64,512]{2,1,0:T(8,128)(2,1)}) %reduce-scatter.13.cloned.1.call-update) | async-done | bytes 196624 | tf_op jit(solution)/shard_map/reduce_scatter | solution.py:201
  2329.3 73.5 %reduce-scatter.17.cloned.1.call-done = bf16[64,2048]{1,0:T(8,128)(2,1)} async-done(((bf16[1024,2048]{1,0:T(8,128)(2,1)}), bf16[64,2048]{1,0:T(8,128)(2,1)}) %reduce-scatter.17.cloned.1.call-update) | async-done | bytes 262160 | tf_op jit(solution)/shard_map/reduce_scatter | solution.py:207
  2404.5 74.3 %reduce-scatter.19.cloned.1.call-done = bf16[2048,64]{0,1:T(8,128)(2,1)} async-done(((bf16[2048,1024]{0,1:T(8,128)(2,1)}), bf16[2048,64]{0,1:T(8,128)(2,1)}) %reduce-scatter.19.cloned.1.call-update) | async-done | bytes 262160 | tf_op jit(solution)/shard_map/reduce_scatter | solution.py:210
  2480.6 137.5 %reduce-scatter.21.cloned.1.call-done = f32[256,64]{0,1:T(8,128)} async-done(((f32[256,2048]{0,1:T(8,128)}), f32[256,64]{0,1:T(8,128)}) %reduce-scatter.21.cloned.1.call-update) | async-done | bytes 65552 | tf_op jit(solution)/shard_map/reduce_scatter | solution.py:217
  (732 shorter events, 810.4 us)
Async XLA Ops:
  11.3 43.8 %all-gather.9.cloned.1.call-start = ((), (), s32[]{:S(2)}) async-start(), calls=%async_computation.16 | async-start | bytes 3145728 | tf_op jit(solution)/shard_map/while/body/eval_jaxpr/all_gather | solution.py:68
  12.8 42.4 %copy-start.18 = (f32[512]{0:T(512)}, f32[512]{0:T(512)S(1)}, u32[]{:S(2)}) copy-start(f32[512]{0:T(512)S(1)} %broadcast_multiply_fusion.4) | copy-start | bytes 6148 | tf_op jit(solution)/shard_map/while
  14.5 40.7 %copy-start.22 = (f32[512]{0:T(512)}, f32[512]{0:T(512)S(1)}, u32[]{:S(2)}) copy-start(f32[512]{0:T(512)S(1)} %fusion.207) | copy-start | bytes 6148 | tf_op jit(solution)/shard_map/while
  16.5 38.7 %copy-start.12 = (f32[1,1024]{1,0:T(1,128)}, f32[1,1024]{1,0:T(1,128)S(1)}, u32[]{:S(2)}) copy-start(f32[1,1024]{1,0:T(1,128)S(1)} %get-tuple-element.724) | copy-start | bytes 12292 | tf_op jit(solution)/shard_map/while
  16.5 38.7 %copy-start.14 = (f32[1,1024]{1,0:T(1,128)}, f32[1,1024]{1,0:T(1,128)S(1)}, u32[]{:S(2)}) copy-start(f32[1,1024]{1,0:T(1,128)S(1)} %get-tuple-element.725) | copy-start | bytes 12292 | tf_op jit(solution)/shard_map/while
  19.2 108.4 %reduce-scatter.25.cloned.1.call-start = ((), (), s32[]{:S(2)}) async-start(), calls=%async_computation.17 | async-start | bytes 3145728 | tf_op jit(solution)/shard_map/while/body/eval_jaxpr/reduce_scatter | solution.py:88
  95.6 36.1 %copy-start.20 = (f32[1,1024]{1,0:T(1,128)S(1)}, f32[1,1024]{1,0:T(1,128)}, u32[]{:S(2)}) copy-start(f32[1,1024]{1,0:T(1,128)} %get-tuple-element.731) | copy-start | bytes 12292 | tf_op jit(solution)/shard_map/while
  95.6 36.1 %copy-start.21 = (f32[1,1024]{1,0:T(1,128)S(1)}, f32[1,1024]{1,0:T(1,128)}, u32[]{:S(2)}) copy-start(f32[1,1024]{1,0:T(1,128)} %get-tuple-element.732) | copy-start | bytes 12292 | tf_op jit(solution)/shard_map/while
  95.6 72.1 %all-gather.11.cloned.1.call-start = ((), (), s32[]{:S(2)}) async-start(), calls=%async_computation.18 | async-start | bytes 3145728 | tf_op jit(solution)/shard_map/while/body/eval_jaxpr/all_gather | solution.py:98
  134.4 67.8 %all-gather.13.cloned.1.call-start = ((), (), s32[]{:S(2)}) async-start(), calls=%async_computation.19 | async-start | bytes 3145728 | tf_op jit(solution)/shard_map/while/body/eval_jaxpr/all_gather | solution.py:110
  136.8 118.3 %reduce-scatter.27.cloned.1.call-start = ((), (), s32[]{:S(2)}) async-start(), calls=%async_computation.20 | async-start | bytes 3145728 | tf_op jit(solution)/shard_map/while/body/eval_jaxpr/reduce_scatter | solution.py:116
  223.1 75.1 %all-gather.15.cloned.1.call-start = ((), (), s32[]{:S(2)}) async-start(), calls=%async_computation.21 | async-start | bytes 3145728 | tf_op jit(solution)/shard_map/while/body/eval_jaxpr/all_gather | solution.py:127
  264.9 226.6 %reduce-scatter.29.cloned.1.call-start = ((), (), s32[]{:S(2)}) async-start(), calls=%async_computation.22 | async-start | bytes 3145728 | tf_op jit(solution)/shard_map/while/body/eval_jaxpr/reduce_scatter | solution.py:171
  455.4 66.1 %reduce-scatter.31.cloned.1.call-start = ((), (), s32[]{:S(2)}) async-start(), calls=%async_computation.23 | async-start | bytes 3145728 | tf_op jit(solution)/shard_map/while/body/eval_jaxpr/reduce_scatter | solution.py:101
  491.5 30.0 %copy-start.4 = (bf16[512,1024]{1,0:T(8,128)(2,1)S(1)}, bf16[512,1024]{1,0:T(8,128)(2,1)}, u32[]{:S(2)}) copy-start(bf16[512,1024]{1,0:T(8,128)(2,1)} %reduce-scatter.25.cloned.1.call-done) | copy-start | bytes 3145732 | tf_op jit(solution)/shard_map/while
  525.8 41.2 %all-gather.9.cloned.1.call-start = ((), (), s32[]{:S(2)}) async-start(), calls=%async_computation.16 | async-start | bytes 3145728 | tf_op jit(solution)/shard_map/while/body/eval_jaxpr/all_gather | solution.py:68
  527.3 39.7 %copy-start.18 = (f32[512]{0:T(512)}, f32[512]{0:T(512)S(1)}, u32[]{:S(2)}) copy-start(f32[512]{0:T(512)S(1)} %broadcast_multiply_fusion.4) | copy-start | bytes 6148 | tf_op jit(solution)/shard_map/while
  529.0 38.0 %copy-start.22 = (f32[512]{0:T(512)}, f32[512]{0:T(512)S(1)}, u32[]{:S(2)}) copy-start(f32[512]{0:T(512)S(1)} %fusion.207) | copy-start | bytes 6148 | tf_op jit(solution)/shard_map/while
  531.0 36.0 %copy-start.12 = (f32[1,1024]{1,0:T(1,128)}, f32[1,1024]{1,0:T(1,128)S(1)}, u32[]{:S(2)}) copy-start(f32[1,1024]{1,0:T(1,128)S(1)} %get-tuple-element.724) | copy-start | bytes 12292 | tf_op jit(solution)/shard_map/while
  531.0 36.0 %copy-start.14 = (f32[1,1024]{1,0:T(1,128)}, f32[1,1024]{1,0:T(1,128)S(1)}, u32[]{:S(2)}) copy-start(f32[1,1024]{1,0:T(1,128)S(1)} %get-tuple-element.725) | copy-start | bytes 12292 | tf_op jit(solution)/shard_map/while
  533.7 105.7 %reduce-scatter.25.cloned.1.call-start = ((), (), s32[]{:S(2)}) async-start(), calls=%async_computation.17 | async-start | bytes 3145728 | tf_op jit(solution)/shard_map/while/body/eval_jaxpr/reduce_scatter | solution.py:88
  607.3 36.1 %copy-start.20 = (f32[1,1024]{1,0:T(1,128)S(1)}, f32[1,1024]{1,0:T(1,128)}, u32[]{:S(2)}) copy-start(f32[1,1024]{1,0:T(1,128)} %get-tuple-element.731) | copy-start | bytes 12292 | tf_op jit(solution)/shard_map/while
  607.3 36.1 %copy-start.21 = (f32[1,1024]{1,0:T(1,128)S(1)}, f32[1,1024]{1,0:T(1,128)}, u32[]{:S(2)}) copy-start(f32[1,1024]{1,0:T(1,128)} %get-tuple-element.732) | copy-start | bytes 12292 | tf_op jit(solution)/shard_map/while
  607.4 72.1 %all-gather.11.cloned.1.call-start = ((), (), s32[]{:S(2)}) async-start(), calls=%async_computation.18 | async-start | bytes 3145728 | tf_op jit(solution)/shard_map/while/body/eval_jaxpr/all_gather | solution.py:98
  646.2 67.8 %all-gather.13.cloned.1.call-start = ((), (), s32[]{:S(2)}) async-start(), calls=%async_computation.19 | async-start | bytes 3145728 | tf_op jit(solution)/shard_map/while/body/eval_jaxpr/all_gather | solution.py:110
  648.6 118.3 %reduce-scatter.27.cloned.1.call-start = ((), (), s32[]{:S(2)}) async-start(), calls=%async_computation.20 | async-start | bytes 3145728 | tf_op jit(solution)/shard_map/while/body/eval_jaxpr/reduce_scatter | solution.py:116
  734.9 75.1 %all-gather.15.cloned.1.call-start = ((), (), s32[]{:S(2)}) async-start(), calls=%async_computation.21 | async-start | bytes 3145728 | tf_op jit(solution)/shard_map/while/body/eval_jaxpr/all_gather | solution.py:127
  776.7 233.2 %reduce-scatter.29.cloned.1.call-start = ((), (), s32[]{:S(2)}) async-start(), calls=%async_computation.22 | async-start | bytes 3145728 | tf_op jit(solution)/shard_map/while/body/eval_jaxpr/reduce_scatter | solution.py:171
  967.2 65.9 %reduce-scatter.31.cloned.1.call-start = ((), (), s32[]{:S(2)}) async-start(), calls=%async_computation.23 | async-start | bytes 3145728 | tf_op jit(solution)/shard_map/while/body/eval_jaxpr/reduce_scatter | solution.py:101
  1037.4 41.2 %all-gather.9.cloned.1.call-start = ((), (), s32[]{:S(2)}) async-start(), calls=%async_computation.16 | async-start | bytes 3145728 | tf_op jit(solution)/shard_map/while/body/eval_jaxpr/all_gather | solution.py:68
  1038.9 39.7 %copy-start.18 = (f32[512]{0:T(512)}, f32[512]{0:T(512)S(1)}, u32[]{:S(2)}) copy-start(f32[512]{0:T(512)S(1)} %broadcast_multiply_fusion.4) | copy-start | bytes 6148 | tf_op jit(solution)/shard_map/while
  1040.6 38.0 %copy-start.22 = (f32[512]{0:T(512)}, f32[512]{0:T(512)S(1)}, u32[]{:S(2)}) copy-start(f32[512]{0:T(512)S(1)} %fusion.207) | copy-start | bytes 6148 | tf_op jit(solution)/shard_map/while
  1042.6 36.0 %copy-start.12 = (f32[1,1024]{1,0:T(1,128)}, f32[1,1024]{1,0:T(1,128)S(1)}, u32[]{:S(2)}) copy-start(f32[1,1024]{1,0:T(1,128)S(1)} %get-tuple-element.724) | copy-start | bytes 12292 | tf_op jit(solution)/shard_map/while
  1042.6 36.0 %copy-start.14 = (f32[1,1024]{1,0:T(1,128)}, f32[1,1024]{1,0:T(1,128)S(1)}, u32[]{:S(2)}) copy-start(f32[1,1024]{1,0:T(1,128)S(1)} %get-tuple-element.725) | copy-start | bytes 12292 | tf_op jit(solution)/shard_map/while
  1045.3 105.7 %reduce-scatter.25.cloned.1.call-start = ((), (), s32[]{:S(2)}) async-start(), calls=%async_computation.17 | async-start | bytes 3145728 | tf_op jit(solution)/shard_map/while/body/eval_jaxpr/reduce_scatter | solution.py:88
  1118.9 36.1 %copy-start.20 = (f32[1,1024]{1,0:T(1,128)S(1)}, f32[1,1024]{1,0:T(1,128)}, u32[]{:S(2)}) copy-start(f32[1,1024]{1,0:T(1,128)} %get-tuple-element.731) | copy-start | bytes 12292 | tf_op jit(solution)/shard_map/while
  1118.9 36.1 %copy-start.21 = (f32[1,1024]{1,0:T(1,128)S(1)}, f32[1,1024]{1,0:T(1,128)}, u32[]{:S(2)}) copy-start(f32[1,1024]{1,0:T(1,128)} %get-tuple-element.732) | copy-start | bytes 12292 | tf_op jit(solution)/shard_map/while
  1119.0 72.1 %all-gather.11.cloned.1.call-start = ((), (), s32[]{:S(2)}) async-start(), calls=%async_computation.18 | async-start | bytes 3145728 | tf_op jit(solution)/shard_map/while/body/eval_jaxpr/all_gather | solution.py:98
  1157.8 67.8 %all-gather.13.cloned.1.call-start = ((), (), s32[]{:S(2)}) async-start(), calls=%async_computation.19 | async-start | bytes 3145728 | tf_op jit(solution)/shard_map/while/body/eval_jaxpr/all_gather | solution.py:110
  1160.2 118.3 %reduce-scatter.27.cloned.1.call-start = ((), (), s32[]{:S(2)}) async-start(), calls=%async_computation.20 | async-start | bytes 3145728 | tf_op jit(solution)/shard_map/while/body/eval_jaxpr/reduce_scatter | solution.py:116
  1246.5 75.1 %all-gather.15.cloned.1.call-start = ((), (), s32[]{:S(2)}) async-start(), calls=%async_computation.21 | async-start | bytes 3145728 | tf_op jit(solution)/shard_map/while/body/eval_jaxpr/all_gather | solution.py:127
  1288.3 233.2 %reduce-scatter.29.cloned.1.call-start = ((), (), s32[]{:S(2)}) async-start(), calls=%async_computation.22 | async-start | bytes 3145728 | tf_op jit(solution)/shard_map/while/body/eval_jaxpr/reduce_scatter | solution.py:171
  1478.8 65.9 %reduce-scatter.31.cloned.1.call-start = ((), (), s32[]{:S(2)}) async-start(), calls=%async_computation.23 | async-start | bytes 3145728 | tf_op jit(solution)/shard_map/while/body/eval_jaxpr/reduce_scatter | solution.py:101
  1549.0 41.2 %all-gather.9.cloned.1.call-start = ((), (), s32[]{:S(2)}) async-start(), calls=%async_computation.16 | async-start | bytes 3145728 | tf_op jit(solution)/shard_map/while/body/eval_jaxpr/all_gather | solution.py:68
  1550.5 39.7 %copy-start.18 = (f32[512]{0:T(512)}, f32[512]{0:T(512)S(1)}, u32[]{:S(2)}) copy-start(f32[512]{0:T(512)S(1)} %broadcast_multiply_fusion.4) | copy-start | bytes 6148 | tf_op jit(solution)/shard_map/while
  1552.2 38.0 %copy-start.22 = (f32[512]{0:T(512)}, f32[512]{0:T(512)S(1)}, u32[]{:S(2)}) copy-start(f32[512]{0:T(512)S(1)} %fusion.207) | copy-start | bytes 6148 | tf_op jit(solution)/shard_map/while
  1554.2 36.0 %copy-start.12 = (f32[1,1024]{1,0:T(1,128)}, f32[1,1024]{1,0:T(1,128)S(1)}, u32[]{:S(2)}) copy-start(f32[1,1024]{1,0:T(1,128)S(1)} %get-tuple-element.724) | copy-start | bytes 12292 | tf_op jit(solution)/shard_map/while
  1554.2 36.0 %copy-start.14 = (f32[1,1024]{1,0:T(1,128)}, f32[1,1024]{1,0:T(1,128)S(1)}, u32[]{:S(2)}) copy-start(f32[1,1024]{1,0:T(1,128)S(1)} %get-tuple-element.725) | copy-start | bytes 12292 | tf_op jit(solution)/shard_map/while
  1556.9 105.7 %reduce-scatter.25.cloned.1.call-start = ((), (), s32[]{:S(2)}) async-start(), calls=%async_computation.17 | async-start | bytes 3145728 | tf_op jit(solution)/shard_map/while/body/eval_jaxpr/reduce_scatter | solution.py:88
  1630.5 36.1 %copy-start.20 = (f32[1,1024]{1,0:T(1,128)S(1)}, f32[1,1024]{1,0:T(1,128)}, u32[]{:S(2)}) copy-start(f32[1,1024]{1,0:T(1,128)} %get-tuple-element.731) | copy-start | bytes 12292 | tf_op jit(solution)/shard_map/while
  1630.5 36.1 %copy-start.21 = (f32[1,1024]{1,0:T(1,128)S(1)}, f32[1,1024]{1,0:T(1,128)}, u32[]{:S(2)}) copy-start(f32[1,1024]{1,0:T(1,128)} %get-tuple-element.732) | copy-start | bytes 12292 | tf_op jit(solution)/shard_map/while
  1630.6 72.1 %all-gather.11.cloned.1.call-start = ((), (), s32[]{:S(2)}) async-start(), calls=%async_computation.18 | async-start | bytes 3145728 | tf_op jit(solution)/shard_map/while/body/eval_jaxpr/all_gather | solution.py:98
  1669.4 68.0 %all-gather.13.cloned.1.call-start = ((), (), s32[]{:S(2)}) async-start(), calls=%async_computation.19 | async-start | bytes 3145728 | tf_op jit(solution)/shard_map/while/body/eval_jaxpr/all_gather | solution.py:110
  1671.8 118.4 %reduce-scatter.27.cloned.1.call-start = ((), (), s32[]{:S(2)}) async-start(), calls=%async_computation.20 | async-start | bytes 3145728 | tf_op jit(solution)/shard_map/while/body/eval_jaxpr/reduce_scatter | solution.py:116
  1758.2 75.1 %all-gather.15.cloned.1.call-start = ((), (), s32[]{:S(2)}) async-start(), calls=%async_computation.21 | async-start | bytes 3145728 | tf_op jit(solution)/shard_map/while/body/eval_jaxpr/all_gather | solution.py:127
  1800.1 233.2 %reduce-scatter.29.cloned.1.call-start = ((), (), s32[]{:S(2)}) async-start(), calls=%async_computation.22 | async-start | bytes 3145728 | tf_op jit(solution)/shard_map/while/body/eval_jaxpr/reduce_scatter | solution.py:171
  1990.5 66.1 %reduce-scatter.31.cloned.1.call-start = ((), (), s32[]{:S(2)}) async-start(), calls=%async_computation.23 | async-start | bytes 3145728 | tf_op jit(solution)/shard_map/while/body/eval_jaxpr/reduce_scatter | solution.py:101
  2064.3 137.2 %reduce-scatter.23.cloned.1.call-start = ((), (), s32[]{:S(2)}) async-start(), calls=%async_computation.15 | async-start | bytes 540672
  2066.1 192.7 %reduce-scatter.15.cloned.1.call-start = ((), (), s32[]{:S(2)}) async-start(), calls=%async_computation.11 | async-start | bytes 1114112 | tf_op jit(solution)/shard_map/reduce_scatter | solution.py:204
  2068.7 258.8 %reduce-scatter.13.cloned.1.call-start = ((), (), s32[]{:S(2)}) async-start(), calls=%async_computation.10 | async-start | bytes 3342336 | tf_op jit(solution)/shard_map/reduce_scatter | solution.py:201
  2074.2 328.6 %reduce-scatter.17.cloned.1.call-start = ((), (), s32[]{:S(2)}) async-start(), calls=%async_computation.12 | async-start | bytes 4456448 | tf_op jit(solution)/shard_map/reduce_scatter | solution.py:207
  2080.2 398.6 %reduce-scatter.19.cloned.1.call-start = ((), (), s32[]{:S(2)}) async-start(), calls=%async_computation.13 | async-start | bytes 4456448 | tf_op jit(solution)/shard_map/reduce_scatter | solution.py:210
  2087.7 530.4 %copy-start.1 = (f32[256,2048]{1,0:T(8,128)S(1)}, f32[256,2048]{1,0:T(8,128)}, u32[]{:S(2)}) copy-start(f32[256,2048]{1,0:T(8,128)} %param.20) | copy-start | bytes 6291460
  2087.7 530.3 %reduce-scatter.21.cloned.1.call-start = ((), (), s32[]{:S(2)}) async-start(), calls=%async_computation.14 | async-start | bytes 2162688 | tf_op jit(solution)/shard_map/reduce_scatter | solution.py:217
  (149 other events, 1107.3 us)
Sparse Core Ops, SparseCore 0:
  19.3 35.8 all-gather.8
  95.7 31.8 reduce-scatter.24
  134.6 33.1 all-gather.10
  169.1 33.1 all-gather.12
  223.2 31.8 reduce-scatter.26
  265.1 33.1 all-gather.14
  455.5 31.8 reduce-scatter.28
  489.6 31.8 reduce-scatter.30
  533.8 33.1 all-gather.8
  607.5 31.8 reduce-scatter.24
  646.3 33.1 all-gather.10
  680.9 33.1 all-gather.12
  735.0 31.8 reduce-scatter.26
  776.8 33.1 all-gather.14
  967.3 31.8 reduce-scatter.28
  1001.2 31.8 reduce-scatter.30
  1045.4 33.1 all-gather.8
  1119.1 31.8 reduce-scatter.24
  1157.9 33.1 all-gather.10
  1192.5 33.1 all-gather.12
  1246.6 31.8 reduce-scatter.26
  1288.4 33.1 all-gather.14
  1478.9 31.8 reduce-scatter.28
  1512.9 31.8 reduce-scatter.30
  1557.0 33.1 all-gather.8
  1630.7 31.8 reduce-scatter.24
  1669.5 33.1 all-gather.10
  1704.2 33.1 all-gather.12
  1758.3 31.8 reduce-scatter.26
  1800.2 33.1 all-gather.14
  1990.6 31.8 reduce-scatter.28
  2024.8 31.8 reduce-scatter.30
Sparse Core Ops, SparseCore 1:
  2067.6 133.9 reduce-scatter.22
  2205.4 53.2 reduce-scatter.14
  2262.4 65.1 reduce-scatter.12
  2331.4 71.2 reduce-scatter.16
  2407.1 71.6 reduce-scatter.18
  2481.7 136.4 reduce-scatter.20
where the time goes:
time: 2630 us
  waiting for transfers between devices  1270 us (48%)
  matrix products  1000 us (38%)
  other arithmetic  190 us (7%)
  local copies, waits for them, and re-layouts  139 us (5%)
    dot_general x8, matrix products, attend_back(): jnp.einsum('hqk,khd->qhd', d_raw, key_rows, preferred_element_type=jnp.fl...  203 us
    dot_general x8, matrix products, attend_back(): jnp.einsum('hqk,qhd->khd', d_raw, query_block, preferred_element_type=jnp...  189 us
    reduce_scatter x1, waiting for transfers between devices, per_device(): lax.psum_scatter(time_part, ('dp', 'mp'), scatter_dimension=1, tiled=True)  137 us
    all_gather x4, waiting for transfers between devices, step_item(): lax.all_gather(d_resid.astype(jnp.bfloat16), 'mp', axis=0, tiled=True)  133 us
    all_gather x4, waiting for transfers between devices, step_item(): lax.all_gather(norm_a.astype(jnp.bfloat16), 'mp', axis=0, tiled=True)  131 us
    reduce_scatter x4, waiting for transfers between devices, step_item(): lax.psum_scatter(jnp.einsum('tf,df->td', d_up, up_weight, preferred_eleme...  127 us
    reduce_scatter x4, waiting for transfers between devices, step_item(): lax.psum_scatter(jnp.dot(mixed_heads, out_weight, preferred_element_type=...  126 us
    all_gather x4, waiting for transfers between devices, step_item(): lax.all_gather(norm_b.astype(jnp.bfloat16), 'mp', axis=0, tiled=True)  123 us
  transfers between devices with their start and end apart: 38, of which 34 were waited for; matrix products, arithmetic and copies ran while one was open for 13% of the time, Pallas kernels for 0%

commit v1 on v0

--- a/solution.py
+++ b/solution.py
@@ -3,6 +3,8 @@
 import jax
 import jax.numpy as jnp
 from jax import lax
+from jax.experimental import pallas as pl
+from jax.experimental.pallas import tpu as pltpu
 from jax.sharding import PartitionSpec as P
 
 HEAD = 64
@@ -228,6 +230,757 @@
     )
 
 
+BF = jnp.bfloat16
+F32 = jnp.float32
+VMEM_LIMIT = 62 << 20
+EXP_SCALE = 0.125 * math.log2(math.e)
+HOLD = pl.Buffered(1)
+ANY = pl.BlockSpec(memory_space=pl.ANY)
+
+
+def contract(left, right, left_dim, right_dim):
+    return lax.dot_general(
+        left, right, (((left_dim,), (right_dim,)), ((), ())), preferred_element_type=F32
+    )
+
+
+def call(body, meta, args, grid, in_specs, out_specs, out_shape, flops, scratch=(), aliases=None):
+    moved = sum(a.size * a.dtype.itemsize for a in args)
+    moved += sum(math.prod(o.shape) * jnp.dtype(o.dtype).itemsize for o in out_shape)
+    return pl.pallas_call(
+        body,
+        grid_spec=pltpu.PrefetchScalarGridSpec(
+            num_scalar_prefetch=1,
+            grid=grid,
+            in_specs=in_specs,
+            out_specs=out_specs,
+            scratch_shapes=list(scratch),
+        ),
+        out_shape=out_shape,
+        input_output_aliases=aliases or {},
+        compiler_params=pltpu.CompilerParams(vmem_limit_bytes=VMEM_LIMIT),
+        cost_estimate=pl.CostEstimate(flops=int(flops), bytes_accessed=int(moved), transcendentals=0),
+    )(meta, *args)
+
+
+def shape(dims, kind=BF):
+    return jax.ShapeDtypeStruct(tuple(dims), kind)
+
+
+def normalize(values):
+    center = values - jnp.mean(values, axis=-1, keepdims=True)
+    spread = jnp.mean(center * center, axis=-1, keepdims=True)
+    root = lax.rsqrt(spread + 1e-05)
+    return center * root, root
+
+
+def norm_back(d_out, unit, root, gain):
+    d_unit = d_out * gain
+    return root * (
+        d_unit
+        - jnp.mean(d_unit, axis=-1, keepdims=True)
+        - unit * jnp.mean(d_unit * unit, axis=-1, keepdims=True)
+    )
+
+
+def first_proj(meta, s, tok, recv, gain, weight, prev):
+    _, rows, width = tok.shape
+    part = weight.shape[2]
+    seqs = gain.shape[0]
+
+    def body(m, loc, rec, g, w, *refs):
+        tokf, hid, qkv = refs[-3:]
+
+        @pl.when(pl.program_id(0) == m[0])
+        def _():
+            tokf[0] = loc[0]
+
+        @pl.when(pl.program_id(0) != m[0])
+        def _():
+            tokf[0] = rec[0]
+
+        unit, _ = normalize(tokf[0].astype(F32))
+        hidden = (unit * g[0]).astype(BF)
+        hid[0] = hidden
+        for c in range(3):
+            qkv[0, c] = contract(w[c], hidden, 0, 1).astype(BF)
+
+    length = 2 * rows
+    outs = [shape((seqs, length, width)), shape((seqs, length, width)), shape((seqs, 3, part, length))]
+    return call(
+        body,
+        meta,
+        [tok, recv, gain, weight] + list(prev),
+        (2,),
+        [
+            pl.BlockSpec((1, rows, width), lambda h, m: (m[1 + s], 0, 0)),
+            pl.BlockSpec((1, rows, width), lambda h, m: (0, 0, 0)),
+            pl.BlockSpec((1, 1, width), lambda h, m: (s, 0, 0)),
+            pl.BlockSpec((3, width, part), lambda h, m: (0, 0, 0), pipeline_mode=HOLD),
+        ]
+        + [ANY] * len(prev),
+        [
+            pl.BlockSpec((1, rows, width), lambda h, m: (s, h, 0)),
+            pl.BlockSpec((1, rows, width), lambda h, m: (s, h, 0)),
+            pl.BlockSpec((1, 3, part, rows), lambda h, m: (s, 0, 0, h)),
+        ],
+        outs,
+        6 * length * width * part,
+        aliases={5 + i: i for i in range(len(prev))},
+    )
+
+
+def other_proj(meta, hid, weight, s, prev):
+    seqs, length, width = hid.shape
+    part = weight.shape[2]
+    rows = length // 2
+
+    def body(m, h_ref, w, *refs):
+        for c in range(3):
+            refs[-1][0, c] = contract(w[c], h_ref[0], 0, 1).astype(BF)
+
+    return call(
+        body,
+        meta,
+        [hid, weight] + list(prev),
+        (2,),
+        [
+            pl.BlockSpec((1, rows, width), lambda h, m: (s, h, 0)),
+            pl.BlockSpec((3, width, part), lambda h, m: (0, 0, 0), pipeline_mode=HOLD),
+        ]
+        + [ANY] * len(prev),
+        [pl.BlockSpec((1, 3, part, rows), lambda h, m: (s, 0, 0, h))],
+        [shape((seqs, 3, part, length))],
+        6 * length * width * part,
+        aliases={3 + i: i for i in range(len(prev))},
+    )
+
+
+def mask_rows(valid, length, block):
+    first = lax.broadcasted_iota(jnp.int32, (16, length), 0) == 0
+    hidden = lax.broadcasted_iota(jnp.int32, (16, length), 1) >= valid
+    keys = jnp.where(first & hidden, -1e30, 0.0).astype(BF)
+    ones = jnp.where(lax.broadcasted_iota(jnp.int32, (16, block), 0) == 0, 1.0, 0.0).astype(BF)
+    return keys, ones
+
+
+def attention(meta, qkv, first, count, prev):
+    seqs, _, part, length = qkv.shape
+    heads = part // HEAD
+    view = qkv.reshape(seqs, 3, heads, HEAD, length)
+    lens_at = 1 + seqs
+
+    def body(m, q, k, v, *refs):
+        out, logs = refs[-2:]
+        valid = m[lens_at + first + pl.program_id(0)]
+        key_mask, ones = mask_rows(valid, length, length)
+        scores = contract(
+            jnp.concatenate([k[0, 0, 0], key_mask], 0), jnp.concatenate([q[0, 0, 0], ones], 0), 0, 0
+        )
+        top = jnp.max(scores, 0, keepdims=True)
+        expo = jnp.exp2((scores - top) * EXP_SCALE)
+        total = jnp.sum(expo, 0, keepdims=True)
+        mixed = contract(v[0, 0, 0], expo.astype(BF), 1, 0)
+        out[0, 0] = (mixed / total).astype(BF)
+        logs[0, 0] = top * EXP_SCALE + jnp.log2(total)
+
+    def spec(c):
+        return pl.BlockSpec((1, 1, 1, HEAD, length), lambda s, h, m: (s + first, c, h, 0, 0))
+
+    return call(
+        body,
+        meta,
+        [view, view, view] + list(prev),
+        (count, heads),
+        [spec(0), spec(1), spec(2)] + [ANY] * len(prev),
+        [
+            pl.BlockSpec((1, 1, HEAD, length), lambda s, h, m: (s + first, h, 0, 0)),
+            pl.BlockSpec((1, 1, 1, length), lambda s, h, m: (s + first, h, 0, 0)),
+        ],
+        [shape((seqs, heads, HEAD, length)), shape((seqs, heads, 1, length), F32)],
+        16 * count * heads * length * length * HEAD,
+        aliases={4 + i: i for i in range(len(prev))},
+    )
+
+
+def attention_back(meta, qkv, out, d_out, logs, first, prev):
+    seqs, _, part, length = qkv.shape
+    heads = part // HEAD
+    view = qkv.reshape(seqs, 3, heads, HEAD, length)
+    lens_at = 1 + seqs
+    block = min(256, length)
+    group = 2 if heads % 2 == 0 else 1
+
+    def body(m, q, k, v, o, do, ls, *refs):
+        d_qkv, dk_sum, dv_sum = refs[-3:]
+        valid = m[lens_at + first]
+        key_mask, ones = mask_rows(valid, length, block)
+        for h in range(group):
+            keys = k[0, 0, h]
+            masked_keys = jnp.concatenate([keys, key_mask], 0)
+            for i in range(length // block):
+                sl = slice(i * block, (i + 1) * block)
+                query = q[0, 0, h, :, sl]
+                d_mix = do[0, h, :, sl]
+                scores = contract(masked_keys, jnp.concatenate([query, ones], 0), 0, 0)
+                probs = jnp.exp2(scores * EXP_SCALE - ls[0, h, :, sl])
+                inner = jnp.sum(d_mix.astype(F32) * o[0, h, :, sl].astype(F32), 0, keepdims=True)
+                d_probs = contract(v[0, 0, h], d_mix, 0, 0)
+                d_raw = (probs * (d_probs - inner) * 0.125).astype(BF)
+                d_value = contract(d_mix, probs.astype(BF), 1, 1)
+                d_key = contract(query, d_raw, 1, 1)
+                if i == 0:
+                    dk_sum[...] = d_key
+                    dv_sum[...] = d_value
+                else:
+                    dk_sum[...] += d_key
+                    dv_sum[...] += d_value
+                d_qkv[0, 0, h, :, sl] = contract(keys, d_raw, 1, 0).astype(BF)
+            d_qkv[0, 1, h] = dk_sum[...].astype(BF)
+            d_qkv[0, 2, h] = dv_sum[...].astype(BF)
+
+    def spec(c):
+        return pl.BlockSpec((1, 1, group, HEAD, length), lambda h, m: (first, c, h, 0, 0))
+
+    head_spec = pl.BlockSpec((1, group, HEAD, length), lambda h, m: (first, h, 0, 0))
+    return call(
+        body,
+        meta,
+        [view, view, view, out, d_out, logs] + list(prev),
+        (heads // group,),
+        [
+            spec(0),
+            spec(1),
+            spec(2),
+            head_spec,
+            head_spec,
+            pl.BlockSpec((1, group, 1, length), lambda h, m: (first, h, 0, 0)),
+        ]
+        + [ANY] * len(prev),
+        [pl.BlockSpec((1, 3, group, HEAD, length), lambda h, m: (first, 0, h, 0, 0))],
+        [shape((seqs, 3, heads, HEAD, length))],
+        40 * heads * length * length * HEAD,
+        scratch=[pltpu.VMEM((HEAD, length), F32)] * 2,
+        aliases={7 + i: i for i in range(len(prev))},
+    )
+
+
+def out_proj(meta, own_mix, oth_mix, tokf, cot, cot_recv, own_w, oth_w, gain):
+    seqs, length, width = tokf.shape
+    rows = length // 2
+    part = own_w.shape[0]
+    own_mix = own_mix.reshape(seqs, part, length)
+    oth_mix = oth_mix.reshape(seqs, part, length)
+
+    def body(m, a, b, t, cl, cr, wa, wb, g, resid, hid, cotf):
+        @pl.when(pl.program_id(1) == m[0])
+        def _():
+            cotf[0] = cl[0]
+
+        @pl.when(pl.program_id(1) != m[0])
+        def _():
+            cotf[0] = cr[0]
+
+        branch = contract(a[0], wa[...], 0, 0) + contract(b[0], wb[...], 0, 0)
+        total = t[0].astype(F32) + branch
+        resid[0] = total.astype(BF)
+        unit, _ = normalize(total)
+        hid[0] = (unit * g[0]).astype(BF)
+
+    mix_spec = pl.BlockSpec((1, part, rows), lambda s, h, m: (s, 0, h))
+    row_spec = pl.BlockSpec((1, rows, width), lambda s, h, m: (s, h, 0))
+    w_spec = pl.BlockSpec((part, width), lambda s, h, m: (0, 0), pipeline_mode=HOLD)
+    return call(
+        body,
+        meta,
+        [own_mix, oth_mix, tokf, cot, cot_recv, own_w, oth_w, gain],
+        (seqs, 2),
+        [
+            mix_spec,
+            mix_spec,
+            row_spec,
+            pl.BlockSpec((1, rows, width), lambda s, h, m: (m[1 + s], 0, 0)),
+            pl.BlockSpec((1, rows, width), lambda s, h, m: (s, 0, 0)),
+            w_spec,
+            w_spec,
+            pl.BlockSpec((1, 1, width), lambda s, h, m: (s, 0, 0)),
+        ],
+        [row_spec] * 3,
+        [shape((seqs, length, width))] * 3,
+        4 * seqs * length * width * part,
+    )
+
+
+def feed_forward(meta, hid, cot, up_w, down_w, sums):
+    seqs, length, width = hid.shape
+    tokens = seqs * length
+    hidden = up_w.shape[1]
+    block = min(512, hidden)
+    rows = min(512, tokens)
+    steps = hidden // block
+    last = len(sums) > 0
+    half_root = 1.0 / math.sqrt(2.0)
+    density = 1.0 / math.sqrt(2.0 * math.pi)
+
+    def body(m, h_ref, c_ref, wu, wd, *refs):
+        sums_in = refs[: len(sums)]
+        out, d_hid, grads, act, d_up, out_sum, hid_sum, stage, sem = refs[len(sums) :]
+        step = pl.program_id(0)
+
+        def moves(r):
+            sl = pl.ds(r * rows, rows)
+            if last:
+                return [
+                    pltpu.make_async_copy(sums_in[0].at[sl], out_sum.at[sl], sem.at[0, r]),
+                    pltpu.make_async_copy(sums_in[1].at[sl], hid_sum.at[sl], sem.at[1, r]),
+                ]
+            return [
+                pltpu.make_async_copy(out_sum.at[sl], out.at[sl], sem.at[0, r]),
+                pltpu.make_async_copy(hid_sum.at[sl], d_hid.at[sl], sem.at[1, r]),
+            ]
+
+        def stores(r):
+            sl = pl.ds(r * rows, rows)
+            return [
+                pltpu.make_async_copy(stage.at[0, r], out.at[sl], sem.at[0, r]),
+                pltpu.make_async_copy(stage.at[1, r], d_hid.at[sl], sem.at[1, r]),
+            ]
+
+        count = tokens // rows
+
+        @pl.when(step == 0)
+        def _():
+            if last:
+                for r in range(count):
+                    for move in moves(r):
+                        move.start()
+            else:
+                out_sum[...] = jnp.zeros_like(out_sum)
+                hid_sum[...] = jnp.zeros_like(hid_sum)
+
+        for r in range(count):
+            sl = slice(r * rows, (r + 1) * rows)
+            up = contract(h_ref[sl, :], wu[...], 1, 0)
+            d_act = contract(c_ref[sl, :], wd[...], 1, 1)
+            cdf = 0.5 * (1.0 + lax.erf(up * half_root))
+            slope = cdf + up * (density * jnp.exp(-0.5 * up * up))
+            a = (up * cdf).astype(BF)
+            d = (d_act * slope).astype(BF)
+            act[sl, :] = a
+            d_up[sl, :] = d
+            if last:
+
+                @pl.when(step == 0)
+                def _():
+                    for move in moves(r):
+                        move.wait()
+
+            out_sum[sl, :] += contract(a, wd[...], 1, 0)
+            hid_sum[sl, :] += contract(d, wu[...], 1, 1)
+
+            @pl.when(step == steps - 1)
+            def _():
+                if last:
+                    stage[0, r] = out_sum[sl, :].astype(BF)
+                    stage[1, r] = hid_sum[sl, :].astype(BF)
+                for move in stores(r) if last else moves(r):
+                    move.start()
+
+        grads[0] = contract(h_ref[...], d_up[...], 0, 0).astype(BF)
+        grads[1] = contract(c_ref[...], act[...], 0, 0).astype(BF)
+
+        @pl.when(step == steps - 1)
+        def _():
+            for r in range(count):
+                for move in stores(r) if last else moves(r):
+                    move.wait()
+
+    kind = BF if last else F32
+    full = pl.BlockSpec((tokens, width), lambda j, m: (0, 0), pipeline_mode=HOLD)
+    staged = (2, tokens // rows, rows, width) if last else (1, 1, 16, 128)
+    return call(
+        body,
+        meta,
+        [hid.reshape(tokens, width), cot.reshape(tokens, width), up_w, down_w] + list(sums),
+        (steps,),
+        [
+            full,
+            full,
+            pl.BlockSpec((width, block), lambda j, m: (0, j)),
+            pl.BlockSpec((block, width), lambda j, m: (j, 0)),
+        ]
+        + [ANY] * len(sums),
+        [ANY, ANY, pl.BlockSpec((2, width, block), lambda j, m: (0, 0, j))],
+        [shape((tokens, width), kind), shape((tokens, width), kind), shape((2, width, hidden))],
+        12 * tokens * width * hidden,
+        scratch=[
+            pltpu.VMEM((tokens, block), BF),
+            pltpu.VMEM((tokens, block), BF),
+            pltpu.VMEM((tokens, width), F32),
+            pltpu.VMEM((tokens, width), F32),
+            pltpu.VMEM(staged, BF),
+            pltpu.SemaphoreType.DMA((2, tokens // rows)),
+        ],
+    )
+
+
+def middle(meta, resid, mlp, d_hid, cotf, own_mix, oth_mix, own_w, oth_w, gain, items):
+    seqs, length, width = resid.shape
+    rows = length // 2
+    part = own_w.shape[0]
+    mixes = [a.reshape(seqs, part, length) for a in (own_mix, oth_mix)]
+    mlp = mlp.reshape(resid.shape)
+    d_hid = d_hid.reshape(resid.shape)
+
+    def body(m, res, up, dh, ct, ma, mb, wa, wb, g, mine, away, branch, dma, dmb, grad, gsum, grad_sum, vec):
+        phase, s = pl.program_id(0), pl.program_id(1)
+
+        @pl.when((phase == 0) & (s == 0))
+        def _():
+            grad_sum[...] = jnp.zeros_like(grad_sum)
+            vec[...] = jnp.zeros_like(vec)
+
+        resid_f = res[0].astype(F32)
+        total = (resid_f + up[0].astype(F32)).astype(BF)
+
+        @pl.when(phase == 0)
+        def _():
+            away[0] = total
+
+        @pl.when(phase == 1)
+        def _():
+            mine[0] = total
+
+        unit, root = normalize(resid_f)
+        d_out = dh[0].astype(F32)
+        vec[s] += jnp.sum(d_out * unit, axis=0, keepdims=True)
+        d_res = (ct[0].astype(F32) + norm_back(d_out, unit, root, g[0])).astype(BF)
+        branch[0] = d_res
+        dma[0] = contract(wa[...], d_res, 1, 1).astype(BF)
+        dmb[0] = contract(wb[...], d_res, 1, 1).astype(BF)
+        grad_sum[0] += contract(d_res, ma[0], 0, 1)
+        grad_sum[1] += contract(d_res, mb[0], 0, 1)
+
+        @pl.when((phase == 1) & (s == seqs - 1))
+        def _():
+            grad[...] = grad_sum[...].astype(BF)
+            gsum[...] = vec[...]
+
+    def at(p, m):
+        return (1 - m[0]) + p * (2 * m[0] - 1)
+
+    row_spec = pl.BlockSpec((1, rows, width), lambda p, s, m: (s, at(p, m), 0))
+    mix_spec = pl.BlockSpec((1, part, rows), lambda p, s, m: (s, 0, at(p, m)))
+    w_spec = pl.BlockSpec((part, width), lambda p, s, m: (0, 0), pipeline_mode=HOLD)
+    return call(
+        body,
+        meta,
+        [resid, mlp, d_hid, cotf, mixes[0], mixes[1], own_w, oth_w, gain],
+        (2, seqs),
+        [row_spec] * 4
+        + [mix_spec] * 2
+        + [w_spec] * 2
+        + [pl.BlockSpec((1, 1, width), lambda p, s, m: (s, 0, 0))],
+        [
+            pl.BlockSpec((1, rows, width), lambda p, s, m: (m[1 + p * s], 0, 0)),
+            pl.BlockSpec((1, rows, width), lambda p, s, m: (s + p * (seqs - 1 - s), 0, 0)),
+            row_spec,
+            mix_spec,
+            mix_spec,
+            pl.BlockSpec((2, width, part), lambda p, s, m: (0, 0, 0), pipeline_mode=HOLD),
+            pl.BlockSpec((seqs, 1, width), lambda p, s, m: (0, 0, 0)),
+        ],
+        [
+            shape((items, rows, width)),
+            shape((seqs, rows, width)),
+            shape((seqs, length, width)),
+            shape((seqs, part, length)),
+            shape((seqs, part, length)),
+            shape((2, width, part)),
+            shape((seqs, 1, width), F32),
+        ],
+        8 * seqs * length * width * part,
+        scratch=[pltpu.VMEM((2, width, part), F32), pltpu.VMEM((seqs, 1, width), F32)],
+    )
+
+
+def proj_grad(meta, hid, d_qkv):
+    seqs, length, width = hid.shape
+    part = d_qkv.shape[2] * d_qkv.shape[3]
+    d_qkv = d_qkv.reshape(seqs, 3, part, length)
+
+    def body(m, h_ref, d_ref, grad):
+        total = contract(d_ref[0, 0], h_ref[0], 1, 0)
+        for s in range(1, seqs):
+            total += contract(d_ref[s, 0], h_ref[s], 1, 0)
+        grad[0] = total.astype(BF).T
+
+    return call(
+        body,
+        meta,
+        [hid, d_qkv],
+        (3,),
+        [
+            pl.BlockSpec((seqs, length, width), lambda c, m: (0, 0, 0), pipeline_mode=HOLD),
+            pl.BlockSpec((seqs, 1, part, length), lambda c, m: (0, c, 0, 0)),
+        ],
+        [pl.BlockSpec((1, width, part), lambda c, m: (c, 0, 0))],
+        [shape((3, width, part))],
+        6 * seqs * length * width * part,
+    )[0]
+
+
+def input_back(meta, tokf, branch, own_d, oth_d, own_w, oth_w, gain, items, stay, first, count):
+    seqs, length, width = tokf.shape
+    rows = length // 2
+    part = own_w.shape[2]
+    own_d = own_d.reshape(seqs, 3, part, length)
+    oth_d = oth_d.reshape(seqs, 3, part, length)
+
+    def body(m, tok, br, da, db, wa, wb, g, out, gsum):
+        d_hid = contract(da[0, 0], wa[0], 0, 1) + contract(db[0, 0], wb[0], 0, 1)
+        for c in range(1, 3):
+            d_hid += contract(da[0, c], wa[c], 0, 1) + contract(db[0, c], wb[c], 0, 1)
+        unit, root = normalize(tok[0].astype(F32))
+        gsum[0] = jnp.sum(d_hid * unit, axis=0, keepdims=True)
+        out[0] = (br[0].astype(F32) + norm_back(d_hid, unit, root, g[0])).astype(BF)
+
+    def at(m):
+        return m[0] if stay else 1 - m[0]
+
+    row_spec = pl.BlockSpec((1, rows, width), lambda s, m: (s + first, at(m), 0))
+    d_spec = pl.BlockSpec((1, 3, part, rows), lambda s, m: (s + first, 0, 0, at(m)))
+    w_spec = pl.BlockSpec((3, width, part), lambda s, m: (0, 0, 0), pipeline_mode=HOLD)
+    return call(
+        body,
+        meta,
+        [tokf, branch, own_d, oth_d, own_w, oth_w, gain],
+        (count,),
+        [row_spec, row_spec, d_spec, d_spec, w_spec, w_spec]
+        + [pl.BlockSpec((1, 1, width), lambda s, m: (s + first, 0, 0))],
+        [
+            pl.BlockSpec((1, rows, width), lambda s, m: (m[1 + s] if stay else s, 0, 0)),
+            pl.BlockSpec((1, 1, width), lambda s, m: (s, 0, 0)),
+        ],
+        [shape((items if stay else count, rows, width)), shape((count, 1, width), F32)],
+        12 * count * rows * width * part,
+    )
+
+
+def place(meta, base, came, first, seqs):
+    count, rows, width = came.shape
+    at = 1 + 2 * seqs + first
+
+    def body(m, src, _, out):
+        out[...] = src[...]
+
+    return call(
+        body,
+        meta,
+        [came, base],
+        (count,),
+        [pl.BlockSpec((1, rows, width), lambda s, m: (s, 0, 0)), ANY],
+        [pl.BlockSpec((1, rows, width), lambda s, m: (m[at + s], 0, 0))],
+        [shape(base.shape)],
+        1,
+        aliases={2: 0},
+    )[0]
+
+
+def after(value, *earlier):
+    return lax.optimization_barrier((value,) + earlier)[0]
+
+
+def per_device_pair(
+    tokens,
+    lengths,
+    timesteps,
+    norm_gains,
+    time_weight,
+    qkv_weight,
+    out_weight,
+    up_weight,
+    down_weight,
+    cotangent,
+):
+    micro_count, seq_dev, rows, width = tokens.shape
+    items = micro_count * seq_dev
+    seqs = items // 2
+    x = lax.axis_index("mp")
+    dp = lax.axis_index("dp")
+    dp_count = lax.axis_size("dp")
+    part = qkv_weight.shape[2]
+    hidden = up_weight.shape[1]
+    tok = tokens.reshape(items, rows, width)
+    cot = cotangent.reshape(items, rows, width)
+    lens = lengths.reshape(items)
+    own = x * seqs + jnp.arange(seqs, dtype=jnp.int32)
+    oth = (1 - x) * seqs + jnp.arange(seqs, dtype=jnp.int32)
+    meta = jnp.concatenate([x[None].astype(jnp.int32), own, lens[own], oth]).astype(jnp.int32)
+    steps = timesteps.reshape(items)
+
+    def swap(value):
+        return lax.ppermute(value, "mp", [(0, 1), (1, 0)])
+
+    def shard(value):
+        count = value.shape[0] // dp_count
+        return lax.dynamic_slice_in_dim(value, dp * count, count, 0)
+
+    def spread(value):
+        return lax.all_gather(value, "dp", axis=0, tiled=True)
+
+    qkv_rows = qkv_weight.reshape(3 * width, part)
+    qkv_shard = swap(shard(qkv_rows))
+    qkv_oth = spread(qkv_shard).reshape(qkv_weight.shape)
+    def sent(rows_of, s, count):
+        return lax.dynamic_slice_in_dim(rows_of, (1 - x) * seqs + s, count, 0)
+
+    tok_recv = [swap(sent(tok, 0, 1))]
+
+    feats = sinusoid(lax.dynamic_slice_in_dim(steps, x * seqs, seqs, 0))
+    pairs = jnp.dot(feats, time_weight, precision=lax.Precision.HIGHEST)
+    widened = 1.0 + pairs.reshape(seqs, 2, 1, width)
+    gain_a = norm_gains[0] * widened[:, 0]
+    gain_b = norm_gains[1] * widened[:, 1]
+
+    far_shards = [swap(after(shard(w), tok_recv[0])) for w in (out_weight, up_weight, down_weight)]
+    base, qkv_far, mix_own, mix_oth = (), (), (), ()
+    for s in range(seqs):
+        base = first_proj(meta, s, tok, tok_recv[s], gain_a, qkv_weight, base)
+        mix_own = attention(meta, base[2], s, 1, mix_own)
+        if s == 0:
+            out_oth, up_oth, down_oth = [spread(after(w, mix_own[1])) for w in far_shards]
+        if s + 1 < seqs:
+            tok_recv.append(swap(after(sent(tok, s + 1, 1), mix_own[1], *far_shards)))
+        qkv_far = other_proj(meta, base[1], qkv_oth, s, qkv_far)
+        mix_oth = attention(meta, qkv_far[0], s, 1, mix_oth)
+        if s == 0:
+            cot_recv = swap(after(sent(cot, 0, seqs), mix_oth[1], tok_recv[-1]))
+    tokf, hid_a, qkv_own = base
+    qkv_far = qkv_far[0]
+    resid, hid_b, cotf = out_proj(
+        meta, mix_own[0], mix_oth[0], tokf, cot, cot_recv, out_weight, out_oth, gain_b
+    )
+    out_part, hid_part, grads_own = feed_forward(meta, hid_b, cotf, up_weight, down_weight, ())
+    mlp, d_hid_b, grads_oth = feed_forward(meta, hid_b, cotf, up_oth, down_oth, (out_part, hid_part))
+
+    def tree_send(value, step):
+        count, cols = value.shape[0], value.shape[-1]
+        value = value.reshape(count, -1, 1, 2, width // dp_count, cols)
+        mine_at = dp // step % 2
+        keep = lax.dynamic_index_in_dim(value, mine_at, 3, False)
+        send = lax.dynamic_index_in_dim(value, 1 - mine_at, 3, False)
+        return keep, lax.ppermute(send, "dp", [(i, i ^ step) for i in range(dp_count)])
+
+    def tree_add(pair, gate):
+        keep, came = pair[0], after(pair[1], *gate)
+        return (keep.astype(F32) + came.astype(F32)).astype(BF)
+
+    def tree(value):
+        step = 1
+        while step < dp_count:
+            pair = tree_send(value, step)
+            value = tree_add(pair, (yield value))
+            step *= 2
+        yield value.reshape(value.shape[0], width // dp_count, value.shape[-1])
+
+    def reduce(value):
+        return lax.psum_scatter(value, "dp", scatter_dimension=1, tiled=True)
+
+    ffn_own = reduce(grads_own)
+    ffn_oth = reduce(grads_oth)
+    out_stay, out_away, branch, d_mix_own, d_mix_oth, out_grads, sum_b = middle(
+        meta, resid, mlp, d_hid_b, cotf, mix_own[0], mix_oth[0], out_weight, out_oth, gain_b, items
+    )
+    out_came = swap(out_away)
+
+    def heads_view(value):
+        return value.reshape(seqs, part // HEAD, HEAD, 2 * rows)
+
+    class Job:
+        def __init__(self, value):
+            self.run, self.value, self.done = tree(value), None, False
+            self.value = next(self.run)
+
+        def go(self, *gate):
+            if not self.done:
+                try:
+                    self.value = self.run.send(gate)
+                except StopIteration:
+                    self.done = True
+            return self.value
+
+    d_mix_own, d_mix_oth = heads_view(d_mix_own), heads_view(d_mix_oth)
+    jobs = [Job(out_grads)]
+    d_oth, d_own = (), ()
+    order = meta
+
+    def ready(*gate):
+        return after(meta, *[job.go(*gate) for job in jobs])
+
+    for s in range(seqs):
+        d_oth = attention_back(order, qkv_far, mix_oth[0], d_mix_oth, mix_oth[1], s, d_oth)
+        order = ready(d_oth[0])
+    grad_oth = proj_grad(order, hid_a, d_oth[0])
+    jobs.append(Job(grad_oth))
+    order = after(meta, grad_oth, ffn_own)
+    for s in range(seqs):
+        d_own = attention_back(order, qkv_own, mix_own[0], d_mix_own, mix_own[1], s, d_own)
+        order = ready(d_own[0])
+    grad_own = proj_grad(order, hid_a, d_own[0])
+    order = ready(grad_own)
+    jobs.append(Job(grad_own))
+    in_away, sums_a = [], []
+    for s in range(seqs):
+        rows_out, vec = input_back(
+            order, tokf, branch, d_own[0], d_oth[0], qkv_weight, qkv_oth, gain_a, items, False, s, 1
+        )
+        in_away.append(swap(rows_out))
+        sums_a.append(vec)
+        order = ready(rows_out)
+    in_stay, sum_stay = input_back(
+        after(order, ffn_oth), tokf, branch, d_own[0], d_oth[0], qkv_weight, qkv_oth, gain_a, items, True, 0, seqs
+    )
+    sum_a = jnp.concatenate(sums_a, 0) + sum_stay
+    for job in jobs:
+        while not job.done:
+            job.go(in_stay)
+    out_red, qkv_red_oth, qkv_red_own = [job.value for job in jobs]
+    output = place(meta, out_stay, out_came, 0, seqs)
+    input_grad = in_stay
+    for s in range(seqs):
+        input_grad = place(meta, input_grad, in_away[s], s, seqs)
+
+    ffn = ffn_own.astype(F32) + swap(ffn_oth).astype(F32)
+    out_sum = out_red[0].astype(F32) + swap(out_red[1]).astype(F32)
+    qkv_sum = qkv_red_own.astype(F32) + swap(qkv_red_oth).astype(F32)
+
+    sums = jnp.stack([sum_a, sum_b], 0)[:, :, 0]
+    d_pair = sums * norm_gains[:, None, :]
+    gain_part = jnp.sum(sums * jnp.swapaxes(widened[:, :, 0], 0, 1), axis=1)
+    count = 2 * dp_count
+    cols, gain_cols, time_cols = 2 * width // count, width // count, feats.shape[1]
+    by_pair = jnp.moveaxis(d_pair.reshape(2, seqs, dp_count, cols), 1, 2).reshape(count, seqs * cols)
+    by_gain = jnp.moveaxis(gain_part.reshape(2, count, gain_cols), 0, 1).reshape(count, 2 * gain_cols)
+    by_feat = jnp.broadcast_to(feats.reshape(1, seqs * time_cols), (count, seqs * time_cols))
+    packed = jnp.concatenate([by_pair, by_gain, by_feat], 1)
+    everyone = lax.all_to_all(packed, ("dp", "mp"), 0, 0, tiled=True)
+    mine = everyone[:, : seqs * cols].reshape(count * seqs, cols)
+    gains_grad = jnp.sum(everyone[:, seqs * cols :][:, : 2 * gain_cols], axis=0).reshape(2, gain_cols)
+    all_feats = everyone[:, seqs * cols + 2 * gain_cols :].reshape(count * seqs, time_cols)
+    time_grad = jnp.dot(all_feats.T, mine, precision=lax.Precision.HIGHEST)
+    return (
+        output.reshape(tokens.shape),
+        input_grad.reshape(tokens.shape),
+        qkv_sum,
+        out_sum.T,
+        ffn[0],
+        ffn[1].T,
+        gains_grad,
+        time_grad,
+    )
+
+
 def solution(mesh):
     in_specs = (
         P(None, "dp", "mp", None),
@@ -251,6 +1004,8 @@
         P(None, ("dp", "mp")),
         P(None, ("dp", "mp")),
     )
+    dp_count = mesh.shape["dp"]
+    paired = mesh.shape["mp"] == 2 and dp_count & (dp_count - 1) == 0
     return jax.shard_map(
-        per_device, mesh=mesh, in_specs=in_specs, out_specs=out_specs, check_vma=False
-    )
+        per_device_pair if paired else per_device, mesh=mesh, in_specs=in_specs, out_specs=out_specs, check_vma=False
+    )

time: 2630 us -> 600 us (0.23)
  waiting for transfers between devices: 1270 us -> 59.7 us
  matrix products: 1000 us -> 1.98 us
  Pallas kernels: 0 us -> 438 us
  other arithmetic: 190 us -> 21.8 us
  local copies, waits for them, and re-layouts: 139 us -> 26.4 us
    dot_general x106 -> x2, matrix products: 1000 us -> 1.98 us  [the longest x1 1.1 us: per_device_pair(): pairs = jnp.dot(feats, time_weight, precision=lax.Precision.HIGHEST)]
    reduce_scatter x21 -> x2, waiting for transfers between devices: 734 us -> 0.01 us  [reduce(): return lax.psum_scatter(value, 'dp', scatter_dimension=1, tiled=True)]
    pallas_call x0 -> x24, Pallas kernels: none -> 438 us  [call(): pl.pallas_call(body, grid_spec=pltpu.PrefetchScalarGridSpec(num_scalar_pr...]
    all_gather x16 -> x4, waiting for transfers between devices: 422 us -> 0.02 us  [spread(): return lax.all_gather(value, 'dp', axis=0, tiled=True)]
    unnamed x7 -> x6, waiting for transfers between devices: 110 us -> 0.1 us
    reduce_sum x40 -> x2, other arithmetic: 104 us -> 0.06 us  [the longest x1 0.04 us: per_device_pair(): gain_part = jnp.sum(sums * jnp.swapaxes(widened[:, :, 0], 0, 1), axis=1)]
    while x355 -> x0, local copies, waits for them, and re-layouts: 89.1 us -> none
    ppermute x0 -> x25, waiting for transfers between devices: none -> 52.5 us  [the longest x13 32.6 us: swap(): return lax.ppermute(value, 'mp', [(0, 1), (1, 0)])]
  transfers between devices with their start and end apart: 38 -> 32, of which waited for: 34 -> 9; matrix products, arithmetic and copies ran while one was open for 13% -> 7% of each run, Pallas kernels for 0% -> 74%
where the time goes in v1:
time: 600 us; the launch traced here: 594 us
  Pallas kernels  438 us (73%)
  waiting for transfers between devices  59.7 us (10%)
  starting transfers between devices  30.3 us (5%)
  local copies, waits for them, and re-layouts  26.4 us (4%)
  other arithmetic  21.8 us (4%)
  between operations  15.2 us (3%)
    pallas_call x24, Pallas kernels, call(): pl.pallas_call(body, grid_spec=pltpu.PrefetchScalarGridSpec(num_scalar_pr...  438 us
    ppermute x13, waiting for transfers between devices, swap(): return lax.ppermute(value, 'mp', [(0, 1), (1, 0)])  32.6 us
    ppermute x12, waiting for transfers between devices, tree_send(): lax.ppermute(send, 'dp', [(i, i ^ step) for i in range(dp_count)])  19.9 us
    ppermute x13, starting transfers between devices, swap(): return lax.ppermute(value, 'mp', [(0, 1), (1, 0)])  15.6 us
    convert_element_type x10, other arithmetic, tree_add(): return (keep.astype(F32) + came.astype(F32)).astype(BF)  14.2 us
  transfers between devices with their start and end apart: 32, of which 9 were waited for; matrix products, arithmetic and copies ran while one was open for 7% of the time, Pallas kernels for 74%

profile of v1, /device:TPU:0, one launch (start us, length us, event | category | flops | bytes accessed | tf_op | source)
XLA Modules:
  0.0 593.5 jit_solution(18367248668190735119)
XLA Ops:
  7.3 1.1 constant_dynamic-slice_fusion.5
  8.3 3.0 collective-permute-start.5
  11.3 4.9 collective-permute-done.5
  17.0 2.7 dynamic-slice_bitcast_fusion.4
  19.7 1.7 collective-permute-start
  22.3 1.1 convolution_add_fusion
  26.1 18.2 %collective-permute-done.rec = bf16[1,512,1024]{2,1,0:T(8,128)(2,1)} collective-permute-done((bf16[1,512,1024]{2,1,0:T(8,128)(2,1)}, bf16[1,512,1024]{2,1,0:T(8,128)(2,1)}, u32[]{:S(2)}, u32[]{:S(2)}) %collective-permute-start) | collective-permute-done | bytes 1048608 | tf_op jit(solution)/shard_map/ppermute | solution.py:823
  44.4 1.4 collective-permute-start.1
  45.8 9.4 %shard_map.161 = (bf16[2,1024,1024]{2,1,0:T(8,128)(2,1)}, bf16[2,1024,1024]{2,1,0:T(8,128)(2,1)}, bf16[2,3,512,1024]{3,2,1,0:T(8,128)(2,1)}) custom-call(s32[7]{0:T(128)} %pad_add_fusion.m, bf16[4,512,1024]{2,1,0:T(8,128)(2,1)} %bitcast.183, bf16[1,512,1024]{2,1,0:T(8,128)(2,1)} %collective-permute-done.rec, f32[2,1,1024]{2,1,0:T(1,128)} %get-tuple-element.179.g, ...), custom_call_target="tpu_custom_call" | custom-call | flops 3221225472 | bytes 23076864 | tf_op jit(solution)/shard_map/pallas_call | solution.py:250
  55.2 16.2 %shard_map.162 = (bf16[2,8,64,1024]{3,2,1,0:T(8,128)(2,1)}, f32[2,8,1,1024]{3,2,1,0:T(1,128)}) custom-call(s32[7]{0:T(128)} %pad_add_fusion.m, bf16[2,3,8,64,1024]{4,3,2,1,0:T(8,128)(2,1)} %bitcast.189, bf16[2,3,8,64,1024]{4,3,2,1,0:T(8,128)(2,1)} %bitcast.190, bf16[2,3,8,64,1024]{4,3,2,1,0:T(8,128)(2,1)} %bitcast.191), custom_call_target="tpu_custom_call" | custom-call | flops 8589934592 | bytes 21037056 | tf_op jit(solution)/shard_map/pallas_call | solution.py:250
  72.2 1.0 constant_dynamic-slice_fusion.7
  73.8 5.8 collective-permute-done.2
  80.4 1.0 constant_dynamic-slice_fusion.6
  82.3 3.1 dynamic-slice_bitcast_fusion
  85.4 3.6 collective-permute-done.3
  90.3 7.8 %shard_map.165.refs_0_ = bf16[2,3,512,1024]{3,2,1,0:T(8,128)(2,1)} custom-call(s32[7]{0:T(128)} %pad_add_fusion.m, bf16[2,1024,1024]{2,1,0:T(8,128)(2,1)} %get-tuple-element.80.refs_1_.h_ref, bf16[3,1024,512]{2,1,0:T(8,128)(2,1)} %bitcast.155), custom_call_target="tpu_custom_call" | custom-call | flops 3221225472 | bytes 13631488 | tf_op jit(solution)/shard_map/pallas_call | solution.py:250
  98.1 16.2 %shard_map.167 = (bf16[2,8,64,1024]{3,2,1,0:T(8,128)(2,1)}, f32[2,8,1,1024]{3,2,1,0:T(1,128)}) custom-call(s32[7]{0:T(128)} %pad_add_fusion.m, bf16[2,3,8,64,1024]{4,3,2,1,0:T(8,128)(2,1)} %bitcast.169, bf16[2,3,8,64,1024]{4,3,2,1,0:T(8,128)(2,1)} %bitcast.170, bf16[2,3,8,64,1024]{4,3,2,1,0:T(8,128)(2,1)} %bitcast.171), custom_call_target="tpu_custom_call" | custom-call | flops 8589934592 | bytes 21037056 | tf_op jit(solution)/shard_map/pallas_call | solution.py:250
  114.3 1.4 collective-permute-start.6
  115.7 9.4 %shard_map.163 = (bf16[2,1024,1024]{2,1,0:T(8,128)(2,1)}, bf16[2,1024,1024]{2,1,0:T(8,128)(2,1)}, bf16[2,3,512,1024]{3,2,1,0:T(8,128)(2,1)}) custom-call(s32[7]{0:T(128)} %pad_add_fusion.m, bf16[4,512,1024]{2,1,0:T(8,128)(2,1)} %bitcast.184, ...), custom_call_target="tpu_custom_call", output_to_operand_aliasing={{0}: (5, {}), {1}: (6, {}), {2}: (7, {})} | custom-call | flops 3221225472 | bytes 37756928 | tf_op jit(solution)/shard_map/pallas_call | solution.py:250
  125.1 7.8 %shard_map.166 = bf16[2,3,512,1024]{3,2,1,0:T(8,128)(2,1)} custom-call(s32[7]{0:T(128)} %pad_add_fusion.m, bf16[2,1024,1024]{2,1,0:T(8,128)(2,1)} %get-tuple-element.84.h_ref, bf16[3,1024,512]{2,1,0:T(8,128)(2,1)} %bitcast.156, bf16[2,3,512,1024]{3,2,1,0:T(8,128)(2,1)} %shard_map.165.refs_0_), custom_call_target="tpu_custom_call", output_to_operand_aliasing={{}: (3, {})} | custom-call | flops 3221225472 | bytes 19922944 | tf_op jit(solution)/shard_map/pallas_call | solution.py:250
  132.9 16.2 %shard_map.164 = (bf16[2,8,64,1024]{3,2,1,0:T(8,128)(2,1)}, f32[2,8,1,1024]{3,2,1,0:T(1,128)}) custom-call(s32[7]{0:T(128)} %pad_add_fusion.m, bf16[2,3,8,64,1024]{4,3,2,1,0:T(8,128)(2,1)} %bitcast.192, bf16[2,3,8,64,1024]{4,3,2,1,0:T(8,128)(2,1)} %bitcast.193, bf16[2,3,8,64,1024]{4,3,2,1,0:T(8,128)(2,1)} %bitcast.194, ...), custom_call_target="tpu_custom_call", output_to_operand_aliasing={{0}: (4, {}), {1}: (5, {})} | custom-call | flops 8589934592 | bytes 23199744 | tf_op jit(solution)/shard_map/pallas_call | solution.py:250
  149.1 16.2 %shard_map.168 = (bf16[2,8,64,1024]{3,2,1,0:T(8,128)(2,1)}, f32[2,8,1,1024]{3,2,1,0:T(1,128)}) custom-call(s32[7]{0:T(128)} %pad_add_fusion.m, bf16[2,3,8,64,1024]{4,3,2,1,0:T(8,128)(2,1)} %bitcast.172, bf16[2,3,8,64,1024]{4,3,2,1,0:T(8,128)(2,1)} %bitcast.173, bf16[2,3,8,64,1024]{4,3,2,1,0:T(8,128)(2,1)} %bitcast.174, ...), custom_call_target="tpu_custom_call", output_to_operand_aliasing={{0}: (4, {}), {1}: (5, {})} | custom-call | flops 8589934592 | bytes 23199744 | tf_op jit(solution)/shard_map/pallas_call | solution.py:250
  165.3 14.8 %shard_map.169 = (bf16[2,1024,1024]{2,1,0:T(8,128)(2,1)}, bf16[2,1024,1024]{2,1,0:T(8,128)(2,1)}, bf16[2,1024,1024]{2,1,0:T(8,128)(2,1)}) custom-call(s32[7]{0:T(128)} %pad_add_fusion.m, bf16[2,512,1024]{2,1,0:T(8,128)(2,1)} %bitcast.211, bf16[2,512,1024]{2,1,0:T(8,128)(2,1)} %bitcast.213, bf16[2,1024,1024]{2,1,0:T(8,128)(2,1)} %get-tuple-element.88.t.tok, ...), custom_call_target="tpu_custom_call" | custom-call | flops 4294967296 | bytes 29368320 | tf_op jit(solution)/shard_map/pallas_call | solution.py:250
  180.1 64.0 %shard_map.170 = (f32[2048,1024]{1,0:T(8,128)}, f32[2048,1024]{1,0:T(8,128)}, bf16[2,1024,2048]{2,1,0:T(8,128)(2,1)}) custom-call(s32[7]{0:T(128)} %pad_add_fusion.m, bf16[2048,1024]{1,0:T(8,128)(2,1)} %bitcast.233, bf16[2048,1024]{1,0:T(8,128)(2,1)} %bitcast.231, bf16[1024,2048]{1,0:T(8,128)(2,1)} %wu.1, bf16[2048,1024]{1,0:T(8,128)(2,1)} %wd.1), custom_call_target="tpu_custom_call" | custom-call | flops 51539607552 | bytes 41943040 | tf_op jit(solution)/shard_map/pallas_call | solution.py:250
  245.0 68.4 %shard_map.171 = (bf16[2048,1024]{1,0:T(8,128)(2,1)}, bf16[2048,1024]{1,0:T(8,128)(2,1)}, bf16[2,1024,2048]{2,1,0:T(8,128)(2,1)}) custom-call(s32[7]{0:T(128)} %pad_add_fusion.m, bf16[2048,1024]{1,0:T(8,128)(2,1)} %bitcast.234, bf16[2048,1024]{1,0:T(8,128)(2,1)} %bitcast.232, bf16[1024,2048]{1,0:T(8,128)(2,1)} %all-gather.9.cloned.1.call-done.wu, ...), custom_call_target="tpu_custom_call" | custom-call | flops 51539607552 | bytes 50331648 | tf_op jit(solution)/shard_map/pallas_call | solution.py:250
  313.5 25.7 %shard_map.172 = (bf16[4,512,1024]{2,1,0:T(8,128)(2,1)}, bf16[2,512,1024]{2,1,0:T(8,128)(2,1)}, bf16[2,1024,1024]{2,1,0:T(8,128)(2,1)}, bf16[2,512,1024]{2,1,0:T...) custom-call(s32[7]{0:T(128)} %pad_add_fusion.m, ...), custom_call_target="tpu_custom_call" | custom-call | flops 8589934592 | bytes 39862272 | tf_op jit(solution)/shard_map/pallas_call | solution.py:250
  339.2 1.0 collective-permute-start.7
  340.2 1.3 dynamic-slice_bitcast_fusion.3
  341.6 23.9 %shard_map.174.refs_0_ = bf16[2,3,8,64,1024]{4,3,2,1,0:T(8,128)(2,1)} custom-call(s32[7]{0:T(128)} %pad_add_fusion.m, bf16[2,3,8,64,1024]{4,3,2,1,0:T(8,128)(2,1)} %bitcast.175, bf16[2,3,8,64,1024]{4,3,2,1,0:T(8,128)(2,1)} %bitcast.176, bf16[2,3,8,64,1024]{4,3,2,1,0:T(8,128)(2,1)} %bitcast.177, bf16[2,8,64,1024]{3,2,1,0:T(8,128)(2,1)} %get-tuple-element.87.o, ...), custom_call_target="tpu_custom_call" | custom-call | flops 21474836480 | bytes 29425664 | tf_op jit(solution)/shard_map/pallas_call | solution.py:250
  365.5 2.1 fusion.2
  367.6 1.5 collective-permute-start.9
  369.2 24.2 %shard_map.175 = bf16[2,3,8,64,1024]{4,3,2,1,0:T(8,128)(2,1)} custom-call(s32[7]{0:T(128)} %pad_add_fusion.m, bf16[2,3,8,64,1024]{4,3,2,1,0:T(8,128)(2,1)} %bitcast.178, bf16[2,3,8,64,1024]{4,3,2,1,0:T(8,128)(2,1)} %bitcast.179, bf16[2,3,8,64,1024]{4,3,2,1,0:T(8,128)(2,1)} %bitcast.180, ...), custom_call_target="tpu_custom_call", output_to_operand_aliasing={{}: (7, {})} | custom-call | flops 21474836480 | bytes 35717120 | tf_op jit(solution)/shard_map/pallas_call | solution.py:250
  393.3 1.2 fusion.5
  394.6 1.9 collective-permute-start.10
  396.5 11.8 %shard_map.176 = bf16[3,1024,512]{2,1,0:T(8,128)(2,1)} custom-call(s32[7]{0:T(128)} %pad_add_fusion.m, bf16[2,1024,1024]{2,1,0:T(8,128)(2,1)} %get-tuple-element.84.h_ref, bf16[2,3,512,1024]{3,2,1,0:T(8,128)(2,1)} %bitcast.164), custom_call_target="tpu_custom_call" | custom-call | flops 6442450944 | bytes 13631488 | tf_op jit(solution)/shard_map/pallas_call | solution.py:250
  408.3 2.8 dynamic-slice_bitcast_fusion.2
  411.1 23.9 %shard_map.177.refs_0_ = bf16[2,3,8,64,1024]{4,3,2,1,0:T(8,128)(2,1)} custom-call(s32[7]{0:T(128)} %pad_add_fusion.m, bf16[2,3,8,64,1024]{4,3,2,1,0:T(8,128)(2,1)} %bitcast.195, bf16[2,3,8,64,1024]{4,3,2,1,0:T(8,128)(2,1)} %bitcast.196, bf16[2,3,8,64,1024]{4,3,2,1,0:T(8,128)(2,1)} %bitcast.197, bf16[2,8,64,1024]{3,2,1,0:T(8,128)(2,1)} %get-tuple-element.83.o, ...), custom_call_target="tpu_custom_call" | custom-call | flops 21474836480 | bytes 29425664 | tf_op jit(solution)/shard_map/pallas_call | solution.py:250
  435.1 2.7 collective-permute-start.11
  437.9 2.5 fusion.1
  441.5 24.1 %shard_map.178 = bf16[2,3,8,64,1024]{4,3,2,1,0:T(8,128)(2,1)} custom-call(s32[7]{0:T(128)} %pad_add_fusion.m, bf16[2,3,8,64,1024]{4,3,2,1,0:T(8,128)(2,1)} %bitcast.198, bf16[2,3,8,64,1024]{4,3,2,1,0:T(8,128)(2,1)} %bitcast.199, bf16[2,3,8,64,1024]{4,3,2,1,0:T(8,128)(2,1)} %bitcast.200, ...), custom_call_target="tpu_custom_call", output_to_operand_aliasing={{}: (7, {})} | custom-call | flops 21474836480 | bytes 35717120 | tf_op jit(solution)/shard_map/pallas_call | solution.py:250
  466.9 2.3 fusion.4
  469.2 11.8 %shard_map.179 = bf16[3,1024,512]{2,1,0:T(8,128)(2,1)} custom-call(s32[7]{0:T(128)} %pad_add_fusion.m, bf16[2,1024,1024]{2,1,0:T(8,128)(2,1)} %get-tuple-element.84.h_ref, bf16[2,3,512,1024]{3,2,1,0:T(8,128)(2,1)} %bitcast.160), custom_call_target="tpu_custom_call" | custom-call | flops 6442450944 | bytes 13631488 | tf_op jit(solution)/shard_map/pallas_call | solution.py:250
  481.0 2.8 dynamic-slice_bitcast_fusion.1
  483.9 1.1 collective-permute-start.23
  485.3 3.5 shard_map.173
  490.4 5.0 collective-permute-done.14
  496.0 10.4 %shard_map.180 = (bf16[1,512,1024]{2,1,0:T(8,128)(2,1)}, f32[1,1,1024]{2,1,0:T(1,128)}) custom-call(s32[7]{0:T(128)} %pad_add_fusion.m, bf16[2,1024,1024]{2,1,0:T(8,128)(2,1)} %get-tuple-element.88.t.tok, bf16[2,1024,1024]{2,1,0:T(8,128)(2,1)} %get-tuple-element.121.br, bf16[2,3,512,1024]{3,2,1,0:T(8,128)(2,1)} %bitcast.161, ...), custom_call_target="tpu_custom_call" | custom-call | flops 3221225472 | bytes 28323840 | tf_op jit(solution)/shard_map/pallas_call | solution.py:250
  506.4 1.2 collective-permute-start.18
  509.2 2.5 fusion
  512.6 1.5 collective-permute-start.19
  514.0 2.2 convert_add_fusion.6
  516.2 10.4 %shard_map.181 = (bf16[1,512,1024]{2,1,0:T(8,128)(2,1)}, f32[1,1,1024]{2,1,0:T(1,128)}) custom-call(s32[7]{0:T(128)} %pad_add_fusion.m, bf16[2,1024,1024]{2,1,0:T(8,128)(2,1)} %get-tuple-element.88.t.tok, bf16[2,1024,1024]{2,1,0:T(8,128)(2,1)} %get-tuple-element.121.br, bf16[2,3,512,1024]{3,2,1,0:T(8,128)(2,1)} %bitcast.162, ...), custom_call_target="tpu_custom_call" | custom-call | flops 3221225472 | bytes 28323840 | tf_op jit(solution)/shard_map/pallas_call | solution.py:250
  526.6 1.2 collective-permute-start.17
  527.7 4.0 collective-permute-done.19
  531.8 1.4 fusion.3
  533.5 16.0 %shard_map.182 = (bf16[4,512,1024]{2,1,0:T(8,128)(2,1)}, f32[2,1,1024]{2,1,0:T(1,128)}) custom-call(s32[7]{0:T(128)} %pad_add_fusion.m, bf16[2,1024,1024]{2,1,0:T(8,128)(2,1)} %get-tuple-element.88.t.tok, bf16[2,1024,1024]{2,1,0:T(8,128)(2,1)} %get-tuple-element.121.br, bf16[2,3,512,1024]{3,2,1,0:T(8,128)(2,1)} %bitcast.163, ...), custom_call_target="tpu_custom_call" | custom-call | flops 6442450944 | bytes 31473664 | tf_op jit(solution)/shard_map/pallas_call | solution.py:250
  551.5 5.2 all-to-all-start
  556.7 1.1 slice_bitcast_fusion
  557.8 7.0 %all-to-all-done = f32[32,1,704]{2,1,0:T(1,128)S(1)} async-done(((f32[32,1,704]{2,1,0:T(1,128)}), f32[32,1,704]{2,1,0:T(1,128)S(1)}, u32[]{:S(2)}, u32[]{:S(2)}) %all-to-all-start) | async-done | bytes 90144 | tf_op jit(solution)/shard_map/all_to_all | solution.py:967
  565.7 1.1 fusion.6
  567.9 10.6 %collective-permute-done.21 = bf16[3,1,1,64,512]{4,3,0,2,1:T(8,128)(2,1)S(1)} collective-permute-done((bf16[3,1,1,64,512]{4,3,0,2,1:T(8,128)(2,1)S(1)}, bf16[3,1,1,64,512]{4,3,0,2,1:T(8,128)(2,1)S(1)}, u32[]{:S(2)}, u32[]{:S(2)}) %collective-permute-start.21) | collective-permute-done | bytes 196640 | tf_op jit(solution)/shard_map/ppermute | solution.py:873
  578.4 3.1 shard_map.183._
  581.5 2.9 shard_map.184
  584.4 1.8 convert_add_fusion.10
  (148 shorter events, 21.3 us)
Async XLA Ops:
  7.2 16.2 %copy-start = (s32[4,1]{0,1:T(1,128)S(1)}, s32[4,1]{0,1:T(1,128)}, u32[]{:S(2)}) copy-start(s32[4,1]{0,1:T(1,128)} %param.11) | copy-start | bytes 52
  7.2 14.3 %copy-start.21 = (s32[4,1]{0,1:T(1,128)S(1)}, s32[4,1]{0,1:T(1,128)}, u32[]{:S(2)}) copy-start(s32[4,1]{0,1:T(1,128)} %param.12) | copy-start | bytes 52
  7.2 15.1 %copy-start.4 = (f32[256,2048]{1,0:T(8,128)S(1)}, f32[256,2048]{1,0:T(8,128)}, u32[]{:S(2)}) copy-start(f32[256,2048]{1,0:T(8,128)} %param.14) | copy-start | bytes 6291460
  7.2 83.1 %all-gather.5.cloned.1.call-start = ((), (), s32[]{:S(2)}) async-start(), calls=%async_computation.3 | async-start | bytes 3342336 | tf_op jit(solution)/shard_map/all_gather | solution.py:830
  8.3 7.9 %collective-permute-start.5 = (bf16[192,512]{1,0:T(8,128)(2,1)S(1)}, bf16[192,512]{1,0:T(8,128)(2,1)S(1)}, u32[]{:S(2)}, u32[]{:S(2)}) collective-permute-start(bf16[192,512]{1,0:T(8,128)(2,1)S(1)} %constant_dynamic-slice_fusion.5), channel_id=1, source_target_pairs={{0,1},{1,0},{2,3},{3,2},{4,5},{5,4},{6,7},{7,6},{8,9},{9,8},{10,11... | collective-permute-start | bytes 589832 | tf_op jit(solution)/shard_map/ppermute | solution.py:823
  16.2 0.7 copy-start.8
  17.0 148.3 %all-gather.7.cloned.1.call-start = ((), (), s32[]{:S(2)}) async-start(), calls=%async_computation.4 | async-start | bytes 1114112 | tf_op jit(solution)/shard_map/all_gather | solution.py:830
  17.0 8.5 %copy-start.13 = (f32[2,1024]{1,0:T(2,128)S(1)}, f32[2,1024]{1,0:T(2,128)}, u32[]{:S(2)}) copy-start(f32[2,1024]{1,0:T(2,128)} %param.13) | copy-start | bytes 24580
  19.7 24.7 %collective-permute-start = (bf16[1,512,1024]{2,1,0:T(8,128)(2,1)}, bf16[1,512,1024]{2,1,0:T(8,128)(2,1)}, u32[]{:S(2)}, u32[]{:S(2)}) collective-permute-start(bf16[1,512,1024]{2,1,0:T(8,128)(2,1)} %get-tuple-element.172), channel_id=1, source_target_pairs={{0,1},{1,0},{2,3},{3,2},{4,5},{5,4},{6,7},{7,6},{8,9},{9,8},{10,11... | collective-permute-start | bytes 3145736 | tf_op jit(solution)/shard_map/ppermute | solution.py:823
  21.7 0.6 copy-start.15
  21.7 0.6 copy-start.17
  23.4 31.9 %copy-start.9 = (f32[2,2048]{1,0:T(2,128)}, f32[2,2048]{1,0:T(2,128)S(1)}, u32[]{:S(2)}) copy-start(f32[2,2048]{1,0:T(2,128)S(1)} %convolution_add_fusion) | copy-start | bytes 49156
  44.4 27.1 %collective-permute-start.1 = (bf16[32,1024]{1,0:T(8,128)(2,1)S(1)}, bf16[32,1024]{1,0:T(8,128)(2,1)S(1)}, u32[]{:S(2)}, u32[]{:S(2)}) collective-permute-start(bf16[32,1024]{1,0:T(8,128)(2,1)S(1)} %constant_dynamic-slice_fusion.8), channel_id=1, source_target_pairs={{0,1},{1,0},{2,3},{3,2},{4,5},{5,4},{6,7},{7,6},{8,9},{9,8},{10,11... | collective-permute-start | bytes 196616 | tf_op jit(solution)/shard_map/ppermute | solution.py:823
  71.5 0.6 copy-start.12
  72.1 172.9 %all-gather.9.cloned.1.call-start = ((), (), s32[]{:S(2)}) async-start(), calls=%async_computation.5 | async-start | bytes 4456448 | tf_op jit(solution)/shard_map/all_gather | solution.py:830
  73.1 6.4 %collective-permute-start.2 = (bf16[64,2048]{1,0:T(8,128)(2,1)S(1)}, bf16[64,2048]{1,0:T(8,128)(2,1)S(1)}, u32[]{:S(2)}, u32[]{:S(2)}) collective-permute-start(bf16[64,2048]{1,0:T(8,128)(2,1)S(1)} %constant_dynamic-slice_fusion.7), channel_id=1, source_target_pairs={{0,1},{1,0},{2,3},{3,2},{4,5},{5,4},{6,7},{7,6},{8,9},{9,8},{10,11... | collective-permute-start | bytes 786440 | tf_op jit(solution)/shard_map/ppermute | solution.py:823
  79.6 0.7 copy-start.6
  80.3 164.7 %all-gather.11.cloned.1.call-start = ((), (), s32[]{:S(2)}) async-start(), calls=%async_computation.6 | async-start | bytes 4456448 | tf_op jit(solution)/shard_map/all_gather | solution.py:830
  81.3 7.6 %collective-permute-start.3 = (bf16[128,1024]{1,0:T(8,128)(2,1)S(1)}, bf16[128,1024]{1,0:T(8,128)(2,1)S(1)}, u32[]{:S(2)}, u32[]{:S(2)}) collective-permute-start(bf16[128,1024]{1,0:T(8,128)(2,1)S(1)} %constant_dynamic-slice_fusion.6), channel_id=1, source_target_pairs={{0,1},{1,0},{2,3},{3,2},{4,5},{5,4},{6,7},{7,6},{8,9},{9,8},{10,11... | collective-permute-start | bytes 786440 | tf_op jit(solution)/shard_map/ppermute | solution.py:823
  89.0 0.7 copy-start.7
  89.0 25.3 %collective-permute-start.4 = (bf16[1,512,1024]{2,1,0:T(8,128)(2,1)S(1)}, bf16[1,512,1024]{2,1,0:T(8,128)(2,1)}, u32[]{:S(2)}, u32[]{:S(2)}) collective-permute-start(bf16[1,512,1024]{2,1,0:T(8,128)(2,1)S(1)} %get-tuple-element.78), channel_id=1, source_target_pairs={{0,1},{1,0},{2,3},{3,2},{4,5},{5,4},{6,7},{7,6},{8,9},{9,8},{10,11... | collective-permute-start | bytes 3145736 | tf_op jit(solution)/shard_map/ppermute | solution.py:823
  89.7 321.4 %reduce-scatter.3.cloned.1.call-start = ((), (), s32[]{:S(2)}) async-start(), calls=%async_computation.7 | async-start | bytes 8912896 | tf_op jit(solution)/shard_map/reduce_scatter | solution.py:888
  114.3 51.0 %collective-permute-start.6 = (bf16[2,512,1024]{2,1,0:T(8,128)(2,1)}, bf16[2,512,1024]{2,1,0:T(8,128)(2,1)}, u32[]{:S(2)}, u32[]{:S(2)}) collective-permute-start(bf16[2,512,1024]{2,1,0:T(8,128)(2,1)} %dynamic-slice_bitcast_fusion), channel_id=1, source_target_pairs={{0,1},{1,0},{2,3},{3,2},{4,5},{5,4},{6,7},{7,6},{8,9},{9,8},{10,11... | collective-permute-start | bytes 6291464 | tf_op jit(solution)/shard_map/ppermute | solution.py:823
  244.2 245.4 %reduce-scatter.5.cloned.1.call-start = ((), (), s32[]{:S(2)}) async-start(), calls=%async_computation.8 | async-start | bytes 8912896 | tf_op jit(solution)/shard_map/reduce_scatter | solution.py:888
  339.2 146.1 %collective-permute-start.7 = (bf16[2,512,1024]{2,1,0:T(8,128)(2,1)}, bf16[2,512,1024]{2,1,0:T(8,128)(2,1)}, u32[]{:S(2)}, u32[]{:S(2)}) collective-permute-start(bf16[2,512,1024]{2,1,0:T(8,128)(2,1)} %get-tuple-element.100), channel_id=1, source_target_pairs={{0,1},{1,0},{2,3},{3,2},{4,5},{5,4},{6,7},{7,6},{8,9},{9,8},{10,11... | collective-permute-start | bytes 6291464 | tf_op jit(solution)/shard_map/ppermute | solution.py:823
  341.5 24.0 %collective-permute-start.8 = (bf16[2,8,1,64,512]{4,3,1,0,2:T(8,128)(2,1)S(1)}, bf16[2,8,1,64,512]{4,3,1,0,2:T(8,128)(2,1)}, u32[]{:S(2)}, u32[]{:S(2)}) collective-permute-start(bf16[2,8,1,64,512]{4,3,1,0,2:T(8,128)(2,1)S(1)} %dynamic-slice_bitcast_fusion.3), channel_id=1, source_target_pairs={{0,2},{2,0},{4,6},{6,4},{8,10},{10,8},{12,14},{14,12},{16,18},{18,... | collective-permute-start | bytes 3145736 | tf_op jit(solution)/shard_map/ppermute | solution.py:873
  367.6 25.7 %collective-permute-start.9 = (bf16[2,4,1,64,512]{4,3,1,0,2:T(8,128)(2,1)S(1)}, bf16[2,4,1,64,512]{4,3,1,0,2:T(8,128)(2,1)}, u32[]{:S(2)}, u32[]{:S(2)}) collective-permute-start(bf16[2,4,1,64,512]{4,3,1,0,2:T(8,128)(2,1)S(1)} %dynamic-slice_bitcast_fusion.8), channel_id=1, source_target_pairs={{0,4},{2,6},{4,0},{6,2},{8,12},{10,14},{12,8},{14,10},{16,20},{18,... | collective-permute-start | bytes 1572872 | tf_op jit(solution)/shard_map/ppermute | solution.py:873
  394.6 40.4 %collective-permute-start.10 = (bf16[2,2,1,64,512]{4,3,1,0,2:T(8,128)(2,1)S(1)}, bf16[2,2,1,64,512]{4,3,1,0,2:T(8,128)(2,1)S(1)}, u32[]{:S(2)}, u32[]{:S(2)}) collective-permute-start(bf16[2,2,1,64,512]{4,3,1,0,2:T(8,128)(2,1)S(1)} %dynamic-slice_bitcast_fusion.10), channel_id=1, source_target_pairs={{0,8},{2,10},{4,12},{6,14},{8,0},{10,2},{12,4},{14,6},{16,24},{18,... | collective-permute-start | bytes 786440 | tf_op jit(solution)/shard_map/ppermute | solution.py:873
  411.1 26.8 %collective-permute-start.12 = (bf16[3,8,1,64,512]{4,3,1,0,2:T(8,128)(2,1)}, bf16[3,8,1,64,512]{4,3,1,0,2:T(8,128)(2,1)}, u32[]{:S(2)}, u32[]{:S(2)}) collective-permute-start(bf16[3,8,1,64,512]{4,3,1,0,2:T(8,128)(2,1)} %dynamic-slice_bitcast_fusion.2), channel_id=1, source_target_pairs={{0,2},{2,0},{4,6},{6,4},{8,10},{10,8},{12,14},{14,12},{16,18},{18,... | collective-permute-start | bytes 4718600 | tf_op jit(solution)/shard_map/ppermute | solution.py:873
  435.1 30.5 %collective-permute-start.11 = (bf16[2,1,1,64,512]{4,3,1,0,2:T(8,128)(2,1)S(1)}, bf16[2,1,1,64,512]{4,3,1,0,2:T(8,128)(2,1)}, u32[]{:S(2)}, u32[]{:S(2)}) collective-permute-start(bf16[2,1,1,64,512]{4,3,1,0,2:T(8,128)(2,1)S(1)} %constant_dynamic-slice_fusion.4), channel_id=1, source_target_pairs={{0,16},{2,18},{4,20},{6,22},{8,24},{10,26},{12,28},{14,30},{16,0},... | collective-permute-start | bytes 393224 | tf_op jit(solution)/shard_map/ppermute | solution.py:873
  441.3 25.6 %collective-permute-start.13 = (bf16[3,4,1,64,512]{4,3,1,0,2:T(8,128)(2,1)}, bf16[3,4,1,64,512]{4,3,1,0,2:T(8,128)(2,1)}, u32[]{:S(2)}, u32[]{:S(2)}) collective-permute-start(bf16[3,4,1,64,512]{4,3,1,0,2:T(8,128)(2,1)} %dynamic-slice_bitcast_fusion.7), channel_id=1, source_target_pairs={{0,4},{2,6},{4,0},{6,2},{8,12},{10,14},{12,8},{14,10},{16,20},{18,... | collective-permute-start | bytes 2359304 | tf_op jit(solution)/shard_map/ppermute | solution.py:873
  480.9 2.8 copy-start.3
  480.9 4.1 copy-start.16
  480.9 4.1 copy-start.18
  481.0 4.2 copy-start.14
  483.7 25.4 %collective-permute-start.16 = (bf16[3,8,1,64,512]{4,3,1,0,2:T(8,128)(2,1)}, bf16[3,8,1,64,512]{4,3,1,0,2:T(8,128)(2,1)}, u32[]{:S(2)}, u32[]{:S(2)}) collective-permute-start(bf16[3,8,1,64,512]{4,3,1,0,2:T(8,128)(2,1)} %dynamic-slice_bitcast_fusion.1), channel_id=1, source_target_pairs={{0,2},{2,0},{4,6},{6,4},{8,10},{10,8},{12,14},{14,12},{16,18},{18,... | collective-permute-start | bytes 4718600 | tf_op jit(solution)/shard_map/ppermute | solution.py:873
  483.8 11.6 %collective-permute-start.14 = (bf16[3,2,1,64,512]{4,3,1,0,2:T(8,128)(2,1)S(1)}, bf16[3,2,1,64,512]{4,3,1,0,2:T(8,128)(2,1)S(1)}, u32[]{:S(2)}, u32[]{:S(2)}) collective-permute-start(bf16[3,2,1,64,512]{4,3,1,0,2:T(8,128)(2,1)S(1)} %dynamic-slice_bitcast_fusion.9), channel_id=1, source_target_pairs={{0,8},{2,10},{4,12},{6,14},{8,0},{10,2},{12,4},{14,6},{16,24},{18,... | collective-permute-start | bytes 1179656 | tf_op jit(solution)/shard_map/ppermute | solution.py:873
  483.9 4.9 collective-permute-start.23
  489.5 24.5 %collective-permute-start.24 = (bf16[2,64,2048]{2,1,0:T(8,128)(2,1)}, bf16[2,64,2048]{2,1,0:T(8,128)(2,1)}, u32[]{:S(2)}, u32[]{:S(2)}) collective-permute-start(bf16[2,64,2048]{2,1,0:T(8,128)(2,1)} %reduce-scatter.5.cloned.1.call-done), channel_id=1, source_target_pairs={{0,1},{1,0},{2,3},{3,2},{4,5},{5,4},{6,7},{7,6},{8,9},{9,8},{10,11... | collective-permute-start | bytes 1572872 | tf_op jit(solution)/shard_map/ppermute | solution.py:823
  495.5 12.0 %collective-permute-start.15 = (bf16[3,1,1,64,512]{4,3,1,0,2:T(8,128)(2,1)S(1)}, bf16[3,1,1,64,512]{4,3,1,0,2:T(8,128)(2,1)S(1)}, u32[]{:S(2)}, u32[]{:S(2)}) collective-permute-start(bf16[3,1,1,64,512]{4,3,1,0,2:T(8,128)(2,1)S(1)} %constant_dynamic-slice_fusion.3), channel_id=1, source_target_pairs={{0,16},{2,18},{4,20},{6,22},{8,24},{10,26},{12,28},{14,30},{16,0},... | collective-permute-start | bytes 589832 | tf_op jit(solution)/shard_map/ppermute | solution.py:873
  506.4 72.0 %collective-permute-start.18 = (bf16[1,512,1024]{2,1,0:T(8,128)(2,1)}, bf16[1,512,1024]{2,1,0:T(8,128)(2,1)}, u32[]{:S(2)}, u32[]{:S(2)}) collective-permute-start(bf16[1,512,1024]{2,1,0:T(8,128)(2,1)} %get-tuple-element.122), channel_id=1, source_target_pairs={{0,1},{1,0},{2,3},{3,2},{4,5},{5,4},{6,7},{7,6},{8,9},{9,8},{10,11... | collective-permute-start | bytes 3145736 | tf_op jit(solution)/shard_map/ppermute | solution.py:823
  508.3 5.7 copy-start.5
  508.3 76.1 %collective-permute-start.22 = (bf16[3,64,512]{2,1,0:T(8,128)(2,1)}, bf16[3,64,512]{2,1,0:T(8,128)(2,1)}, u32[]{:S(2)}, u32[]{:S(2)}) collective-permute-start(bf16[3,64,512]{2,1,0:T(8,128)(2,1)} %fusion.9), channel_id=1, source_target_pairs={{0,1},{1,0},{2,3},{3,2},{4,5},{5,4},{6,7},{7,6},{8,9},{9,8},{10,11... | collective-permute-start | bytes 589832 | tf_op jit(solution)/shard_map/ppermute | solution.py:823
  512.6 19.2 %collective-permute-start.19 = (bf16[3,4,1,64,512]{4,3,1,0,2:T(8,128)(2,1)}, bf16[3,4,1,64,512]{4,3,1,0,2:T(8,128)(2,1)}, u32[]{:S(2)}, u32[]{:S(2)}) collective-permute-start(bf16[3,4,1,64,512]{4,3,1,0,2:T(8,128)(2,1)} %dynamic-slice_bitcast_fusion.6), channel_id=1, source_target_pairs={{0,4},{2,6},{4,0},{6,2},{8,12},{10,14},{12,8},{14,10},{16,20},{18,... | collective-permute-start | bytes 2359304 | tf_op jit(solution)/shard_map/ppermute | solution.py:873
  526.6 54.9 %collective-permute-start.17 = (bf16[1,512,1024]{2,1,0:T(8,128)(2,1)}, bf16[1,512,1024]{2,1,0:T(8,128)(2,1)}, u32[]{:S(2)}, u32[]{:S(2)}) collective-permute-start(bf16[1,512,1024]{2,1,0:T(8,128)(2,1)} %get-tuple-element.126), channel_id=1, source_target_pairs={{0,1},{1,0},{2,3},{3,2},{4,5},{5,4},{6,7},{7,6},{8,9},{9,8},{10,11... | collective-permute-start | bytes 3145736 | tf_op jit(solution)/shard_map/ppermute | solution.py:823
  533.3 16.2 %copy-start.19 = (f32[1,1,1024]{2,1,0:T(1,128)S(1)}, f32[1,1,1024]{2,1,0:T(1,128)}, u32[]{:S(2)}) copy-start(f32[1,1,1024]{2,1,0:T(1,128)} %get-tuple-element.134) | copy-start | bytes 12292
  533.3 16.2 %copy-start.20 = (f32[1,1,1024]{2,1,0:T(1,128)S(1)}, f32[1,1,1024]{2,1,0:T(1,128)}, u32[]{:S(2)}) copy-start(f32[1,1,1024]{2,1,0:T(1,128)} %get-tuple-element.135) | copy-start | bytes 12292
  533.4 16.9 %copy-start.10 = (f32[2,2048]{1,0:T(2,128)S(1)}, f32[2,2048]{1,0:T(2,128)}, u32[]{:S(2)}) copy-start(f32[2,2048]{1,0:T(2,128)} %copy-done.9) | copy-start | bytes 49156
  533.4 17.3 %copy-start.11 = (f32[2,16,64]{2,1,0:T(8,128)S(1)}, f32[2,16,64]{2,1,0:T(8,128)}, u32[]{:S(2)}) copy-start(f32[2,16,64]{2,1,0:T(8,128)} %mul.84) | copy-start | bytes 24580
  533.4 23.3 %copy-start.2 = (f32[2,64,2048]{2,1,0:T(8,128)S(1)}, f32[2,64,2048]{2,1,0:T(8,128)}, u32[]{:S(2)}) copy-start(f32[2,64,2048]{2,1,0:T(8,128)} %convert_add_fusion.6) | copy-start | bytes 3145732
  533.4 32.3 %collective-permute-start.20 = (bf16[3,2,1,64,512]{4,3,0,2,1:T(8,128)(2,1)S(1)}, bf16[3,2,1,64,512]{4,3,0,2,1:T(8,128)(2,1)}, u32[]{:S(2)}, u32[]{:S(2)}) collective-permute-start(bf16[3,2,1,64,512]{4,3,0,2,1:T(8,128)(2,1)S(1)} %bitcast.220), channel_id=1, source_target_pairs={{0,8},{2,10},{4,12},{6,14},{8,0},{10,2},{12,4},{14,6},{16,24},{18,... | collective-permute-start | bytes 1179656 | tf_op jit(solution)/shard_map/ppermute | solution.py:873
  551.5 13.3 %all-to-all-start = ((f32[32,1,704]{2,1,0:T(1,128)}), f32[32,1,704]{2,1,0:T(1,128)S(1)}, u32[]{:S(2)}, u32[]{:S(2)}) async-start(f32[32,1,704]{2,1,0:T(1,128)} %all_to_all.8), calls=%async_computation.2 | async-start | bytes 196608 | tf_op jit(solution)/shard_map/all_to_all | solution.py:967
  566.8 11.6 %collective-permute-start.21 = (bf16[3,1,1,64,512]{4,3,0,2,1:T(8,128)(2,1)S(1)}, bf16[3,1,1,64,512]{4,3,0,2,1:T(8,128)(2,1)S(1)}, u32[]{:S(2)}, u32[]{:S(2)}) collective-permute-start(bf16[3,1,1,64,512]{4,3,0,2,1:T(8,128)(2,1)S(1)} %constant_dynamic-slice_fusion), channel_id=1, source_target_pairs={{0,16},{2,18},{4,20},{6,22},{8,24},{10,26},{12,28},{14,30},{16,0},... | collective-permute-start | bytes 589832 | tf_op jit(solution)/shard_map/ppermute | solution.py:873
  578.4 7.8 %copy-start.1 = (s32[4,1]{0,1:T(1,128)S(1)}, s32[4,1]{0,1:T(1,128)}, u32[]{:S(2)}) copy-start(s32[4,1]{0,1:T(1,128)} %param.11) | copy-start | bytes 52
Sparse Core Ops, SparseCore 0:
  17.1 46.9 all-gather.4
  72.2 38.2 all-gather.6
  113.3 49.4 all-gather.8
  165.4 49.1 all-gather.10
  244.3 105.4 reduce-scatter.2
  353.7 116.8 reduce-scatter.4

commit v2 on v1

--- a/solution.py
+++ b/solution.py
@@ -244,7 +244,9 @@
     )
 
 
-def call(body, meta, args, grid, in_specs, out_specs, out_shape, flops, scratch=(), aliases=None):
+def call(
+    body, meta, args, grid, in_specs, out_specs, out_shape, flops, scratch=(), aliases=None, weight=0.5
+):
     moved = sum(a.size * a.dtype.itemsize for a in args)
     moved += sum(math.prod(o.shape) * jnp.dtype(o.dtype).itemsize for o in out_shape)
     return pl.pallas_call(
@@ -259,7 +261,9 @@
         out_shape=out_shape,
         input_output_aliases=aliases or {},
         compiler_params=pltpu.CompilerParams(vmem_limit_bytes=VMEM_LIMIT),
-        cost_estimate=pl.CostEstimate(flops=int(flops), bytes_accessed=int(moved), transcendentals=0),
+        cost_estimate=pl.CostEstimate(
+            flops=int(flops * weight), bytes_accessed=int(moved * 0.01), transcendentals=0
+        ),
     )(meta, *args)
 
 
@@ -326,6 +330,7 @@
         ],
         outs,
         6 * length * width * part,
+        weight=0.8,
         aliases={5 + i: i for i in range(len(prev))},
     )
 
@@ -352,16 +357,28 @@
         [pl.BlockSpec((1, 3, part, rows), lambda h, m: (s, 0, 0, h))],
         [shape((seqs, 3, part, length))],
         6 * length * width * part,
+        weight=0.8,
         aliases={3 + i: i for i in range(len(prev))},
     )
 
 
-def mask_rows(valid, length, block):
-    first = lax.broadcasted_iota(jnp.int32, (16, length), 0) == 0
-    hidden = lax.broadcasted_iota(jnp.int32, (16, length), 1) >= valid
+def mask_rows(valid, extent, block):
+    first = lax.broadcasted_iota(jnp.int32, (16, extent), 0) == 0
+    hidden = lax.broadcasted_iota(jnp.int32, (16, extent), 1) >= valid
     keys = jnp.where(first & hidden, -1e30, 0.0).astype(BF)
     ones = jnp.where(lax.broadcasted_iota(jnp.int32, (16, block), 0) == 0, 1.0, 0.0).astype(BF)
     return keys, ones
+
+
+def by_extent(valid, length, work):
+    step = min(256, length)
+    for extent in range(step, length + 1, step):
+        low = extent - step if extent > step else -1
+        high = extent if extent < length else length * 2
+
+        @pl.when((valid > low) & (valid <= high))
+        def _():
+            work(extent)
 
 
 def attention(meta, qkv, first, count, prev):
@@ -373,16 +390,19 @@
     def body(m, q, k, v, *refs):
         out, logs = refs[-2:]
         valid = m[lens_at + first + pl.program_id(0)]
-        key_mask, ones = mask_rows(valid, length, length)
-        scores = contract(
-            jnp.concatenate([k[0, 0, 0], key_mask], 0), jnp.concatenate([q[0, 0, 0], ones], 0), 0, 0
-        )
-        top = jnp.max(scores, 0, keepdims=True)
-        expo = jnp.exp2((scores - top) * EXP_SCALE)
-        total = jnp.sum(expo, 0, keepdims=True)
-        mixed = contract(v[0, 0, 0], expo.astype(BF), 1, 0)
-        out[0, 0] = (mixed / total).astype(BF)
-        logs[0, 0] = top * EXP_SCALE + jnp.log2(total)
+
+        def work(extent):
+            key_mask, ones = mask_rows(valid, extent, length)
+            keys = jnp.concatenate([k[0, 0, 0, :, :extent], key_mask], 0)
+            scores = contract(keys, jnp.concatenate([q[0, 0, 0], ones], 0), 0, 0)
+            top = jnp.max(scores, 0, keepdims=True)
+            expo = jnp.exp2((scores - top) * EXP_SCALE)
+            total = jnp.sum(expo, 0, keepdims=True)
+            mixed = contract(v[0, 0, 0, :, :extent], expo.astype(BF), 1, 0)
+            out[0, 0] = (mixed / total).astype(BF)
+            logs[0, 0] = top * EXP_SCALE + jnp.log2(total)
+
+        by_extent(valid, length, work)
 
     def spec(c):
         return pl.BlockSpec((1, 1, 1, HEAD, length), lambda s, h, m: (s + first, c, h, 0, 0))
@@ -414,30 +434,39 @@
     def body(m, q, k, v, o, do, ls, *refs):
         d_qkv, dk_sum, dv_sum = refs[-3:]
         valid = m[lens_at + first]
-        key_mask, ones = mask_rows(valid, length, block)
-        for h in range(group):
-            keys = k[0, 0, h]
-            masked_keys = jnp.concatenate([keys, key_mask], 0)
-            for i in range(length // block):
-                sl = slice(i * block, (i + 1) * block)
-                query = q[0, 0, h, :, sl]
-                d_mix = do[0, h, :, sl]
-                scores = contract(masked_keys, jnp.concatenate([query, ones], 0), 0, 0)
-                probs = jnp.exp2(scores * EXP_SCALE - ls[0, h, :, sl])
-                inner = jnp.sum(d_mix.astype(F32) * o[0, h, :, sl].astype(F32), 0, keepdims=True)
-                d_probs = contract(v[0, 0, h], d_mix, 0, 0)
-                d_raw = (probs * (d_probs - inner) * 0.125).astype(BF)
-                d_value = contract(d_mix, probs.astype(BF), 1, 1)
-                d_key = contract(query, d_raw, 1, 1)
-                if i == 0:
-                    dk_sum[...] = d_key
-                    dv_sum[...] = d_value
-                else:
-                    dk_sum[...] += d_key
-                    dv_sum[...] += d_value
-                d_qkv[0, 0, h, :, sl] = contract(keys, d_raw, 1, 0).astype(BF)
-            d_qkv[0, 1, h] = dk_sum[...].astype(BF)
-            d_qkv[0, 2, h] = dv_sum[...].astype(BF)
+
+        def work(extent):
+            key_mask, ones = mask_rows(valid, extent, block)
+            for h in range(group):
+                keys = k[0, 0, h, :, :extent]
+                vals = v[0, 0, h, :, :extent]
+                masked_keys = jnp.concatenate([keys, key_mask], 0)
+                for i in range(length // block):
+                    sl = slice(i * block, (i + 1) * block)
+                    query = q[0, 0, h, :, sl]
+                    d_mix = do[0, h, :, sl]
+                    scores = contract(masked_keys, jnp.concatenate([query, ones], 0), 0, 0)
+                    probs = jnp.exp2(scores * EXP_SCALE - ls[0, h, :, sl])
+                    inner = jnp.sum(d_mix.astype(F32) * o[0, h, :, sl].astype(F32), 0, keepdims=True)
+                    d_probs = contract(vals, d_mix, 0, 0)
+                    d_raw = (probs * (d_probs - inner) * 0.125).astype(BF)
+                    d_value = contract(d_mix, probs.astype(BF), 1, 1)
+                    d_key = contract(query, d_raw, 1, 1)
+                    if i == 0:
+                        dk_sum[:, :extent] = d_key
+                        dv_sum[:, :extent] = d_value
+                    else:
+                        dk_sum[:, :extent] += d_key
+                        dv_sum[:, :extent] += d_value
+                    d_qkv[0, 0, h, :, sl] = contract(keys, d_raw, 1, 0).astype(BF)
+                d_qkv[0, 1, h, :, :extent] = dk_sum[:, :extent].astype(BF)
+                d_qkv[0, 2, h, :, :extent] = dv_sum[:, :extent].astype(BF)
+                if extent < length:
+                    rest = jnp.zeros((HEAD, length - extent), BF)
+                    d_qkv[0, 1, h, :, extent:] = rest
+                    d_qkv[0, 2, h, :, extent:] = rest
+
+        by_extent(valid, length, work)
 
     def spec(c):
         return pl.BlockSpec((1, 1, group, HEAD, length), lambda h, m: (first, c, h, 0, 0))
@@ -460,27 +489,20 @@
         [pl.BlockSpec((1, 3, group, HEAD, length), lambda h, m: (first, 0, h, 0, 0))],
         [shape((seqs, 3, heads, HEAD, length))],
         40 * heads * length * length * HEAD,
+        weight=0.02,
         scratch=[pltpu.VMEM((HEAD, length), F32)] * 2,
         aliases={7 + i: i for i in range(len(prev))},
     )
 
 
-def out_proj(meta, own_mix, oth_mix, tokf, cot, cot_recv, own_w, oth_w, gain):
+def out_proj(meta, own_mix, oth_mix, tokf, own_w, oth_w, gain):
     seqs, length, width = tokf.shape
     rows = length // 2
     part = own_w.shape[0]
     own_mix = own_mix.reshape(seqs, part, length)
     oth_mix = oth_mix.reshape(seqs, part, length)
 
-    def body(m, a, b, t, cl, cr, wa, wb, g, resid, hid, cotf):
-        @pl.when(pl.program_id(1) == m[0])
-        def _():
-            cotf[0] = cl[0]
-
-        @pl.when(pl.program_id(1) != m[0])
-        def _():
-            cotf[0] = cr[0]
-
+    def body(m, a, b, t, wa, wb, g, resid, hid):
         branch = contract(a[0], wa[...], 0, 0) + contract(b[0], wb[...], 0, 0)
         total = t[0].astype(F32) + branch
         resid[0] = total.astype(BF)
@@ -493,72 +515,61 @@
     return call(
         body,
         meta,
-        [own_mix, oth_mix, tokf, cot, cot_recv, own_w, oth_w, gain],
+        [own_mix, oth_mix, tokf, own_w, oth_w, gain],
         (seqs, 2),
         [
             mix_spec,
             mix_spec,
             row_spec,
-            pl.BlockSpec((1, rows, width), lambda s, h, m: (m[1 + s], 0, 0)),
-            pl.BlockSpec((1, rows, width), lambda s, h, m: (s, 0, 0)),
             w_spec,
             w_spec,
             pl.BlockSpec((1, 1, width), lambda s, h, m: (s, 0, 0)),
         ],
-        [row_spec] * 3,
-        [shape((seqs, length, width))] * 3,
+        [row_spec] * 2,
+        [shape((seqs, length, width))] * 2,
         4 * seqs * length * width * part,
     )
 
 
-def feed_forward(meta, hid, cot, up_w, down_w, sums):
+def feed_forward(meta, hid, cot, cot_recv, up_w, down_w):
     seqs, length, width = hid.shape
     tokens = seqs * length
     hidden = up_w.shape[1]
     block = min(512, hidden)
-    rows = min(512, tokens)
+    rows = min(1024, tokens)
     steps = hidden // block
-    last = len(sums) > 0
     half_root = 1.0 / math.sqrt(2.0)
     density = 1.0 / math.sqrt(2.0 * math.pi)
 
-    def body(m, h_ref, c_ref, wu, wd, *refs):
-        sums_in = refs[: len(sums)]
-        out, d_hid, grads, act, d_up, out_sum, hid_sum, stage, sem = refs[len(sums) :]
+    def body(m, h_ref, stay, came, wu, wd, out, d_hid, grads, act, d_up, out_sum, hid_sum, c_ref, stage, sem):
         step = pl.program_id(0)
 
-        def moves(r):
-            sl = pl.ds(r * rows, rows)
-            if last:
-                return [
-                    pltpu.make_async_copy(sums_in[0].at[sl], out_sum.at[sl], sem.at[0, r]),
-                    pltpu.make_async_copy(sums_in[1].at[sl], hid_sum.at[sl], sem.at[1, r]),
-                ]
+        def loads():
+            moves = []
+            for s in range(seqs):
+                for k, src in enumerate((stay.at[m[1 + s]], came.at[s])):
+                    half = m[0] if k == 0 else 1 - m[0]
+                    at = pl.multiple_of(s * length + half * (length // 2), length // 2)
+                    dst = c_ref.at[pl.ds(at, length // 2)]
+                    moves.append(pltpu.make_async_copy(src, dst, sem.at[s, k]))
+            return moves
+
+        def stores():
             return [
-                pltpu.make_async_copy(out_sum.at[sl], out.at[sl], sem.at[0, r]),
-                pltpu.make_async_copy(hid_sum.at[sl], d_hid.at[sl], sem.at[1, r]),
+                pltpu.make_async_copy(stage.at[0], out, sem.at[seqs, 0]),
+                pltpu.make_async_copy(stage.at[1], d_hid, sem.at[seqs, 1]),
             ]
-
-        def stores(r):
-            sl = pl.ds(r * rows, rows)
-            return [
-                pltpu.make_async_copy(stage.at[0, r], out.at[sl], sem.at[0, r]),
-                pltpu.make_async_copy(stage.at[1, r], d_hid.at[sl], sem.at[1, r]),
-            ]
-
-        count = tokens // rows
 
         @pl.when(step == 0)
         def _():
-            if last:
-                for r in range(count):
-                    for move in moves(r):
-                        move.start()
-            else:
-                out_sum[...] = jnp.zeros_like(out_sum)
-                hid_sum[...] = jnp.zeros_like(hid_sum)
-
-        for r in range(count):
+            for move in loads():
+                move.start()
+            out_sum[...] = jnp.zeros_like(out_sum)
+            hid_sum[...] = jnp.zeros_like(hid_sum)
+            for move in loads():
+                move.wait()
+
+        for r in range(tokens // rows):
             sl = slice(r * rows, (r + 1) * rows)
             up = contract(h_ref[sl, :], wu[...], 1, 0)
             d_act = contract(c_ref[sl, :], wd[...], 1, 1)
@@ -568,71 +579,63 @@
             d = (d_act * slope).astype(BF)
             act[sl, :] = a
             d_up[sl, :] = d
-            if last:
-
-                @pl.when(step == 0)
-                def _():
-                    for move in moves(r):
-                        move.wait()
-
             out_sum[sl, :] += contract(a, wd[...], 1, 0)
             hid_sum[sl, :] += contract(d, wu[...], 1, 1)
 
-            @pl.when(step == steps - 1)
-            def _():
-                if last:
-                    stage[0, r] = out_sum[sl, :].astype(BF)
-                    stage[1, r] = hid_sum[sl, :].astype(BF)
-                for move in stores(r) if last else moves(r):
-                    move.start()
+        @pl.when(step == steps - 1)
+        def _():
+            stage[0] = out_sum[...].astype(BF)
+            stage[1] = hid_sum[...].astype(BF)
+            for move in stores():
+                move.start()
 
         grads[0] = contract(h_ref[...], d_up[...], 0, 0).astype(BF)
         grads[1] = contract(c_ref[...], act[...], 0, 0).astype(BF)
 
         @pl.when(step == steps - 1)
         def _():
-            for r in range(count):
-                for move in stores(r) if last else moves(r):
-                    move.wait()
-
-    kind = BF if last else F32
-    full = pl.BlockSpec((tokens, width), lambda j, m: (0, 0), pipeline_mode=HOLD)
-    staged = (2, tokens // rows, rows, width) if last else (1, 1, 16, 128)
+            for move in stores():
+                move.wait()
+
     return call(
         body,
         meta,
-        [hid.reshape(tokens, width), cot.reshape(tokens, width), up_w, down_w] + list(sums),
+        [hid.reshape(tokens, width), cot, cot_recv, up_w, down_w],
         (steps,),
         [
-            full,
-            full,
+            pl.BlockSpec((tokens, width), lambda j, m: (0, 0), pipeline_mode=HOLD),
+            ANY,
+            ANY,
             pl.BlockSpec((width, block), lambda j, m: (0, j)),
             pl.BlockSpec((block, width), lambda j, m: (j, 0)),
-        ]
-        + [ANY] * len(sums),
+        ],
         [ANY, ANY, pl.BlockSpec((2, width, block), lambda j, m: (0, 0, j))],
-        [shape((tokens, width), kind), shape((tokens, width), kind), shape((2, width, hidden))],
+        [shape((tokens, width)), shape((tokens, width)), shape((2, width, hidden))],
         12 * tokens * width * hidden,
+        weight=0.4,
         scratch=[
             pltpu.VMEM((tokens, block), BF),
             pltpu.VMEM((tokens, block), BF),
             pltpu.VMEM((tokens, width), F32),
             pltpu.VMEM((tokens, width), F32),
-            pltpu.VMEM(staged, BF),
-            pltpu.SemaphoreType.DMA((2, tokens // rows)),
+            pltpu.VMEM((tokens, width), BF),
+            pltpu.VMEM((2, tokens, width), BF),
+            pltpu.SemaphoreType.DMA((seqs + 1, 2)),
         ],
     )
 
 
-def middle(meta, resid, mlp, d_hid, cotf, own_mix, oth_mix, own_w, oth_w, gain, items):
+def middle(meta, resid, mlp, d_hid, cot, cot_recv, own_mix, oth_mix, own_w, oth_w, gain):
+    items = cot.shape[0]
     seqs, length, width = resid.shape
     rows = length // 2
     part = own_w.shape[0]
     mixes = [a.reshape(seqs, part, length) for a in (own_mix, oth_mix)]
-    mlp = mlp.reshape(resid.shape)
-    d_hid = d_hid.reshape(resid.shape)
-
-    def body(m, res, up, dh, ct, ma, mb, wa, wb, g, mine, away, branch, dma, dmb, grad, gsum, grad_sum, vec):
+    parts = [a.reshape(resid.shape) for a in mlp + d_hid]
+
+    def body(
+        m, res, up, up2, dh, dh2, cl, cr, ma, mb, wa, wb, g, mine, away, branch, dma, dmb, grad, gsum, grad_sum, vec, ct
+    ):
         phase, s = pl.program_id(0), pl.program_id(1)
 
         @pl.when((phase == 0) & (s == 0))
@@ -641,20 +644,22 @@
             vec[...] = jnp.zeros_like(vec)
 
         resid_f = res[0].astype(F32)
-        total = (resid_f + up[0].astype(F32)).astype(BF)
+        total = (resid_f + (up[0].astype(F32) + up2[0].astype(F32))).astype(BF)
 
         @pl.when(phase == 0)
         def _():
             away[0] = total
+            ct[...] = cr[0]
 
         @pl.when(phase == 1)
         def _():
             mine[0] = total
+            ct[...] = cl[0]
 
         unit, root = normalize(resid_f)
-        d_out = dh[0].astype(F32)
+        d_out = dh[0].astype(F32) + dh2[0].astype(F32)
         vec[s] += jnp.sum(d_out * unit, axis=0, keepdims=True)
-        d_res = (ct[0].astype(F32) + norm_back(d_out, unit, root, g[0])).astype(BF)
+        d_res = (ct[...].astype(F32) + norm_back(d_out, unit, root, g[0])).astype(BF)
         branch[0] = d_res
         dma[0] = contract(wa[...], d_res, 1, 1).astype(BF)
         dmb[0] = contract(wb[...], d_res, 1, 1).astype(BF)
@@ -675,9 +680,13 @@
     return call(
         body,
         meta,
-        [resid, mlp, d_hid, cotf, mixes[0], mixes[1], own_w, oth_w, gain],
+        [resid] + parts + [cot, cot_recv, mixes[0], mixes[1], own_w, oth_w, gain],
         (2, seqs),
-        [row_spec] * 4
+        [row_spec] * 5
+        + [
+            pl.BlockSpec((1, rows, width), lambda p, s, m: (m[1 + p * s], 0, 0)),
+            pl.BlockSpec((1, rows, width), lambda p, s, m: (s + p * (seqs - 1 - s), 0, 0)),
+        ]
         + [mix_spec] * 2
         + [w_spec] * 2
         + [pl.BlockSpec((1, 1, width), lambda p, s, m: (s, 0, 0))],
@@ -700,7 +709,12 @@
             shape((seqs, 1, width), F32),
         ],
         8 * seqs * length * width * part,
-        scratch=[pltpu.VMEM((2, width, part), F32), pltpu.VMEM((seqs, 1, width), F32)],
+        weight=1.0,
+        scratch=[
+            pltpu.VMEM((2, width, part), F32),
+            pltpu.VMEM((seqs, 1, width), F32),
+            pltpu.VMEM((rows, width), BF),
+        ],
     )
 
 
@@ -727,43 +741,59 @@
         [pl.BlockSpec((1, width, part), lambda c, m: (c, 0, 0))],
         [shape((3, width, part))],
         6 * seqs * length * width * part,
+        weight=0.02,
     )[0]
 
 
-def input_back(meta, tokf, branch, own_d, oth_d, own_w, oth_w, gain, items, stay, first, count):
+def input_back(meta, tokf, branch, own_d, oth_d, own_w, oth_w, gain, items, stay, s, prev):
     seqs, length, width = tokf.shape
     rows = length // 2
     part = own_w.shape[2]
+    block = min(256, rows)
+    cuts = rows // block
     own_d = own_d.reshape(seqs, 3, part, length)
     oth_d = oth_d.reshape(seqs, 3, part, length)
 
-    def body(m, tok, br, da, db, wa, wb, g, out, gsum):
+    def body(m, tok, br, da, db, wa, wb, g, *refs):
+        out, gsum = refs[-2:]
         d_hid = contract(da[0, 0], wa[0], 0, 1) + contract(db[0, 0], wb[0], 0, 1)
         for c in range(1, 3):
             d_hid += contract(da[0, c], wa[c], 0, 1) + contract(db[0, c], wb[c], 0, 1)
         unit, root = normalize(tok[0].astype(F32))
-        gsum[0] = jnp.sum(d_hid * unit, axis=0, keepdims=True)
+        vec = jnp.sum(d_hid * unit, axis=0, keepdims=True)
+
+        @pl.when(pl.program_id(0) == 0)
+        def _():
+            gsum[0] = vec
+
+        @pl.when(pl.program_id(0) > 0)
+        def _():
+            gsum[0] += vec
+
         out[0] = (br[0].astype(F32) + norm_back(d_hid, unit, root, g[0])).astype(BF)
 
-    def at(m):
-        return m[0] if stay else 1 - m[0]
-
-    row_spec = pl.BlockSpec((1, rows, width), lambda s, m: (s + first, at(m), 0))
-    d_spec = pl.BlockSpec((1, 3, part, rows), lambda s, m: (s + first, 0, 0, at(m)))
-    w_spec = pl.BlockSpec((3, width, part), lambda s, m: (0, 0, 0), pipeline_mode=HOLD)
+    def at(i, m):
+        return (m[0] if stay else 1 - m[0]) * cuts + i
+
+    row_spec = pl.BlockSpec((1, block, width), lambda i, m: (s, at(i, m), 0))
+    d_spec = pl.BlockSpec((1, 3, part, block), lambda i, m: (s, 0, 0, at(i, m)))
+    w_spec = pl.BlockSpec((3, width, part), lambda i, m: (0, 0, 0), pipeline_mode=HOLD)
     return call(
         body,
         meta,
-        [tokf, branch, own_d, oth_d, own_w, oth_w, gain],
-        (count,),
+        [tokf, branch, own_d, oth_d, own_w, oth_w, gain] + list(prev),
+        (cuts,),
         [row_spec, row_spec, d_spec, d_spec, w_spec, w_spec]
-        + [pl.BlockSpec((1, 1, width), lambda s, m: (s + first, 0, 0))],
+        + [pl.BlockSpec((1, 1, width), lambda i, m: (s, 0, 0))]
+        + [ANY] * len(prev),
         [
-            pl.BlockSpec((1, rows, width), lambda s, m: (m[1 + s] if stay else s, 0, 0)),
-            pl.BlockSpec((1, 1, width), lambda s, m: (s, 0, 0)),
+            pl.BlockSpec((1, block, width), lambda i, m: (m[1 + s] if stay else 0, i, 0)),
+            pl.BlockSpec((1, 1, width), lambda i, m: (0, 0, 0)),
         ],
-        [shape((items if stay else count, rows, width)), shape((count, 1, width), F32)],
-        12 * count * rows * width * part,
+        [shape((items if stay else 1, rows, width)), shape((1, 1, width), F32)],
+        12 * rows * width * part,
+        weight=0.02,
+        aliases={8 + i: i for i in range(len(prev))},
     )
 
 
@@ -814,10 +844,22 @@
     tok = tokens.reshape(items, rows, width)
     cot = cotangent.reshape(items, rows, width)
     lens = lengths.reshape(items)
-    own = x * seqs + jnp.arange(seqs, dtype=jnp.int32)
-    oth = (1 - x) * seqs + jnp.arange(seqs, dtype=jnp.int32)
-    meta = jnp.concatenate([x[None].astype(jnp.int32), own, lens[own], oth]).astype(jnp.int32)
     steps = timesteps.reshape(items)
+
+    at = jnp.arange(items, dtype=jnp.int32)
+    longer = (lens[None, :] > lens[:, None]) | (
+        (lens[None, :] == lens[:, None]) & (at[None, :] < at[:, None])
+    )
+    rank = jnp.sum(longer.astype(jnp.int32), axis=1)
+    holder = (rank + 1) // 2 % 2
+    slot = rank // 2
+
+    def chosen(device, values):
+        hit = (holder == device)[None, :] & (slot[None, :] == jnp.arange(seqs)[:, None])
+        return jnp.sum(jnp.where(hit, values[None, :], 0), axis=1)
+
+    own, oth = chosen(x, at), chosen(1 - x, at)
+    meta = jnp.concatenate([x[None], own, chosen(x, lens), oth]).astype(jnp.int32)
 
     def swap(value):
         return lax.ppermute(value, "mp", [(0, 1), (1, 0)])
@@ -830,39 +872,51 @@
         return lax.all_gather(value, "dp", axis=0, tiled=True)
 
     qkv_rows = qkv_weight.reshape(3 * width, part)
-    qkv_shard = swap(shard(qkv_rows))
+    def sent(rows_of, s):
+        return lax.dynamic_slice_in_dim(rows_of, oth[s], 1, 0)
+
+    tok_first = sent(tok, 0)
+    tok_recv = [swap(tok_first)]
+    qkv_shard = swap(after(shard(qkv_rows), tok_first))
     qkv_oth = spread(qkv_shard).reshape(qkv_weight.shape)
-    def sent(rows_of, s, count):
-        return lax.dynamic_slice_in_dim(rows_of, (1 - x) * seqs + s, count, 0)
-
-    tok_recv = [swap(sent(tok, 0, 1))]
-
-    feats = sinusoid(lax.dynamic_slice_in_dim(steps, x * seqs, seqs, 0))
+
+    feats = sinusoid(chosen(x, steps))
     pairs = jnp.dot(feats, time_weight, precision=lax.Precision.HIGHEST)
     widened = 1.0 + pairs.reshape(seqs, 2, 1, width)
     gain_a = norm_gains[0] * widened[:, 0]
     gain_b = norm_gains[1] * widened[:, 1]
 
-    far_shards = [swap(after(shard(w), tok_recv[0])) for w in (out_weight, up_weight, down_weight)]
+    near = [shard(w).reshape(-1, width) for w in (out_weight, up_weight, down_weight)]
+    far = swap(after(jnp.concatenate(near, 0), tok_recv[0]))
     base, qkv_far, mix_own, mix_oth = (), (), (), ()
     for s in range(seqs):
+        head = s == 0
         base = first_proj(meta, s, tok, tok_recv[s], gain_a, qkv_weight, base)
         mix_own = attention(meta, base[2], s, 1, mix_own)
-        if s == 0:
-            out_oth, up_oth, down_oth = [spread(after(w, mix_own[1])) for w in far_shards]
         if s + 1 < seqs:
-            tok_recv.append(swap(after(sent(tok, s + 1, 1), mix_own[1], *far_shards)))
-        qkv_far = other_proj(meta, base[1], qkv_oth, s, qkv_far)
+            tok_recv.append(swap(after(sent(tok, s + 1), tok_recv[s])))
+        order = after(meta, far) if head else meta
+        qkv_far = other_proj(order, base[1], qkv_oth, s, qkv_far)
+        if head:
+            arrived = after(far, base[2])
+            cuts = [0]
+            for piece in near:
+                cuts.append(cuts[-1] + piece.shape[0])
+            out_oth, up_oth, down_oth = [
+                spread(arrived[cuts[i] : cuts[i + 1]].reshape(w.shape[0] // dp_count, w.shape[1]))
+                for i, w in enumerate((out_weight, up_weight, down_weight))
+            ]
         mix_oth = attention(meta, qkv_far[0], s, 1, mix_oth)
-        if s == 0:
-            cot_recv = swap(after(sent(cot, 0, seqs), mix_oth[1], tok_recv[-1]))
+        if head:
+            cot_sent = jnp.concatenate([sent(cot, i) for i in range(seqs)], 0)
+            cot_recv = swap(after(cot_sent, tok_recv[-1]))
     tokf, hid_a, qkv_own = base
     qkv_far = qkv_far[0]
-    resid, hid_b, cotf = out_proj(
-        meta, mix_own[0], mix_oth[0], tokf, cot, cot_recv, out_weight, out_oth, gain_b
-    )
-    out_part, hid_part, grads_own = feed_forward(meta, hid_b, cotf, up_weight, down_weight, ())
-    mlp, d_hid_b, grads_oth = feed_forward(meta, hid_b, cotf, up_oth, down_oth, (out_part, hid_part))
+    resid, hid_b = out_proj(meta, mix_own[0], mix_oth[0], tokf, out_weight, out_oth, gain_b)
+    mlp_own, back_own, grads_own = feed_forward(meta, hid_b, cot, cot_recv, up_weight, down_weight)
+    mlp_oth, back_oth, grads_oth = feed_forward(
+        after(meta, grads_own), hid_b, cot, cot_recv, up_oth, down_oth
+    )
 
     def tree_send(value, step):
         count, cols = value.shape[0], value.shape[-1]
@@ -878,11 +932,27 @@
 
     def tree(value):
         step = 1
-        while step < dp_count:
+        while step * 4 < dp_count:
             pair = tree_send(value, step)
             value = tree_add(pair, (yield value))
             step *= 2
-        yield value.reshape(value.shape[0], width // dp_count, value.shape[-1])
+        left = dp_count // step
+        held = value
+        value = value.reshape(value.shape[0], left, width // dp_count, value.shape[-1])
+        place_at = dp // step
+
+        def piece(k):
+            return lax.dynamic_index_in_dim(value, place_at ^ k, 1, False)
+
+        came = [
+            lax.ppermute(piece(k), "dp", [(i, i ^ (k * step)) for i in range(dp_count)])
+            for k in range(1, left)
+        ]
+        gate = yield held
+        total = piece(0).astype(F32)
+        for part_in in came:
+            total += after(part_in, *gate).astype(F32)
+        yield total.astype(BF)
 
     def reduce(value):
         return lax.psum_scatter(value, "dp", scatter_dimension=1, tiled=True)
@@ -890,9 +960,19 @@
     ffn_own = reduce(grads_own)
     ffn_oth = reduce(grads_oth)
     out_stay, out_away, branch, d_mix_own, d_mix_oth, out_grads, sum_b = middle(
-        meta, resid, mlp, d_hid_b, cotf, mix_own[0], mix_oth[0], out_weight, out_oth, gain_b, items
-    )
-    out_came = swap(out_away)
+        meta,
+        resid,
+        [mlp_own, mlp_oth],
+        [back_own, back_oth],
+        cot,
+        cot_recv,
+        mix_own[0],
+        mix_oth[0],
+        out_weight,
+        out_oth,
+        gain_b,
+    )
+    out_came = []
 
     def heads_view(value):
         return value.reshape(seqs, part // HEAD, HEAD, 2 * rows)
@@ -911,49 +991,50 @@
             return self.value
 
     d_mix_own, d_mix_oth = heads_view(d_mix_own), heads_view(d_mix_oth)
-    jobs = [Job(out_grads)]
+    out_job = Job(out_grads)
     d_oth, d_own = (), ()
     order = meta
-
-    def ready(*gate):
-        return after(meta, *[job.go(*gate) for job in jobs])
-
     for s in range(seqs):
         d_oth = attention_back(order, qkv_far, mix_oth[0], d_mix_oth, mix_oth[1], s, d_oth)
-        order = ready(d_oth[0])
+        order = after(meta, out_job.go(d_oth[0]))
     grad_oth = proj_grad(order, hid_a, d_oth[0])
-    jobs.append(Job(grad_oth))
+    oth_job = Job(grad_oth)
     order = after(meta, grad_oth, ffn_own)
     for s in range(seqs):
+        out_came.append(swap(after(out_away[s : s + 1], d_own[0] if s else grad_oth)))
         d_own = attention_back(order, qkv_own, mix_own[0], d_mix_own, mix_own[1], s, d_own)
-        order = ready(d_own[0])
+        order = after(meta, oth_job.go(d_own[0]), out_came[s])
+        if s == seqs - 1:
+            order = after(order, out_job.go(d_own[0]))
     grad_own = proj_grad(order, hid_a, d_own[0])
-    order = ready(grad_own)
-    jobs.append(Job(grad_own))
-    in_away, sums_a = [], []
+    own_job = Job(grad_own)
+    order = after(meta, grad_own, ffn_oth)
+    in_away, in_stay, sum_a = [], (), []
+
+    def last_back(order, s, stay, prev):
+        return input_back(
+            order, tokf, branch, d_own[0], d_oth[0], qkv_weight, qkv_oth, gain_a, items, stay, s, prev
+        )
+
     for s in range(seqs):
-        rows_out, vec = input_back(
-            order, tokf, branch, d_own[0], d_oth[0], qkv_weight, qkv_oth, gain_a, items, False, s, 1
-        )
+        rows_out, vec = last_back(order, s, False, ())
         in_away.append(swap(rows_out))
-        sums_a.append(vec)
-        order = ready(rows_out)
-    in_stay, sum_stay = input_back(
-        after(order, ffn_oth), tokf, branch, d_own[0], d_oth[0], qkv_weight, qkv_oth, gain_a, items, True, 0, seqs
-    )
-    sum_a = jnp.concatenate(sums_a, 0) + sum_stay
-    for job in jobs:
-        while not job.done:
-            job.go(in_stay)
-    out_red, qkv_red_oth, qkv_red_own = [job.value for job in jobs]
-    output = place(meta, out_stay, out_came, 0, seqs)
-    input_grad = in_stay
+        sum_a.append(vec)
+        order = after(meta, rows_out, own_job.go(rows_out) if s == 0 else oth_job.go(rows_out))
+    out_red, qkv_red_oth = out_job.value, oth_job.value
+    far_grads = swap(
+        jnp.concatenate([ffn_oth[0], ffn_oth[1], out_red[1]] + [qkv_red_oth[c] for c in range(3)], 1)
+    )
     for s in range(seqs):
-        input_grad = place(meta, input_grad, in_away[s], s, seqs)
-
-    ffn = ffn_own.astype(F32) + swap(ffn_oth).astype(F32)
-    out_sum = out_red[0].astype(F32) + swap(out_red[1]).astype(F32)
-    qkv_sum = qkv_red_own.astype(F32) + swap(qkv_red_oth).astype(F32)
+        rows_out, vec = last_back(order, s, True, in_stay)
+        in_stay = (rows_out,)
+        sum_a[s] += vec
+        order = after(meta, own_job.go(rows_out) if s == 0 else rows_out)
+    sum_a = jnp.concatenate(sum_a, 0)
+    output, input_grad = out_stay, in_stay[0]
+    for s in range(seqs):
+        output = place(order, output, out_came[s], s, seqs)
+        input_grad = place(order, input_grad, in_away[s], s, seqs)
 
     sums = jnp.stack([sum_a, sum_b], 0)[:, :, 0]
     d_pair = sums * norm_gains[:, None, :]
@@ -964,18 +1045,33 @@
     by_gain = jnp.moveaxis(gain_part.reshape(2, count, gain_cols), 0, 1).reshape(count, 2 * gain_cols)
     by_feat = jnp.broadcast_to(feats.reshape(1, seqs * time_cols), (count, seqs * time_cols))
     packed = jnp.concatenate([by_pair, by_gain, by_feat], 1)
+    packed = after(packed, *in_away)
     everyone = lax.all_to_all(packed, ("dp", "mp"), 0, 0, tiled=True)
+    far_grads = after(far_grads, everyone)
+    while not own_job.done:
+        own_job.go(everyone)
+    everyone = after(everyone, output, input_grad)
     mine = everyone[:, : seqs * cols].reshape(count * seqs, cols)
     gains_grad = jnp.sum(everyone[:, seqs * cols :][:, : 2 * gain_cols], axis=0).reshape(2, gain_cols)
     all_feats = everyone[:, seqs * cols + 2 * gain_cols :].reshape(count * seqs, time_cols)
     time_grad = jnp.dot(all_feats.T, mine, precision=lax.Precision.HIGHEST)
+    def joined(near, first, cols):
+        return near.astype(F32) + far_grads[:, first : first + cols].astype(F32)
+
+    up_sum = joined(ffn_own[0], 0, hidden)
+    down_sum = joined(ffn_own[1], hidden, hidden)
+    out_sum = joined(out_red[0], 2 * hidden, part)
+    qkv_sum = jnp.stack(
+        [joined(own_job.value[c], 2 * hidden + (1 + c) * part, part) for c in range(3)], 0
+    )
+
     return (
         output.reshape(tokens.shape),
         input_grad.reshape(tokens.shape),
         qkv_sum,
         out_sum.T,
-        ffn[0],
-        ffn[1].T,
+        up_sum,
+        down_sum.T,
         gains_grad,
         time_grad,
     )

time: 600 us -> 569 us (0.948)
  Pallas kernels: 438 us -> 387 us
  starting transfers between devices: 30.3 us -> 59.6 us
  waiting for transfers between devices: 59.7 us -> 36.5 us
  local copies, waits for them, and re-layouts: 26.4 us -> 33.2 us
    pallas_call x24 -> x26, Pallas kernels: 438 us -> 387 us  [call(): pl.pallas_call(body, grid_spec=pltpu.PrefetchScalarGridSpec(num_scalar_pr...]
    ppermute x12 -> x6, waiting for transfers between devices: 19.9 us -> 1.15 us  [tree_send(): lax.ppermute(send, 'dp', [(i, i ^ step) for i in range(dp_count)])]
    ppermute x0 -> x9, starting transfers between devices: none -> 18.7 us  [tree(): lax.ppermute(piece(k), 'dp', [(i, i ^ k * step) for i in range(dp_count)])]
    ppermute x13 -> x10, starting transfers between devices: 15.6 us -> 24.4 us  [swap(): return lax.ppermute(value, 'mp', [(0, 1), (1, 0)])]
    all_to_all x1, waiting for transfers between devices: 7.03 us -> 0.01 us  [per_device_pair(): everyone = lax.all_to_all(packed, ('dp', 'mp'), 0, 0, tiled=True)]
    convert_element_type x10 -> x6, other arithmetic: 14.2 us -> 9.88 us  [tree_add(): return (keep.astype(F32) + came.astype(F32)).astype(BF)]
    ppermute x12 -> x6, starting transfers between devices: 8.73 us -> 12.6 us  [tree_send(): lax.ppermute(send, 'dp', [(i, i ^ step) for i in range(dp_count)])]
    ppermute x13 -> x10, waiting for transfers between devices: 32.6 us -> 29.6 us  [swap(): return lax.ppermute(value, 'mp', [(0, 1), (1, 0)])]
  transfers between devices with their start and end apart: 32 -> 32, of which waited for: 9 -> 8; matrix products, arithmetic and copies ran while one was open for 7% -> 8% of each run, Pallas kernels for 74% -> 69%
where the time goes in v2:
time: 569 us; the launch traced here: 563 us
  Pallas kernels  387 us (68%)
  starting transfers between devices  59.6 us (10%)
  waiting for transfers between devices  36.5 us (6%)
  local copies, waits for them, and re-layouts  33.2 us (6%)
  other arithmetic  25.8 us (5%)
  between operations  18.7 us (3%)
    pallas_call x26, Pallas kernels, call(): pl.pallas_call(body, grid_spec=pltpu.PrefetchScalarGridSpec(num_scalar_pr...  387 us
    ppermute x10, waiting for transfers between devices, swap(): return lax.ppermute(value, 'mp', [(0, 1), (1, 0)])  29.6 us
    ppermute x10, starting transfers between devices, swap(): return lax.ppermute(value, 'mp', [(0, 1), (1, 0)])  24.4 us
    ppermute x9, starting transfers between devices, tree(): lax.ppermute(piece(k), 'dp', [(i, i ^ k * step) for i in range(dp_count)])  18.7 us
    ppermute x6, starting transfers between devices, tree_send(): lax.ppermute(send, 'dp', [(i, i ^ step) for i in range(dp_count)])  12.6 us
  transfers between devices with their start and end apart: 32, of which 8 were waited for; matrix products, arithmetic and copies ran while one was open for 8% of the time, Pallas kernels for 69%

profile of v2, /device:TPU:0, one launch (start us, length us, event | category | flops | bytes accessed | tf_op | source)
XLA Modules:
  0.0 562.9 jit_solution(14450391175803746437)
XLA Ops:
  14.4 2.8 dynamic-slice_bitcast_fusion.5
  17.3 2.9 collective-permute-start.2
  20.2 4.9 collective-permute-done.2
  25.9 1.8 collective-permute-start
  31.3 1.8 pad_maximum_fusion.1
  34.3 16.3 %collective-permute-done.rec = bf16[1,512,1024]{2,1,0:T(8,128)(2,1)} collective-permute-done((bf16[1,512,1024]{2,1,0:T(8,128)(2,1)}, bf16[1,512,1024]{2,1,0:T(8,128)(2,1)}, u32[]{:S(2)}, u32[]{:S(2)}) %collective-permute-start) | collective-permute-done | bytes 1048608 | tf_op jit(solution)/shard_map/ppermute | solution.py:865
  50.6 1.4 collective-permute-start.3
  53.4 9.3 %shard_map.161 = (bf16[2,1024,1024]{2,1,0:T(8,128)(2,1)}, bf16[2,1024,1024]{2,1,0:T(8,128)(2,1)}, bf16[2,3,512,1024]{3,2,1,0:T(8,128)(2,1)}) custom-call(s32[7]{0:T(128)} %pad_add_fusion.m, bf16[4,512,1024]{2,1,0:T(8,128)(2,1)} %bitcast.266, bf16[1,512,1024]{2,1,0:T(8,128)(2,1)} %collective-permute-done.rec, f32[2,1,1024]{2,1,0:T(1,128)} %get-tuple-element.234.g, ...), custom_call_target="tpu_custom_call" | custom-call | flops 2576980480 | bytes 230768 | tf_op jit(solution)/shard_map/pallas_call | solution.py:252
  62.7 1.8 collective-permute-done.3
  64.5 1.5 slice.109
  66.1 1.8 fusion.40
  70.2 1.8 dynamic-slice_bitcast_fusion.4
  72.0 1.5 pad_maximum_fusion
  73.5 13.5 %shard_map.163 = (bf16[2,8,64,1024]{3,2,1,0:T(8,128)(2,1)}, f32[2,8,1,1024]{3,2,1,0:T(1,128)}) custom-call(s32[7]{0:T(128)} %pad_add_fusion.m, bf16[2,3,8,64,1024]{4,3,2,1,0:T(8,128)(2,1)} %bitcast.224, bf16[2,3,8,64,1024]{4,3,2,1,0:T(8,128)(2,1)} %bitcast.225, bf16[2,3,8,64,1024]{4,3,2,1,0:T(8,128)(2,1)} %bitcast.226), custom_call_target="tpu_custom_call" | custom-call | flops 4294967296 | bytes 210370 | tf_op jit(solution)/shard_map/pallas_call | solution.py:252
  87.0 5.2 collective-permute-done.1.rec
  93.3 7.9 %shard_map.165.refs_0_ = bf16[2,3,512,1024]{3,2,1,0:T(8,128)(2,1)} custom-call(s32[7]{0:T(128)} %pad_add_fusion.m, bf16[2,1024,1024]{2,1,0:T(8,128)(2,1)} %get-tuple-element.85.refs_1_.h_ref, bf16[3,1024,512]{2,1,0:T(8,128)(2,1)} %bitcast.246), custom_call_target="tpu_custom_call" | custom-call | flops 2576980480 | bytes 136314 | tf_op jit(solution)/shard_map/pallas_call | solution.py:252
  101.2 9.5 %shard_map.162 = (bf16[2,1024,1024]{2,1,0:T(8,128)(2,1)}, bf16[2,1024,1024]{2,1,0:T(8,128)(2,1)}, bf16[2,3,512,1024]{3,2,1,0:T(8,128)(2,1)}) custom-call(s32[7]{0:T(128)} %pad_add_fusion.m, bf16[4,512,1024]{2,1,0:T(8,128)(2,1)} %bitcast.267, ...), custom_call_target="tpu_custom_call", output_to_operand_aliasing={{0}: (5, {}), {1}: (6, {}), {2}: (7, {})} | custom-call | flops 2576980480 | bytes 377569 | tf_op jit(solution)/shard_map/pallas_call | solution.py:252
  110.7 13.5 %shard_map.167 = (bf16[2,8,64,1024]{3,2,1,0:T(8,128)(2,1)}, f32[2,8,1,1024]{3,2,1,0:T(1,128)}) custom-call(s32[7]{0:T(128)} %pad_add_fusion.m, bf16[2,3,8,64,1024]{4,3,2,1,0:T(8,128)(2,1)} %bitcast.212, bf16[2,3,8,64,1024]{4,3,2,1,0:T(8,128)(2,1)} %bitcast.213, bf16[2,3,8,64,1024]{4,3,2,1,0:T(8,128)(2,1)} %bitcast.214), custom_call_target="tpu_custom_call" | custom-call | flops 4294967296 | bytes 210370 | tf_op jit(solution)/shard_map/pallas_call | solution.py:252
  124.2 8.3 %shard_map.166 = bf16[2,3,512,1024]{3,2,1,0:T(8,128)(2,1)} custom-call(s32[7]{0:T(128)} %pad_add_fusion.m, bf16[2,1024,1024]{2,1,0:T(8,128)(2,1)} %get-tuple-element.91.h_ref, bf16[3,1024,512]{2,1,0:T(8,128)(2,1)} %bitcast.247, bf16[2,3,512,1024]{3,2,1,0:T(8,128)(2,1)} %shard_map.165.refs_0_), custom_call_target="tpu_custom_call", output_to_operand_aliasing={{}: (3, {})} | custom-call | flops 2576980480 | bytes 199229 | tf_op jit(solution)/shard_map/pallas_call | solution.py:252
  132.5 9.0 %shard_map.164 = (bf16[2,8,64,1024]{3,2,1,0:T(8,128)(2,1)}, f32[2,8,1,1024]{3,2,1,0:T(1,128)}) custom-call(s32[7]{0:T(128)} %pad_add_fusion.m, bf16[2,3,8,64,1024]{4,3,2,1,0:T(8,128)(2,1)} %bitcast.227, bf16[2,3,8,64,1024]{4,3,2,1,0:T(8,128)(2,1)} %bitcast.228, bf16[2,3,8,64,1024]{4,3,2,1,0:T(8,128)(2,1)} %bitcast.229, ...), custom_call_target="tpu_custom_call", output_to_operand_aliasing={{0}: (4, {}), {1}: (5, {})} | custom-call | flops 4294967296 | bytes 231997 | tf_op jit(solution)/shard_map/pallas_call | solution.py:252
  141.5 9.0 %shard_map.168 = (bf16[2,8,64,1024]{3,2,1,0:T(8,128)(2,1)}, f32[2,8,1,1024]{3,2,1,0:T(1,128)}) custom-call(s32[7]{0:T(128)} %pad_add_fusion.m, bf16[2,3,8,64,1024]{4,3,2,1,0:T(8,128)(2,1)} %bitcast.215, bf16[2,3,8,64,1024]{4,3,2,1,0:T(8,128)(2,1)} %bitcast.216, bf16[2,3,8,64,1024]{4,3,2,1,0:T(8,128)(2,1)} %bitcast.217, ...), custom_call_target="tpu_custom_call", output_to_operand_aliasing={{0}: (4, {}), {1}: (5, {})} | custom-call | flops 4294967296 | bytes 231997 | tf_op jit(solution)/shard_map/pallas_call | solution.py:252
  150.5 11.4 %shard_map.169 = (bf16[2,1024,1024]{2,1,0:T(8,128)(2,1)}, bf16[2,1024,1024]{2,1,0:T(8,128)(2,1)}) custom-call(s32[7]{0:T(128)} %pad_add_fusion.m, bf16[2,512,1024]{2,1,0:T(8,128)(2,1)} %bitcast.253, bf16[2,512,1024]{2,1,0:T(8,128)(2,1)} %bitcast.255, bf16[2,1024,1024]{2,1,0:T(8,128)(2,1)} %get-tuple-element.98.t.tok, bf16[512,1024]{1,0:T(8,128)(2,1)} %wa.7, ...), custom_call_target="tpu_custom_call" | custom-call | flops 2147483648 | bytes 188825 | tf_op jit(solution)/shard_map/pallas_call | solution.py:252
  161.9 64.2 %shard_map.170 = (bf16[2048,1024]{1,0:T(8,128)(2,1)}, bf16[2048,1024]{1,0:T(8,128)(2,1)}, bf16[2,1024,2048]{2,1,0:T(8,128)(2,1)}) custom-call(s32[7]{0:T(128)} %pad_add_fusion.m, bf16[2048,1024]{1,0:T(8,128)(2,1)} %bitcast.295, bf16[4,512,1024]{2,1,0:T(8,128)(2,1)} %bitcast.263, bf16[2,512,1024]{2,1,0:T(8,128)(2,1)} %collective-permute-done.4.came.cr, ...), custom_call_target="tpu_custom_call" | custom-call | flops 20615843840 | bytes 356515 | tf_op jit(solution)/shard_map/pallas_call | solution.py:252
  226.2 64.6 %shard_map.171 = (bf16[2048,1024]{1,0:T(8,128)(2,1)}, bf16[2048,1024]{1,0:T(8,128)(2,1)}, bf16[2,1024,2048]{2,1,0:T(8,128)(2,1)}) custom-call(s32[7]{0:T(128)} %pad_add_fusion.m, bf16[2048,1024]{1,0:T(8,128)(2,1)} %bitcast.296, bf16[4,512,1024]{2,1,0:T(8,128)(2,1)} %bitcast.264, bf16[2,512,1024]{2,1,0:T(8,128)(2,1)} %collective-permute-done.4.came.cr, ...), custom_call_target="tpu_custom_call" | custom-call | flops 20615843840 | bytes 356515 | tf_op jit(solution)/shard_map/pallas_call | solution.py:252
  290.9 28.1 %shard_map.172 = (bf16[4,512,1024]{2,1,0:T(8,128)(2,1)}, bf16[2,512,1024]{2,1,0:T(8,128)(2,1)}, bf16[2,1024,1024]{2,1,0:T(8,128)(2,1)}, bf16[2,512,1024]{2,1,0:T...) custom-call(s32[7]{0:T(128)} %pad_add_fusion.m, ...), custom_call_target="tpu_custom_call" | custom-call | flops 8589934592 | bytes 503480 | tf_op jit(solution)/shard_map/pallas_call | solution.py:252
  319.0 1.3 dynamic-slice_bitcast_fusion.2
  320.5 19.0 %shard_map.173.refs_0_ = bf16[2,3,8,64,1024]{4,3,2,1,0:T(8,128)(2,1)} custom-call(s32[7]{0:T(128)} %pad_add_fusion.m, bf16[2,3,8,64,1024]{4,3,2,1,0:T(8,128)(2,1)} %bitcast.218, bf16[2,3,8,64,1024]{4,3,2,1,0:T(8,128)(2,1)} %bitcast.219, bf16[2,3,8,64,1024]{4,3,2,1,0:T(8,128)(2,1)} %bitcast.220, bf16[2,8,64,1024]{3,2,1,0:T(8,128)(2,1)} %get-tuple-element.97.o, ...), custom_call_target="tpu_custom_call" | custom-call | flops 429496736 | bytes 294256 | tf_op jit(solution)/shard_map/pallas_call | solution.py:252
  339.5 1.9 fusion.2
  341.5 1.5 collective-permute-start.6
  343.0 12.0 %shard_map.174 = bf16[2,3,8,64,1024]{4,3,2,1,0:T(8,128)(2,1)} custom-call(s32[7]{0:T(128)} %pad_add_fusion.m, bf16[2,3,8,64,1024]{4,3,2,1,0:T(8,128)(2,1)} %bitcast.221, bf16[2,3,8,64,1024]{4,3,2,1,0:T(8,128)(2,1)} %bitcast.222, bf16[2,3,8,64,1024]{4,3,2,1,0:T(8,128)(2,1)} %bitcast.223, ...), custom_call_target="tpu_custom_call", output_to_operand_aliasing={{}: (7, {})} | custom-call | flops 429496736 | bytes 357171 | tf_op jit(solution)/shard_map/pallas_call | solution.py:252
  355.2 12.3 %shard_map.175 = bf16[3,1024,512]{2,1,0:T(8,128)(2,1)} custom-call(s32[7]{0:T(128)} %pad_add_fusion.m, bf16[2,1024,1024]{2,1,0:T(8,128)(2,1)} %get-tuple-element.91.h_ref, bf16[2,3,512,1024]{3,2,1,0:T(8,128)(2,1)} %bitcast.241), custom_call_target="tpu_custom_call" | custom-call | flops 128849016 | bytes 136314 | tf_op jit(solution)/shard_map/pallas_call | solution.py:252
  367.5 2.9 dynamic-slice_bitcast_fusion.1
  370.4 5.8 %collective-permute-start.7 = (bf16[3,8,1,64,512]{4,3,1,0,2:T(8,128)(2,1)}, bf16[3,8,1,64,512]{4,3,1,0,2:T(8,128)(2,1)}, u32[]{:S(2)}, u32[]{:S(2)}) collective-permute-start(bf16[3,8,1,64,512]{4,3,1,0,2:T(8,128)(2,1)} %dynamic-slice_bitcast_fusion.1), channel_id=1, source_target_pairs={{0,2},{2,0},{4,6},{6,4},{8,10},{10,8},{12,14},{14,12},{16,18},{18,... | collective-permute-start | bytes 4718600 | tf_op jit(solution)/shard_map/ppermute | solution.py:927
  376.3 1.5 fusion.39
  377.8 12.3 %collective-permute-start.9 = (bf16[1,512,1024]{2,1,0:T(8,128)(2,1)}, bf16[1,512,1024]{2,1,0:T(8,128)(2,1)}, u32[]{:S(2)}, u32[]{:S(2)}) collective-permute-start(bf16[1,512,1024]{2,1,0:T(8,128)(2,1)} %get-tuple-element.121), channel_id=1, source_target_pairs={{0,1},{1,0},{2,3},{3,2},{4,5},{5,4},{6,7},{7,6},{8,9},{9,8},{10,11... | collective-permute-start | bytes 3145736 | tf_op jit(solution)/shard_map/ppermute | solution.py:865
  390.1 19.3 %shard_map.176.refs_0_ = bf16[2,3,8,64,1024]{4,3,2,1,0:T(8,128)(2,1)} custom-call(s32[7]{0:T(128)} %pad_add_fusion.m, bf16[2,3,8,64,1024]{4,3,2,1,0:T(8,128)(2,1)} %bitcast.230, bf16[2,3,8,64,1024]{4,3,2,1,0:T(8,128)(2,1)} %bitcast.231, bf16[2,3,8,64,1024]{4,3,2,1,0:T(8,128)(2,1)} %bitcast.232, bf16[2,8,64,1024]{3,2,1,0:T(8,128)(2,1)} %get-tuple-element.90.o, ...), custom_call_target="tpu_custom_call" | custom-call | flops 429496736 | bytes 294256 | tf_op jit(solution)/shard_map/pallas_call | solution.py:252
  409.4 2.5 fusion.1
  413.9 7.1 %collective-permute-start.13 = (bf16[2,64,512]{2,1,0:T(8,128)(2,1)S(1)}, bf16[2,64,512]{2,1,0:T(8,128)(2,1)S(1)}, u32[]{:S(2)}, u32[]{:S(2)}) collective-permute-start(bf16[2,64,512]{2,1,0:T(8,128)(2,1)S(1)} %get-tuple-element.231), channel_id=1, source_target_pairs={{0,24},{2,26},{4,28},{6,30},{8,16},{10,18},{12,20},{14,22},{16,8},... | collective-permute-start | bytes 393224 | tf_op jit(solution)/shard_map/ppermute | solution.py:948
  421.6 11.8 %shard_map.177 = bf16[2,3,8,64,1024]{4,3,2,1,0:T(8,128)(2,1)} custom-call(s32[7]{0:T(128)} %pad_add_fusion.m, bf16[2,3,8,64,1024]{4,3,2,1,0:T(8,128)(2,1)} %bitcast.233, bf16[2,3,8,64,1024]{4,3,2,1,0:T(8,128)(2,1)} %bitcast.234, bf16[2,3,8,64,1024]{4,3,2,1,0:T(8,128)(2,1)} %bitcast.235, ...), custom_call_target="tpu_custom_call", output_to_operand_aliasing={{}: (7, {})} | custom-call | flops 429496736 | bytes 357171 | tf_op jit(solution)/shard_map/pallas_call | solution.py:252
  434.5 1.6 fusion.4
  436.3 12.2 %shard_map.178 = bf16[3,1024,512]{2,1,0:T(8,128)(2,1)} custom-call(s32[7]{0:T(128)} %pad_add_fusion.m, bf16[2,1024,1024]{2,1,0:T(8,128)(2,1)} %get-tuple-element.91.h_ref, bf16[2,3,512,1024]{3,2,1,0:T(8,128)(2,1)} %bitcast.236), custom_call_target="tpu_custom_call" | custom-call | flops 128849016 | bytes 136314 | tf_op jit(solution)/shard_map/pallas_call | solution.py:252
  448.4 2.8 dynamic-slice_bitcast_fusion
  451.2 4.0 collective-permute-start.14
  456.4 6.2 %collective-permute-start.18 = (bf16[3,64,512]{2,1,0:T(8,128)(2,1)}, bf16[3,64,512]{2,1,0:T(8,128)(2,1)}, u32[]{:S(2)}, u32[]{:S(2)}) collective-permute-start(bf16[3,64,512]{2,1,0:T(8,128)(2,1)} %get-tuple-element.226), channel_id=1, source_target_pairs={{0,24},{2,26},{4,28},{6,30},{8,16},{10,18},{12,20},{14,22},{16,8},... | collective-permute-start | bytes 589832 | tf_op jit(solution)/shard_map/ppermute | solution.py:948
  463.2 10.0 %shard_map.179 = (bf16[1,512,1024]{2,1,0:T(8,128)(2,1)}, f32[1,1,1024]{2,1,0:T(1,128)}) custom-call(s32[7]{0:T(128)} %pad_add_fusion.m, bf16[2,1024,1024]{2,1,0:T(8,128)(2,1)} %get-tuple-element.98.t.tok, bf16[2,1024,1024]{2,1,0:T(8,128)(2,1)} %get-tuple-element.132.br, bf16[2,3,512,1024]{3,2,1,0:T(8,128)(2,1)} %bitcast.237, ...), custom_call_target="tpu_custom_call" | custom-call | flops 64424508 | bytes 283238 | tf_op jit(solution)/shard_map/pallas_call | solution.py:252
  473.2 1.8 collective-permute-start.20
  475.0 2.5 fusion
  477.5 10.0 %shard_map.180 = (bf16[1,512,1024]{2,1,0:T(8,128)(2,1)}, f32[1,1,1024]{2,1,0:T(1,128)}) custom-call(s32[7]{0:T(128)} %pad_add_fusion.m, bf16[2,1024,1024]{2,1,0:T(8,128)(2,1)} %get-tuple-element.98.t.tok, bf16[2,1024,1024]{2,1,0:T(8,128)(2,1)} %get-tuple-element.132.br, bf16[2,3,512,1024]{3,2,1,0:T(8,128)(2,1)} %bitcast.238, ...), custom_call_target="tpu_custom_call" | custom-call | flops 64424508 | bytes 283238 | tf_op jit(solution)/shard_map/pallas_call | solution.py:252
  489.2 1.2 fusion.12
  494.5 1.6 collective-permute-start.24
  496.0 10.0 %shard_map.181 = (bf16[4,512,1024]{2,1,0:T(8,128)(2,1)}, f32[1,1,1024]{2,1,0:T(1,128)}) custom-call(s32[7]{0:T(128)} %pad_add_fusion.m, bf16[2,1024,1024]{2,1,0:T(8,128)(2,1)} %get-tuple-element.98.t.tok, bf16[2,1024,1024]{2,1,0:T(8,128)(2,1)} %get-tuple-element.132.br, bf16[2,3,512,1024]{3,2,1,0:T(8,128)(2,1)} %bitcast.239, ...), custom_call_target="tpu_custom_call" | custom-call | flops 64424508 | bytes 314695 | tf_op jit(solution)/shard_map/pallas_call | solution.py:252
  507.9 1.4 fusion.3
  509.2 10.3 %shard_map.182 = (bf16[4,512,1024]{2,1,0:T(8,128)(2,1)}, f32[1,1,1024]{2,1,0:T(1,128)}) custom-call(s32[7]{0:T(128)} %pad_add_fusion.m, bf16[2,1024,1024]{2,1,0:T(8,128)(2,1)} %get-tuple-element.98.t.tok, bf16[2,1024,1024]{2,1,0:T(8,128)(2,1)} %get-tuple-element.132.br, bf16[2,3,512,1024]{3,2,1,0:T(8,128)(2,1)} %bitcast.240, ...), custom_call_target="tpu_custom_call", output_to_operand_aliasing={{0}: (8, {})} | custom-call | flops 64424508 | bytes 356638 | tf_op jit(solution)/shard_map/pallas_call | solution.py:252
  520.8 1.2 collective-permute-done.19.src
  522.7 3.3 all-to-all-start
  526.9 1.8 collective-permute-start.21
  528.7 2.4 collective-permute-start.23
  531.1 2.9 shard_map.183._
  534.0 2.9 shard_map.184
  536.9 2.9 shard_map.185._
  539.9 2.9 shard_map.186
  543.7 5.6 collective-permute-done.22
  551.3 1.7 fusion.21
  553.7 2.1 fusion.6
  (154 shorter events, 33.7 us)
Async XLA Ops:
  7.2 86.2 %all-gather.5.cloned.1.call-start = ((), (), s32[]{:S(2)}) async-start(), calls=%async_computation.3 | async-start | bytes 3342336 | tf_op jit(solution)/shard_map/all_gather | solution.py:872
  14.4 18.8 %copy-start.2 = (f32[256,2048]{1,0:T(8,128)S(1)}, f32[256,2048]{1,0:T(8,128)}, u32[]{:S(2)}) copy-start(f32[256,2048]{1,0:T(8,128)} %param.14) | copy-start | bytes 6291460
  17.3 34.8 %copy-start.9 = (f32[2,1024]{1,0:T(2,128)S(1)}, f32[2,1024]{1,0:T(2,128)}, u32[]{:S(2)}) copy-start(f32[2,1024]{1,0:T(2,128)} %param.13) | copy-start | bytes 24580
  17.3 7.8 %collective-permute-start.2 = (bf16[192,512]{1,0:T(8,128)(2,1)S(1)}, bf16[192,512]{1,0:T(8,128)(2,1)S(1)}, u32[]{:S(2)}, u32[]{:S(2)}) collective-permute-start(bf16[192,512]{1,0:T(8,128)(2,1)S(1)} %constant_dynamic-slice_fusion.9), channel_id=1, source_target_pairs={{0,1},{1,0},{2,3},{3,2},{4,5},{5,4},{6,7},{7,6},{8,9},{9,8},{10,11... | collective-permute-start | bytes 589832 | tf_op jit(solution)/shard_map/ppermute | solution.py:865
  25.1 0.7 copy-start.6
  25.8 124.7 %all-gather.7.cloned.1.call-start = ((), (), s32[]{:S(2)}) async-start(), calls=%async_computation.4 | async-start | bytes 1114112 | tf_op jit(solution)/shard_map/all_gather | solution.py:872
  25.9 24.7 %collective-permute-start = (bf16[1,512,1024]{2,1,0:T(8,128)(2,1)}, bf16[1,512,1024]{2,1,0:T(8,128)(2,1)}, u32[]{:S(2)}, u32[]{:S(2)}) collective-permute-start(bf16[1,512,1024]{2,1,0:T(8,128)(2,1)} %get-tuple-element.206), channel_id=1, source_target_pairs={{0,1},{1,0},{2,3},{3,2},{4,5},{5,4},{6,7},{7,6},{8,9},{9,8},{10,11... | collective-permute-start | bytes 3145736 | tf_op jit(solution)/shard_map/ppermute | solution.py:865
  33.2 17.4 %copy-start.12 = (f32[2,128]{1,0:T(2,128)}, f32[2,128]{1,0:T(2,128)S(1)}, u32[]{:S(2)}) copy-start(f32[2,128]{1,0:T(2,128)S(1)} %get-tuple-element.239) | copy-start | bytes 3076
  33.2 17.4 %copy-start.14 = (f32[2,128]{1,0:T(2,128)}, f32[2,128]{1,0:T(2,128)S(1)}, u32[]{:S(2)}) copy-start(f32[2,128]{1,0:T(2,128)S(1)} %get-tuple-element.240) | copy-start | bytes 3076
  34.3 28.4 %copy-start.7 = (f32[2,2048]{1,0:T(2,128)}, f32[2,2048]{1,0:T(2,128)S(1)}, u32[]{:S(2)}) copy-start(f32[2,2048]{1,0:T(2,128)S(1)} %convolution_add_fusion) | copy-start | bytes 49156
  50.6 13.9 %collective-permute-start.3 = (bf16[288,1024]{1,0:T(8,128)(2,1)}, bf16[288,1024]{1,0:T(8,128)(2,1)}, u32[]{:S(2)}, u32[]{:S(2)}) collective-permute-start(bf16[288,1024]{1,0:T(8,128)(2,1)} %pad_maximum_fusion.1), channel_id=1, source_target_pairs={{0,1},{1,0},{2,3},{3,2},{4,5},{5,4},{6,7},{7,6},{8,9},{9,8},{10,11... | collective-permute-start | bytes 1769480 | tf_op jit(solution)/shard_map/ppermute | solution.py:865
  66.0 160.2 %all-gather.11.cloned.1.call-start = ((), (), s32[]{:S(2)}) async-start(), calls=%async_computation.6 | async-start | bytes 4456448 | tf_op jit(solution)/shard_map/all_gather | solution.py:872
  67.9 158.4 %all-gather.9.cloned.1.call-start = ((), (), s32[]{:S(2)}) async-start(), calls=%async_computation.5 | async-start | bytes 4456448 | tf_op jit(solution)/shard_map/all_gather | solution.py:872
  68.7 321.4 %reduce-scatter.3.cloned.1.call-start = ((), (), s32[]{:S(2)}) async-start(), calls=%async_computation.7 | async-start | bytes 8912896 | tf_op jit(solution)/shard_map/reduce_scatter | solution.py:958
  69.1 23.2 %collective-permute-start.1 = (bf16[1,512,1024]{2,1,0:T(8,128)(2,1)S(1)}, bf16[1,512,1024]{2,1,0:T(8,128)(2,1)}, u32[]{:S(2)}, u32[]{:S(2)}) collective-permute-start(bf16[1,512,1024]{2,1,0:T(8,128)(2,1)S(1)} %get-tuple-element.83), channel_id=1, source_target_pairs={{0,1},{1,0},{2,3},{3,2},{4,5},{5,4},{6,7},{7,6},{8,9},{9,8},{10,11... | collective-permute-start | bytes 3145736 | tf_op jit(solution)/shard_map/ppermute | solution.py:865
  92.2 69.6 %collective-permute-start.4 = (bf16[2,512,1024]{2,1,0:T(8,128)(2,1)}, bf16[2,512,1024]{2,1,0:T(8,128)(2,1)}, u32[]{:S(2)}, u32[]{:S(2)}) collective-permute-start(bf16[2,512,1024]{2,1,0:T(8,128)(2,1)} %pad_maximum_fusion), channel_id=1, source_target_pairs={{0,1},{1,0},{2,3},{3,2},{4,5},{5,4},{6,7},{7,6},{8,9},{9,8},{10,11... | collective-permute-start | bytes 6291464 | tf_op jit(solution)/shard_map/ppermute | solution.py:865
  226.1 237.1 %reduce-scatter.5.cloned.1.call-start = ((), (), s32[]{:S(2)}) async-start(), calls=%async_computation.8 | async-start | bytes 8912896 | tf_op jit(solution)/shard_map/reduce_scatter | solution.py:958
  320.3 19.2 %collective-permute-start.5 = (bf16[2,8,1,64,512]{4,3,1,0,2:T(8,128)(2,1)S(1)}, bf16[2,8,1,64,512]{4,3,1,0,2:T(8,128)(2,1)}, u32[]{:S(2)}, u32[]{:S(2)}) collective-permute-start(bf16[2,8,1,64,512]{4,3,1,0,2:T(8,128)(2,1)S(1)} %dynamic-slice_bitcast_fusion.2), channel_id=1, source_target_pairs={{0,2},{2,0},{4,6},{6,4},{8,10},{10,8},{12,14},{14,12},{16,18},{18,... | collective-permute-start | bytes 3145736 | tf_op jit(solution)/shard_map/ppermute | solution.py:927
  341.5 13.5 %collective-permute-start.6 = (bf16[2,4,1,64,512]{4,3,0,2,1:T(8,128)(2,1)S(1)}, bf16[2,4,1,64,512]{4,3,0,2,1:T(8,128)(2,1)S(1)}, u32[]{:S(2)}, u32[]{:S(2)}) collective-permute-start(bf16[2,4,1,64,512]{4,3,0,2,1:T(8,128)(2,1)S(1)} %bitcast.282), channel_id=1, source_target_pairs={{0,4},{2,6},{4,0},{6,2},{8,12},{10,14},{12,8},{14,10},{16,20},{18,... | collective-permute-start | bytes 1572872 | tf_op jit(solution)/shard_map/ppermute | solution.py:927
  367.5 8.7 %copy-start.3 = (bf16[2,512,1024]{2,1,0:T(8,128)(2,1)S(1)}, bf16[2,512,1024]{2,1,0:T(8,128)(2,1)}, u32[]{:S(2)}) copy-start(bf16[2,512,1024]{2,1,0:T(8,128)(2,1)} %get-tuple-element.120) | copy-start | bytes 6291460
  370.4 39.0 %collective-permute-start.7 = (bf16[3,8,1,64,512]{4,3,1,0,2:T(8,128)(2,1)}, bf16[3,8,1,64,512]{4,3,1,0,2:T(8,128)(2,1)}, u32[]{:S(2)}, u32[]{:S(2)}) collective-permute-start(bf16[3,8,1,64,512]{4,3,1,0,2:T(8,128)(2,1)} %dynamic-slice_bitcast_fusion.1), channel_id=1, source_target_pairs={{0,2},{2,0},{4,6},{6,4},{8,10},{10,8},{12,14},{14,12},{16,18},{18,... | collective-permute-start | bytes 4718600 | tf_op jit(solution)/shard_map/ppermute | solution.py:927
  377.8 43.2 %collective-permute-start.9 = (bf16[1,512,1024]{2,1,0:T(8,128)(2,1)}, bf16[1,512,1024]{2,1,0:T(8,128)(2,1)}, u32[]{:S(2)}, u32[]{:S(2)}) collective-permute-start(bf16[1,512,1024]{2,1,0:T(8,128)(2,1)} %get-tuple-element.121), channel_id=1, source_target_pairs={{0,1},{1,0},{2,3},{3,2},{4,5},{5,4},{6,7},{7,6},{8,9},{9,8},{10,11... | collective-permute-start | bytes 3145736 | tf_op jit(solution)/shard_map/ppermute | solution.py:865
  413.0 21.4 %collective-permute-start.8 = (bf16[3,4,1,64,512]{4,3,0,2,1:T(8,128)(2,1)}, bf16[3,4,1,64,512]{4,3,0,2,1:T(8,128)(2,1)}, u32[]{:S(2)}, u32[]{:S(2)}) collective-permute-start(bf16[3,4,1,64,512]{4,3,0,2,1:T(8,128)(2,1)} %bitcast.209), channel_id=1, source_target_pairs={{0,4},{2,6},{4,0},{6,2},{8,12},{10,14},{12,8},{14,10},{16,20},{18,... | collective-permute-start | bytes 2359304 | tf_op jit(solution)/shard_map/ppermute | solution.py:927
  413.8 22.4 %collective-permute-start.10 = (bf16[1,512,1024]{2,1,0:T(8,128)(2,1)}, bf16[1,512,1024]{2,1,0:T(8,128)(2,1)}, u32[]{:S(2)}, u32[]{:S(2)}) collective-permute-start(bf16[1,512,1024]{2,1,0:T(8,128)(2,1)} %get-tuple-element.124), channel_id=1, source_target_pairs={{0,1},{1,0},{2,3},{3,2},{4,5},{5,4},{6,7},{7,6},{8,9},{9,8},{10,11... | collective-permute-start | bytes 3145736 | tf_op jit(solution)/shard_map/ppermute | solution.py:865
  413.9 19.6 %collective-permute-start.13 = (bf16[2,64,512]{2,1,0:T(8,128)(2,1)S(1)}, bf16[2,64,512]{2,1,0:T(8,128)(2,1)S(1)}, u32[]{:S(2)}, u32[]{:S(2)}) collective-permute-start(bf16[2,64,512]{2,1,0:T(8,128)(2,1)S(1)} %get-tuple-element.231), channel_id=1, source_target_pairs={{0,24},{2,26},{4,28},{6,30},{8,16},{10,18},{12,20},{14,22},{16,8},... | collective-permute-start | bytes 393224 | tf_op jit(solution)/shard_map/ppermute | solution.py:948
  421.0 12.5 %collective-permute-start.12 = (bf16[2,64,512]{2,1,0:T(8,128)(2,1)S(1)}, bf16[2,64,512]{2,1,0:T(8,128)(2,1)S(1)}, u32[]{:S(2)}, u32[]{:S(2)}) collective-permute-start(bf16[2,64,512]{2,1,0:T(8,128)(2,1)S(1)} %get-tuple-element.232), channel_id=1, source_target_pairs={{0,16},{2,18},{4,20},{6,22},{8,24},{10,26},{12,28},{14,30},{16,0},... | collective-permute-start | bytes 393224 | tf_op jit(solution)/shard_map/ppermute | solution.py:948
  421.0 12.5 %collective-permute-start.11 = (bf16[2,64,512]{2,1,0:T(8,128)(2,1)S(1)}, bf16[2,64,512]{2,1,0:T(8,128)(2,1)}, u32[]{:S(2)}, u32[]{:S(2)}) collective-permute-start(bf16[2,64,512]{2,1,0:T(8,128)(2,1)S(1)} %get-tuple-element.230), channel_id=1, source_target_pairs={{0,8},{2,10},{4,12},{6,14},{8,0},{10,2},{12,4},{14,6},{16,24},{18,... | collective-permute-start | bytes 393224 | tf_op jit(solution)/shard_map/ppermute | solution.py:948
  436.1 19.5 %copy-start = (bf16[3,4,1,64,512]{4,3,0,2,1:T(8,128)(2,1)}, bf16[3,4,1,64,512]{4,3,0,2,1:T(8,128)(2,1)S(1)}, u32[]{:S(2)}) copy-start(bf16[3,4,1,64,512]{4,3,0,2,1:T(8,128)(2,1)S(1)} %fusion.4) | copy-start | bytes 2359300
  448.4 6.8 %copy-start.10 = (f32[2,1024]{1,0:T(2,128)S(1)}, f32[2,1024]{1,0:T(2,128)}, u32[]{:S(2)}) copy-start(f32[2,1024]{1,0:T(2,128)} %param.13) | copy-start | bytes 24580
  448.4 6.9 %copy-start.13 = (f32[2,128]{1,0:T(2,128)S(1)}, f32[2,128]{1,0:T(2,128)}, u32[]{:S(2)}) copy-start(f32[2,128]{1,0:T(2,128)} %copy-done.12) | copy-start | bytes 3076
  448.4 6.9 %copy-start.15 = (f32[2,128]{1,0:T(2,128)S(1)}, f32[2,128]{1,0:T(2,128)}, u32[]{:S(2)}) copy-start(f32[2,128]{1,0:T(2,128)} %copy-done.14) | copy-start | bytes 3076
  448.4 7.0 %copy-start.11 = (f32[2,1,1024]{2,1,0:T(1,128)S(1)}, f32[2,1,1024]{2,1,0:T(1,128)}, u32[]{:S(2)}) copy-start(f32[2,1,1024]{2,1,0:T(1,128)} %get-tuple-element.151) | copy-start | bytes 24580
  451.2 23.8 %collective-permute-start.14 = (bf16[3,8,1,64,512]{4,3,1,0,2:T(8,128)(2,1)}, bf16[3,8,1,64,512]{4,3,1,0,2:T(8,128)(2,1)}, u32[]{:S(2)}, u32[]{:S(2)}) collective-permute-start(bf16[3,8,1,64,512]{4,3,1,0,2:T(8,128)(2,1)} %dynamic-slice_bitcast_fusion), channel_id=1, source_target_pairs={{0,2},{2,0},{4,6},{6,4},{8,10},{10,8},{12,14},{14,12},{16,18},{18,... | collective-permute-start | bytes 4718600 | tf_op jit(solution)/shard_map/ppermute | solution.py:927
  456.4 31.4 %collective-permute-start.16 = (bf16[3,64,512]{2,1,0:T(8,128)(2,1)}, bf16[3,64,512]{2,1,0:T(8,128)(2,1)S(1)}, u32[]{:S(2)}, u32[]{:S(2)}) collective-permute-start(bf16[3,64,512]{2,1,0:T(8,128)(2,1)} %get-tuple-element.225), channel_id=1, source_target_pairs={{0,8},{2,10},{4,12},{6,14},{8,0},{10,2},{12,4},{14,6},{16,24},{18,... | collective-permute-start | bytes 589832 | tf_op jit(solution)/shard_map/ppermute | solution.py:948
  456.4 31.3 %collective-permute-start.18 = (bf16[3,64,512]{2,1,0:T(8,128)(2,1)}, bf16[3,64,512]{2,1,0:T(8,128)(2,1)}, u32[]{:S(2)}, u32[]{:S(2)}) collective-permute-start(bf16[3,64,512]{2,1,0:T(8,128)(2,1)} %get-tuple-element.226), channel_id=1, source_target_pairs={{0,24},{2,26},{4,28},{6,30},{8,16},{10,18},{12,20},{14,22},{16,8},... | collective-permute-start | bytes 589832 | tf_op jit(solution)/shard_map/ppermute | solution.py:948
  462.7 25.1 %collective-permute-start.17 = (bf16[3,64,512]{2,1,0:T(8,128)(2,1)}, bf16[3,64,512]{2,1,0:T(8,128)(2,1)}, u32[]{:S(2)}, u32[]{:S(2)}) collective-permute-start(bf16[3,64,512]{2,1,0:T(8,128)(2,1)} %get-tuple-element.227), channel_id=1, source_target_pairs={{0,16},{2,18},{4,20},{6,22},{8,24},{10,26},{12,28},{14,30},{16,0},... | collective-permute-start | bytes 589832 | tf_op jit(solution)/shard_map/ppermute | solution.py:948
  473.2 47.6 %collective-permute-start.20 = (bf16[1,512,1024]{2,1,0:T(8,128)(2,1)}, bf16[1,512,1024]{2,1,0:T(8,128)(2,1)}, u32[]{:S(2)}, u32[]{:S(2)}) collective-permute-start(bf16[1,512,1024]{2,1,0:T(8,128)(2,1)} %get-tuple-element.133), channel_id=1, source_target_pairs={{0,1},{1,0},{2,3},{3,2},{4,5},{5,4},{6,7},{7,6},{8,9},{9,8},{10,11... | collective-permute-start | bytes 3145736 | tf_op jit(solution)/shard_map/ppermute | solution.py:865
  487.5 2.9 copy-start.4
  487.5 34.5 %collective-permute-start.19 = (bf16[1,512,1024]{2,1,0:T(8,128)(2,1)}, bf16[1,512,1024]{2,1,0:T(8,128)(2,1)}, u32[]{:S(2)}, u32[]{:S(2)}) collective-permute-start(bf16[1,512,1024]{2,1,0:T(8,128)(2,1)} %get-tuple-element.136), channel_id=1, source_target_pairs={{0,1},{1,0},{2,3},{3,2},{4,5},{5,4},{6,7},{7,6},{8,9},{9,8},{10,11... | collective-permute-start | bytes 3145736 | tf_op jit(solution)/shard_map/ppermute | solution.py:865
  488.9 19.0 %collective-permute-start.15 = (bf16[3,4,1,64,512]{4,3,0,2,1:T(8,128)(2,1)S(1)}, bf16[3,4,1,64,512]{4,3,0,2,1:T(8,128)(2,1)}, u32[]{:S(2)}, u32[]{:S(2)}) collective-permute-start(bf16[3,4,1,64,512]{4,3,0,2,1:T(8,128)(2,1)S(1)} %bitcast.281), channel_id=1, source_target_pairs={{0,4},{2,6},{4,0},{6,2},{8,12},{10,14},{12,8},{14,10},{16,20},{18,... | collective-permute-start | bytes 2359304 | tf_op jit(solution)/shard_map/ppermute | solution.py:927
  494.5 11.6 %copy-start.17 = (f32[1,1,1024]{2,1,0:T(1,128)S(1)}, f32[1,1,1024]{2,1,0:T(1,128)}, u32[]{:S(2)}) copy-start(f32[1,1,1024]{2,1,0:T(1,128)} %get-tuple-element.147) | copy-start | bytes 12292
  494.5 13.4 %copy-start.1 = (bf16[3,4,1,1,64,512]{5,4,3,1,0,2:T(8,128)(2,1)S(1)}, bf16[3,4,1,1,64,512]{5,4,3,1,0,2:T(8,128)(2,1)}, u32[]{:S(2)}) copy-start(bf16[3,4,1,1,64,512]{5,4,3,1,0,2:T(8,128)(2,1)} %get-tuple-element.210) | copy-start | bytes 2359300
  494.5 48.4 %collective-permute-start.24 = (bf16[64,6144]{1,0:T(8,128)(2,1)}, bf16[64,6144]{1,0:T(8,128)(2,1)}, u32[]{:S(2)}, u32[]{:S(2)}) collective-permute-start(bf16[64,6144]{1,0:T(8,128)(2,1)} %fusion.22), channel_id=1, source_target_pairs={{0,1},{1,0},{2,3},{3,2},{4,5},{5,4},{6,7},{7,6},{8,9},{9,8},{10,11... | collective-permute-start | bytes 2359304 | tf_op jit(solution)/shard_map/ppermute | solution.py:865
  509.2 10.4 %copy-start.16 = (f32[1,1,1024]{2,1,0:T(1,128)S(1)}, f32[1,1,1024]{2,1,0:T(1,128)}, u32[]{:S(2)}) copy-start(f32[1,1,1024]{2,1,0:T(1,128)} %get-tuple-element.149) | copy-start | bytes 12292
  509.2 11.3 %copy-start.8 = (f32[2,2048]{1,0:T(2,128)S(1)}, f32[2,2048]{1,0:T(2,128)}, u32[]{:S(2)}) copy-start(f32[2,2048]{1,0:T(2,128)} %copy-done.7) | copy-start | bytes 49156
  522.7 20.0 %all-to-all-start = ((f32[32,1,704]{2,1,0:T(1,128)}), f32[32,1,704]{2,1,0:T(1,128)S(1)}, u32[]{:S(2)}, u32[]{:S(2)}) async-start(f32[32,1,704]{2,1,0:T(1,128)} %all_to_all.8), calls=%async_computation.2 | async-start | bytes 196608 | tf_op jit(solution)/shard_map/all_to_all | solution.py:1049
  526.9 16.8 %collective-permute-start.21 = (bf16[3,64,512]{2,1,0:T(8,128)(2,1)}, bf16[3,64,512]{2,1,0:T(8,128)(2,1)S(1)}, u32[]{:S(2)}, u32[]{:S(2)}) collective-permute-start(bf16[3,64,512]{2,1,0:T(8,128)(2,1)} %get-tuple-element.222), channel_id=1, source_target_pairs={{0,8},{2,10},{4,12},{6,14},{8,0},{10,2},{12,4},{14,6},{16,24},{18,... | collective-permute-start | bytes 589832 | tf_op jit(solution)/shard_map/ppermute | solution.py:948
  528.7 15.0 %collective-permute-start.23 = (bf16[3,64,512]{2,1,0:T(8,128)(2,1)}, bf16[3,64,512]{2,1,0:T(8,128)(2,1)}, u32[]{:S(2)}, u32[]{:S(2)}) collective-permute-start(bf16[3,64,512]{2,1,0:T(8,128)(2,1)} %get-tuple-element.223), channel_id=1, source_target_pairs={{0,24},{2,26},{4,28},{6,30},{8,16},{10,18},{12,20},{14,22},{16,8},... | collective-permute-start | bytes 589832 | tf_op jit(solution)/shard_map/ppermute | solution.py:948
  531.0 18.2 %collective-permute-start.22 = (bf16[3,64,512]{2,1,0:T(8,128)(2,1)}, bf16[3,64,512]{2,1,0:T(8,128)(2,1)}, u32[]{:S(2)}, u32[]{:S(2)}) collective-permute-start(bf16[3,64,512]{2,1,0:T(8,128)(2,1)} %get-tuple-element.224), channel_id=1, source_target_pairs={{0,16},{2,18},{4,20},{6,22},{8,24},{10,26},{12,28},{14,30},{16,0},... | collective-permute-start | bytes 589832 | tf_op jit(solution)/shard_map/ppermute | solution.py:948
  542.8 10.9 %copy-start.5 = (bf16[2,64,2048]{2,1,0:T(8,128)(2,1)S(1)}, bf16[2,64,2048]{2,1,0:T(8,128)(2,1)}, u32[]{:S(2)}) copy-start(bf16[2,64,2048]{2,1,0:T(8,128)(2,1)} %reduce-scatter.3.cloned.1.call-done) | copy-start | bytes 1572868
Sparse Core Ops, SparseCore 0:
  25.9 46.9 all-gather.4
  75.6 36.7 all-gather.6
  115.2 49.0 all-gather.10
  166.8 49.7 all-gather.8
  226.2 111.8 reduce-scatter.2
  342.0 113.3 reduce-scatter.4

commit v3 on v2

--- a/solution.py
+++ b/solution.py
@@ -718,16 +718,30 @@
     )
 
 
-def proj_grad(meta, hid, d_qkv):
+def proj_grad(meta, hid, d_qkv, dp_count):
     seqs, length, width = hid.shape
     part = d_qkv.shape[2] * d_qkv.shape[3]
     d_qkv = d_qkv.reshape(seqs, 3, part, length)
-
-    def body(m, h_ref, d_ref, grad):
+    per = width // dp_count
+    parity_at = 1 + 3 * seqs
+
+    def body(m, h_ref, d_ref, keep, send):
         total = contract(d_ref[0, 0], h_ref[0], 1, 0)
         for s in range(1, seqs):
             total += contract(d_ref[s, 0], h_ref[s], 1, 0)
-        grad[0] = total.astype(BF).T
+        grad = total.astype(BF).T.reshape(dp_count // 2, 2, per, part)
+        even = grad[:, 0].reshape(width // 2, part)
+        odd = grad[:, 1].reshape(width // 2, part)
+
+        @pl.when(m[parity_at] == 0)
+        def _():
+            keep[0] = even
+            send[0] = odd
+
+        @pl.when(m[parity_at] != 0)
+        def _():
+            keep[0] = odd
+            send[0] = even
 
     return call(
         body,
@@ -738,11 +752,11 @@
             pl.BlockSpec((seqs, length, width), lambda c, m: (0, 0, 0), pipeline_mode=HOLD),
             pl.BlockSpec((seqs, 1, part, length), lambda c, m: (0, c, 0, 0)),
         ],
-        [pl.BlockSpec((1, width, part), lambda c, m: (c, 0, 0))],
-        [shape((3, width, part))],
+        [pl.BlockSpec((1, width // 2, part), lambda c, m: (c, 0, 0))] * 2,
+        [shape((3, width // 2, part))] * 2,
         6 * seqs * length * width * part,
         weight=0.02,
-    )[0]
+    )
 
 
 def input_back(meta, tokf, branch, own_d, oth_d, own_w, oth_w, gain, items, stay, s, prev):
@@ -797,24 +811,32 @@
     )
 
 
-def place(meta, base, came, first, seqs):
-    count, rows, width = came.shape
-    at = 1 + 2 * seqs + first
-
-    def body(m, src, _, out):
-        out[...] = src[...]
+def place(meta, bases, came):
+    seqs, at = len(came[0]), 1 + 2 * len(came[0])
+    _, rows, width = bases[0].shape
+    flat = [moved for group in came for moved in group]
+
+    def body(m, *refs):
+        outs = refs[len(flat) + len(bases) :]
+        for s in range(seqs):
+
+            @pl.when(pl.program_id(0) == s)
+            def _():
+                for g in range(len(bases)):
+                    outs[g][...] = refs[g * seqs + s][...]
 
     return call(
         body,
         meta,
-        [came, base],
-        (count,),
-        [pl.BlockSpec((1, rows, width), lambda s, m: (s, 0, 0)), ANY],
-        [pl.BlockSpec((1, rows, width), lambda s, m: (m[at + s], 0, 0))],
-        [shape(base.shape)],
+        flat + list(bases),
+        (seqs,),
+        [pl.BlockSpec((1, rows, width), lambda s, m: (0, 0, 0), pipeline_mode=HOLD)] * len(flat)
+        + [ANY] * len(bases),
+        [pl.BlockSpec((1, rows, width), lambda s, m: (m[at + s], 0, 0))] * len(bases),
+        [shape(b.shape) for b in bases],
         1,
-        aliases={2: 0},
-    )[0]
+        aliases={1 + len(flat) + i: i for i in range(len(bases))},
+    )
 
 
 def after(value, *earlier):
@@ -859,7 +881,7 @@
         return jnp.sum(jnp.where(hit, values[None, :], 0), axis=1)
 
     own, oth = chosen(x, at), chosen(1 - x, at)
-    meta = jnp.concatenate([x[None], own, chosen(x, lens), oth]).astype(jnp.int32)
+    meta = jnp.concatenate([x[None], own, chosen(x, lens), oth, dp[None] % 2]).astype(jnp.int32)
 
     def swap(value):
         return lax.ppermute(value, "mp", [(0, 1), (1, 0)])
@@ -932,6 +954,11 @@
 
     def tree(value):
         step = 1
+        if not hasattr(value, "reshape"):
+            keep, send = value
+            came = lax.ppermute(send, "dp", [(i, i ^ 1) for i in range(dp_count)])
+            value = tree_add((keep, came), (yield keep))
+            step = 2
         while step * 4 < dp_count:
             pair = tree_send(value, step)
             value = tree_add(pair, (yield value))
@@ -997,18 +1024,18 @@
     for s in range(seqs):
         d_oth = attention_back(order, qkv_far, mix_oth[0], d_mix_oth, mix_oth[1], s, d_oth)
         order = after(meta, out_job.go(d_oth[0]))
-    grad_oth = proj_grad(order, hid_a, d_oth[0])
+    grad_oth = proj_grad(order, hid_a, d_oth[0], dp_count)
     oth_job = Job(grad_oth)
-    order = after(meta, grad_oth, ffn_own)
+    order = after(meta, grad_oth[0], ffn_own)
     for s in range(seqs):
-        out_came.append(swap(after(out_away[s : s + 1], d_own[0] if s else grad_oth)))
+        out_came.append(swap(after(out_away[s : s + 1], d_own[0] if s else grad_oth[0])))
         d_own = attention_back(order, qkv_own, mix_own[0], d_mix_own, mix_own[1], s, d_own)
         order = after(meta, oth_job.go(d_own[0]), out_came[s])
         if s == seqs - 1:
             order = after(order, out_job.go(d_own[0]))
-    grad_own = proj_grad(order, hid_a, d_own[0])
+    grad_own = proj_grad(order, hid_a, d_own[0], dp_count)
     own_job = Job(grad_own)
-    order = after(meta, grad_own, ffn_oth)
+    order = after(meta, grad_own[0])
     in_away, in_stay, sum_a = [], (), []
 
     def last_back(order, s, stay, prev):
@@ -1021,6 +1048,8 @@
         in_away.append(swap(rows_out))
         sum_a.append(vec)
         order = after(meta, rows_out, own_job.go(rows_out) if s == 0 else oth_job.go(rows_out))
+        if s == 0:
+            order = after(order, ffn_oth)
     out_red, qkv_red_oth = out_job.value, oth_job.value
     far_grads = swap(
         jnp.concatenate([ffn_oth[0], ffn_oth[1], out_red[1]] + [qkv_red_oth[c] for c in range(3)], 1)
@@ -1031,10 +1060,7 @@
         sum_a[s] += vec
         order = after(meta, own_job.go(rows_out) if s == 0 else rows_out)
     sum_a = jnp.concatenate(sum_a, 0)
-    output, input_grad = out_stay, in_stay[0]
-    for s in range(seqs):
-        output = place(order, output, out_came[s], s, seqs)
-        input_grad = place(order, input_grad, in_away[s], s, seqs)
+    output, input_grad = place(order, [out_stay, in_stay[0]], [out_came, in_away])
 
     sums = jnp.stack([sum_a, sum_b], 0)[:, :, 0]
     d_pair = sums * norm_gains[:, None, :]
@@ -1101,7 +1127,7 @@
         P(None, ("dp", "mp")),
     )
     dp_count = mesh.shape["dp"]
-    paired = mesh.shape["mp"] == 2 and dp_count & (dp_count - 1) == 0
+    paired = mesh.shape["mp"] == 2 and dp_count & (dp_count - 1) == 0 and dp_count > 4
     return jax.shard_map(
         per_device_pair if paired else per_device, mesh=mesh, in_specs=in_specs, out_specs=out_specs, check_vma=False
     )

time: 569 us -> 557 us (0.979)
  starting transfers between devices: 59.6 us -> 48.7 us
  waiting for transfers between devices: 36.5 us -> 44.6 us
  Pallas kernels: 387 us -> 381 us
    ppermute x10, starting transfers between devices: 24.4 us -> 11.6 us  [swap(): return lax.ppermute(value, 'mp', [(0, 1), (1, 0)])]
    ppermute x6 -> x4, starting transfers between devices: 12.6 us -> 5.75 us  [tree_send(): lax.ppermute(send, 'dp', [(i, i ^ step) for i in range(dp_count)])]
    pallas_call x26 -> x23, Pallas kernels: 387 us -> 381 us  [call(): pl.pallas_call(body, grid_spec=pltpu.PrefetchScalarGridSpec(num_scalar_pr...]
    ppermute x0 -> x2, starting transfers between devices: none -> 6.32 us  [tree(): came = lax.ppermute(send, 'dp', [(i, i ^ 1) for i in range(dp_count)])]
where the time goes in v3:
time: 557 us; the launch traced here: 550 us
  Pallas kernels  381 us (68%)
  starting transfers between devices  48.7 us (9%)
  waiting for transfers between devices  44.6 us (8%)
  local copies, waits for them, and re-layouts  31.6 us (6%)
  other arithmetic  23.6 us (4%)
  between operations  18.7 us (3%)
    pallas_call x23, Pallas kernels, call(): pl.pallas_call(body, grid_spec=pltpu.PrefetchScalarGridSpec(num_scalar_pr...  381 us
    ppermute x10, waiting for transfers between devices, swap(): return lax.ppermute(value, 'mp', [(0, 1), (1, 0)])  29.3 us
    ppermute x9, starting transfers between devices, tree(): lax.ppermute(piece(k), 'dp', [(i, i ^ k * step) for i in range(dp_count)])  19.5 us
    ppermute x10, starting transfers between devices, swap(): return lax.ppermute(value, 'mp', [(0, 1), (1, 0)])  11.6 us
  transfers between devices with their start and end apart: 32, of which 8 were waited for; matrix products, arithmetic and copies ran while one was open for 8% of the time, Pallas kernels for 69%

profile of v3, /device:TPU:0, one launch (start us, length us, event | category | flops | bytes accessed | tf_op | source)
XLA Modules:
  0.0 549.9 jit_solution(17354386189543992103)
XLA Ops:
  14.4 2.8 dynamic-slice_bitcast_fusion.3
  17.3 2.9 collective-permute-start.2
  20.2 4.9 collective-permute-done.2
  25.9 1.8 collective-permute-start
  33.9 16.7 %collective-permute-done.rec = bf16[1,512,1024]{2,1,0:T(8,128)(2,1)} collective-permute-done((bf16[1,512,1024]{2,1,0:T(8,128)(2,1)}, bf16[1,512,1024]{2,1,0:T(8,128)(2,1)}, u32[]{:S(2)}, u32[]{:S(2)}) %collective-permute-start) | collective-permute-done | bytes 1048608 | tf_op jit(solution)/shard_map/ppermute | solution.py:887
  50.6 1.4 collective-permute-start.3
  52.6 9.3 %shard_map.161 = (bf16[2,1024,1024]{2,1,0:T(8,128)(2,1)}, bf16[2,1024,1024]{2,1,0:T(8,128)(2,1)}, bf16[2,3,512,1024]{3,2,1,0:T(8,128)(2,1)}) custom-call(s32[8]{0:T(128)} %concatenate.22.m, bf16[4,512,1024]{2,1,0:T(8,128)(2,1)} %bitcast.246, bf16[1,512,1024]{2,1,0:T(8,128)(2,1)} %collective-permute-done.rec, f32[2,1,1024]{2,1,0:T(1,128)} %get-tuple-element.248.g, ...), custom_call_target="tpu_custom_call" | custom-call | flops 2576980480 | bytes 230768 | tf_op jit(solution)/shard_map/pallas_call | solution.py:252
  62.0 2.5 collective-permute-done.3
  64.5 1.5 slice.109
  66.1 1.8 fusion.38
  69.2 1.2 collective-permute-start.1
  70.4 1.8 dynamic-slice_bitcast_fusion.2
  72.2 1.5 pad_maximum_fusion
  73.7 13.5 %shard_map.163 = (bf16[2,8,64,1024]{3,2,1,0:T(8,128)(2,1)}, f32[2,8,1,1024]{3,2,1,0:T(1,128)}) custom-call(s32[8]{0:T(128)} %concatenate.22.m, bf16[2,3,8,64,1024]{4,3,2,1,0:T(8,128)(2,1)} %bitcast.209, bf16[2,3,8,64,1024]{4,3,2,1,0:T(8,128)(2,1)} %bitcast.210, bf16[2,3,8,64,1024]{4,3,2,1,0:T(8,128)(2,1)} %bitcast.211), custom_call_target="tpu_custom_call" | custom-call | flops 4294967296 | bytes 210370 | tf_op jit(solution)/shard_map/pallas_call | solution.py:252
  87.2 5.2 collective-permute-done.1.rec
  92.4 1.1 collective-permute-start.4
  93.5 7.8 %shard_map.165.refs_0_ = bf16[2,3,512,1024]{3,2,1,0:T(8,128)(2,1)} custom-call(s32[8]{0:T(128)} %concatenate.22.m, bf16[2,1024,1024]{2,1,0:T(8,128)(2,1)} %get-tuple-element.92.refs_1_.h_ref, bf16[3,1024,512]{2,1,0:T(8,128)(2,1)} %bitcast.231), custom_call_target="tpu_custom_call" | custom-call | flops 2576980480 | bytes 136314 | tf_op jit(solution)/shard_map/pallas_call | solution.py:252
  101.3 9.5 %shard_map.162 = (bf16[2,1024,1024]{2,1,0:T(8,128)(2,1)}, bf16[2,1024,1024]{2,1,0:T(8,128)(2,1)}, bf16[2,3,512,1024]{3,2,1,0:T(8,128)(2,1)}) custom-call(s32[8]{0:T(128)} %concatenate.22.m, bf16[4,512,1024]{2,1,0:T(8,128)(2,1)} %bitcast.247, ...), custom_call_target="tpu_custom_call", output_to_operand_aliasing={{0}: (5, {}), {1}: (6, {}), {2}: (7, {})} | custom-call | flops 2576980480 | bytes 377569 | tf_op jit(solution)/shard_map/pallas_call | solution.py:252
  110.8 13.5 %shard_map.167 = (bf16[2,8,64,1024]{3,2,1,0:T(8,128)(2,1)}, f32[2,8,1,1024]{3,2,1,0:T(1,128)}) custom-call(s32[8]{0:T(128)} %concatenate.22.m, bf16[2,3,8,64,1024]{4,3,2,1,0:T(8,128)(2,1)} %bitcast.197, bf16[2,3,8,64,1024]{4,3,2,1,0:T(8,128)(2,1)} %bitcast.198, bf16[2,3,8,64,1024]{4,3,2,1,0:T(8,128)(2,1)} %bitcast.199), custom_call_target="tpu_custom_call" | custom-call | flops 4294967296 | bytes 210370 | tf_op jit(solution)/shard_map/pallas_call | solution.py:252
  124.3 8.0 %shard_map.166 = bf16[2,3,512,1024]{3,2,1,0:T(8,128)(2,1)} custom-call(s32[8]{0:T(128)} %concatenate.22.m, bf16[2,1024,1024]{2,1,0:T(8,128)(2,1)} %get-tuple-element.98.h_ref, bf16[3,1024,512]{2,1,0:T(8,128)(2,1)} %bitcast.232, bf16[2,3,512,1024]{3,2,1,0:T(8,128)(2,1)} %shard_map.165.refs_0_), custom_call_target="tpu_custom_call", output_to_operand_aliasing={{}: (3, {})} | custom-call | flops 2576980480 | bytes 199229 | tf_op jit(solution)/shard_map/pallas_call | solution.py:252
  132.2 9.0 %shard_map.164 = (bf16[2,8,64,1024]{3,2,1,0:T(8,128)(2,1)}, f32[2,8,1,1024]{3,2,1,0:T(1,128)}) custom-call(s32[8]{0:T(128)} %concatenate.22.m, bf16[2,3,8,64,1024]{4,3,2,1,0:T(8,128)(2,1)} %bitcast.212, bf16[2,3,8,64,1024]{4,3,2,1,0:T(8,128)(2,1)} %bitcast.213, bf16[2,3,8,64,1024]{4,3,2,1,0:T(8,128)(2,1)} %bitcast.214, ...), custom_call_target="tpu_custom_call", output_to_operand_aliasing={{0}: (4, {}), {1}: (5, {})} | custom-call | flops 4294967296 | bytes 231997 | tf_op jit(solution)/shard_map/pallas_call | solution.py:252
  141.2 9.0 %shard_map.168 = (bf16[2,8,64,1024]{3,2,1,0:T(8,128)(2,1)}, f32[2,8,1,1024]{3,2,1,0:T(1,128)}) custom-call(s32[8]{0:T(128)} %concatenate.22.m, bf16[2,3,8,64,1024]{4,3,2,1,0:T(8,128)(2,1)} %bitcast.200, bf16[2,3,8,64,1024]{4,3,2,1,0:T(8,128)(2,1)} %bitcast.201, bf16[2,3,8,64,1024]{4,3,2,1,0:T(8,128)(2,1)} %bitcast.202, ...), custom_call_target="tpu_custom_call", output_to_operand_aliasing={{0}: (4, {}), {1}: (5, {})} | custom-call | flops 4294967296 | bytes 231997 | tf_op jit(solution)/shard_map/pallas_call | solution.py:252
  150.3 11.4 %shard_map.169 = (bf16[2,1024,1024]{2,1,0:T(8,128)(2,1)}, bf16[2,1024,1024]{2,1,0:T(8,128)(2,1)}) custom-call(s32[8]{0:T(128)} %concatenate.22.m, bf16[2,512,1024]{2,1,0:T(8,128)(2,1)} %bitcast.238, bf16[2,512,1024]{2,1,0:T(8,128)(2,1)} %bitcast.240, bf16[2,1024,1024]{2,1,0:T(8,128)(2,1)} %get-tuple-element.105.t.tok, bf16[512,1024]{1,0:T(8,128)(2,1)} %wa.7, ...), custom_call_target="tpu_custom_call" | custom-call | flops 2147483648 | bytes 188825 | tf_op jit(solution)/shard_map/pallas_call | solution.py:252
  161.7 64.3 %shard_map.170 = (bf16[2048,1024]{1,0:T(8,128)(2,1)}, bf16[2048,1024]{1,0:T(8,128)(2,1)}, bf16[2,1024,2048]{2,1,0:T(8,128)(2,1)}) custom-call(s32[8]{0:T(128)} %concatenate.22.m, bf16[2048,1024]{1,0:T(8,128)(2,1)} %bitcast.275, bf16[4,512,1024]{2,1,0:T(8,128)(2,1)} %bitcast.243, bf16[2,512,1024]{2,1,0:T(8,128)(2,1)} %collective-permute-done.4.came.cr, ...), custom_call_target="tpu_custom_call" | custom-call | flops 20615843840 | bytes 356515 | tf_op jit(solution)/shard_map/pallas_call | solution.py:252
  226.1 64.6 %shard_map.171 = (bf16[2048,1024]{1,0:T(8,128)(2,1)}, bf16[2048,1024]{1,0:T(8,128)(2,1)}, bf16[2,1024,2048]{2,1,0:T(8,128)(2,1)}) custom-call(s32[8]{0:T(128)} %concatenate.22.m, bf16[2048,1024]{1,0:T(8,128)(2,1)} %bitcast.276, bf16[4,512,1024]{2,1,0:T(8,128)(2,1)} %bitcast.244, bf16[2,512,1024]{2,1,0:T(8,128)(2,1)} %collective-permute-done.4.came.cr, ...), custom_call_target="tpu_custom_call" | custom-call | flops 20615843840 | bytes 356515 | tf_op jit(solution)/shard_map/pallas_call | solution.py:252
  290.7 28.2 %shard_map.172 = (bf16[4,512,1024]{2,1,0:T(8,128)(2,1)}, bf16[2,512,1024]{2,1,0:T(8,128)(2,1)}, bf16[2,1024,1024]{2,1,0:T(8,128)(2,1)}, bf16[2,512,1024]{2,1,0:T...) custom-call(s32[8]{0:T(128)} %concatenate.22.m, ...), custom_call_target="tpu_custom_call" | custom-call | flops 8589934592 | bytes 503480 | tf_op jit(solution)/shard_map/pallas_call | solution.py:252
  318.9 1.3 dynamic-slice_bitcast_fusion
  320.4 19.1 %shard_map.173.refs_0_ = bf16[2,3,8,64,1024]{4,3,2,1,0:T(8,128)(2,1)} custom-call(s32[8]{0:T(128)} %concatenate.22.m, bf16[2,3,8,64,1024]{4,3,2,1,0:T(8,128)(2,1)} %bitcast.203, bf16[2,3,8,64,1024]{4,3,2,1,0:T(8,128)(2,1)} %bitcast.204, bf16[2,3,8,64,1024]{4,3,2,1,0:T(8,128)(2,1)} %bitcast.205, bf16[2,8,64,1024]{3,2,1,0:T(8,128)(2,1)} %get-tuple-element.104.o, ...), custom_call_target="tpu_custom_call" | custom-call | flops 429496736 | bytes 294256 | tf_op jit(solution)/shard_map/pallas_call | solution.py:252
  339.4 1.9 fusion
  341.5 1.5 collective-permute-start.6
  342.9 12.2 %shard_map.174 = bf16[2,3,8,64,1024]{4,3,2,1,0:T(8,128)(2,1)} custom-call(s32[8]{0:T(128)} %concatenate.22.m, bf16[2,3,8,64,1024]{4,3,2,1,0:T(8,128)(2,1)} %bitcast.206, bf16[2,3,8,64,1024]{4,3,2,1,0:T(8,128)(2,1)} %bitcast.207, bf16[2,3,8,64,1024]{4,3,2,1,0:T(8,128)(2,1)} %bitcast.208, ...), custom_call_target="tpu_custom_call", output_to_operand_aliasing={{}: (7, {})} | custom-call | flops 429496736 | bytes 357171 | tf_op jit(solution)/shard_map/pallas_call | solution.py:252
  355.3 12.5 %shard_map.175 = (bf16[3,512,512]{2,1,0:T(8,128)(2,1)}, bf16[3,512,512]{2,1,0:T(8,128)(2,1)}) custom-call(s32[8]{0:T(128)} %concatenate.22.m, bf16[2,1024,1024]{2,1,0:T(8,128)(2,1)} %get-tuple-element.98.h_ref, bf16[2,3,512,1024]{3,2,1,0:T(8,128)(2,1)} %bitcast.226), custom_call_target="tpu_custom_call" | custom-call | flops 128849016 | bytes 136314 | tf_op jit(solution)/shard_map/pallas_call | solution.py:252
  367.8 4.9 collective-permute-start.7
  372.7 3.1 fusion.37
  375.8 19.3 %shard_map.176.refs_0_ = bf16[2,3,8,64,1024]{4,3,2,1,0:T(8,128)(2,1)} custom-call(s32[8]{0:T(128)} %concatenate.22.m, bf16[2,3,8,64,1024]{4,3,2,1,0:T(8,128)(2,1)} %bitcast.215, bf16[2,3,8,64,1024]{4,3,2,1,0:T(8,128)(2,1)} %bitcast.216, bf16[2,3,8,64,1024]{4,3,2,1,0:T(8,128)(2,1)} %bitcast.217, bf16[2,8,64,1024]{3,2,1,0:T(8,128)(2,1)} %get-tuple-element.97.o, ...), custom_call_target="tpu_custom_call" | custom-call | flops 429496736 | bytes 294256 | tf_op jit(solution)/shard_map/pallas_call | solution.py:252
  395.1 2.3 add_convert_fusion.1
  399.4 11.0 %collective-permute-start.12 = (bf16[2,64,512]{2,1,0:T(8,128)(2,1)S(1)}, bf16[2,64,512]{2,1,0:T(8,128)(2,1)S(1)}, u32[]{:S(2)}, u32[]{:S(2)}) collective-permute-start(bf16[2,64,512]{2,1,0:T(8,128)(2,1)S(1)} %get-tuple-element.246), channel_id=1, source_target_pairs={{0,16},{2,18},{4,20},{6,22},{8,24},{10,26},{12,28},{14,30},{16,0},... | collective-permute-start | bytes 393224 | tf_op jit(solution)/shard_map/ppermute | solution.py:975
  410.8 12.0 %shard_map.177 = bf16[2,3,8,64,1024]{4,3,2,1,0:T(8,128)(2,1)} custom-call(s32[8]{0:T(128)} %concatenate.22.m, bf16[2,3,8,64,1024]{4,3,2,1,0:T(8,128)(2,1)} %bitcast.218, bf16[2,3,8,64,1024]{4,3,2,1,0:T(8,128)(2,1)} %bitcast.219, bf16[2,3,8,64,1024]{4,3,2,1,0:T(8,128)(2,1)} %bitcast.220, ...), custom_call_target="tpu_custom_call", output_to_operand_aliasing={{}: (7, {})} | custom-call | flops 429496736 | bytes 357171 | tf_op jit(solution)/shard_map/pallas_call | solution.py:252
  423.9 2.8 collective-permute-done.8
  426.7 1.4 fusion.2
  428.1 12.3 %shard_map.178 = (bf16[3,512,512]{2,1,0:T(8,128)(2,1)}, bf16[3,512,512]{2,1,0:T(8,128)(2,1)}) custom-call(s32[8]{0:T(128)} %concatenate.22.m, bf16[2,1024,1024]{2,1,0:T(8,128)(2,1)} %get-tuple-element.98.h_ref, bf16[2,3,512,1024]{3,2,1,0:T(8,128)(2,1)} %bitcast.221), custom_call_target="tpu_custom_call" | custom-call | flops 128849016 | bytes 136314 | tf_op jit(solution)/shard_map/pallas_call | solution.py:252
  440.4 1.4 collective-permute-start.14
  443.0 2.8 collective-permute-start.18
  446.5 10.1 %shard_map.179 = (bf16[1,512,1024]{2,1,0:T(8,128)(2,1)}, f32[1,1,1024]{2,1,0:T(1,128)}) custom-call(s32[8]{0:T(128)} %concatenate.22.m, bf16[2,1024,1024]{2,1,0:T(8,128)(2,1)} %get-tuple-element.105.t.tok, bf16[2,1024,1024]{2,1,0:T(8,128)(2,1)} %get-tuple-element.142.br, bf16[2,3,512,1024]{3,2,1,0:T(8,128)(2,1)} %bitcast.222, ...), custom_call_target="tpu_custom_call" | custom-call | flops 64424508 | bytes 283238 | tf_op jit(solution)/shard_map/pallas_call | solution.py:252
  457.6 2.3 add_convert_fusion
  461.0 3.8 collective-permute-start.15
  464.8 10.1 %shard_map.180 = (bf16[1,512,1024]{2,1,0:T(8,128)(2,1)}, f32[1,1,1024]{2,1,0:T(1,128)}) custom-call(s32[8]{0:T(128)} %concatenate.22.m, bf16[2,1024,1024]{2,1,0:T(8,128)(2,1)} %get-tuple-element.105.t.tok, bf16[2,1024,1024]{2,1,0:T(8,128)(2,1)} %get-tuple-element.142.br, bf16[2,3,512,1024]{3,2,1,0:T(8,128)(2,1)} %bitcast.223, ...), custom_call_target="tpu_custom_call" | custom-call | flops 64424508 | bytes 283238 | tf_op jit(solution)/shard_map/pallas_call | solution.py:252
  474.9 1.1 fusion.10
  476.1 1.7 fusion.12
  477.7 1.7 fusion.11
  482.1 2.0 collective-permute-start.24
  484.0 10.0 %shard_map.181 = (bf16[4,512,1024]{2,1,0:T(8,128)(2,1)}, f32[1,1,1024]{2,1,0:T(1,128)}) custom-call(s32[8]{0:T(128)} %concatenate.22.m, bf16[2,1024,1024]{2,1,0:T(8,128)(2,1)} %get-tuple-element.105.t.tok, bf16[2,1024,1024]{2,1,0:T(8,128)(2,1)} %get-tuple-element.142.br, bf16[2,3,512,1024]{3,2,1,0:T(8,128)(2,1)} %bitcast.224, ...), custom_call_target="tpu_custom_call" | custom-call | flops 64424508 | bytes 314695 | tf_op jit(solution)/shard_map/pallas_call | solution.py:252
  494.8 1.4 fusion.1
  496.1 10.2 %shard_map.182 = (bf16[4,512,1024]{2,1,0:T(8,128)(2,1)}, f32[1,1,1024]{2,1,0:T(1,128)}) custom-call(s32[8]{0:T(128)} %concatenate.22.m, bf16[2,1024,1024]{2,1,0:T(8,128)(2,1)} %get-tuple-element.105.t.tok, bf16[2,1024,1024]{2,1,0:T(8,128)(2,1)} %get-tuple-element.142.br, bf16[2,3,512,1024]{3,2,1,0:T(8,128)(2,1)} %bitcast.225, ...), custom_call_target="tpu_custom_call", output_to_operand_aliasing={{0}: (8, {})} | custom-call | flops 64424508 | bytes 356638 | tf_op jit(solution)/shard_map/pallas_call | solution.py:252
  508.3 4.8 all-to-all-start
  513.9 1.8 collective-permute-start.21
  515.7 2.4 collective-permute-start.23
  518.1 5.0 shard_map.183
  523.1 1.5 all-to-all-done
  525.5 2.9 collective-permute-done.23
  528.5 7.8 %collective-permute-done.22 = bf16[3,64,512]{2,1,0:T(8,128)(2,1)} collective-permute-done((bf16[3,64,512]{2,1,0:T(8,128)(2,1)}, bf16[3,64,512]{2,1,0:T(8,128)(2,1)}, u32[]{:S(2)}, u32[]{:S(2)}) %collective-permute-start.22) | collective-permute-done | bytes 196640 | tf_op jit(solution)/shard_map/ppermute | solution.py:975
  537.2 1.1 fusion.7
  538.3 1.7 fusion.19
  540.7 2.1 fusion.4
  (141 shorter events, 28.9 us)
Async XLA Ops:
  7.2 86.3 %all-gather.5.cloned.1.call-start = ((), (), s32[]{:S(2)}) async-start(), calls=%async_computation.3 | async-start | bytes 3342336 | tf_op jit(solution)/shard_map/all_gather | solution.py:894
  14.4 14.0 %copy-start = (f32[256,2048]{1,0:T(8,128)S(1)}, f32[256,2048]{1,0:T(8,128)}, u32[]{:S(2)}) copy-start(f32[256,2048]{1,0:T(8,128)} %param.14) | copy-start | bytes 6291460
  17.3 7.8 %collective-permute-start.2 = (bf16[192,512]{1,0:T(8,128)(2,1)S(1)}, bf16[192,512]{1,0:T(8,128)(2,1)S(1)}, u32[]{:S(2)}, u32[]{:S(2)}) collective-permute-start(bf16[192,512]{1,0:T(8,128)(2,1)S(1)} %constant_dynamic-slice_fusion.9), channel_id=1, source_target_pairs={{0,1},{1,0},{2,3},{3,2},{4,5},{5,4},{6,7},{7,6},{8,9},{9,8},{10,11... | collective-permute-start | bytes 589832 | tf_op jit(solution)/shard_map/ppermute | solution.py:887
  25.1 0.7 copy-start.2
  25.8 124.4 %all-gather.7.cloned.1.call-start = ((), (), s32[]{:S(2)}) async-start(), calls=%async_computation.4 | async-start | bytes 1114112 | tf_op jit(solution)/shard_map/all_gather | solution.py:894
  25.9 24.7 %collective-permute-start = (bf16[1,512,1024]{2,1,0:T(8,128)(2,1)}, bf16[1,512,1024]{2,1,0:T(8,128)(2,1)}, u32[]{:S(2)}, u32[]{:S(2)}) collective-permute-start(bf16[1,512,1024]{2,1,0:T(8,128)(2,1)} %get-tuple-element.220), channel_id=1, source_target_pairs={{0,1},{1,0},{2,3},{3,2},{4,5},{5,4},{6,7},{7,6},{8,9},{9,8},{10,11... | collective-permute-start | bytes 3145736 | tf_op jit(solution)/shard_map/ppermute | solution.py:887
  27.8 0.5 copy-start.8
  27.8 0.6 copy-start.10
  28.4 23.6 %copy-start.5 = (f32[2,1024]{1,0:T(2,128)S(1)}, f32[2,1024]{1,0:T(2,128)}, u32[]{:S(2)}) copy-start(f32[2,1024]{1,0:T(2,128)} %param.13) | copy-start | bytes 24580
  29.5 32.5 %copy-start.3 = (f32[2,2048]{1,0:T(2,128)}, f32[2,2048]{1,0:T(2,128)S(1)}, u32[]{:S(2)}) copy-start(f32[2,2048]{1,0:T(2,128)S(1)} %convolution_add_fusion) | copy-start | bytes 49156
  50.6 13.9 %collective-permute-start.3 = (bf16[288,1024]{1,0:T(8,128)(2,1)}, bf16[288,1024]{1,0:T(8,128)(2,1)}, u32[]{:S(2)}, u32[]{:S(2)}) collective-permute-start(bf16[288,1024]{1,0:T(8,128)(2,1)} %pad_maximum_fusion.1), channel_id=1, source_target_pairs={{0,1},{1,0},{2,3},{3,2},{4,5},{5,4},{6,7},{7,6},{8,9},{9,8},{10,11... | collective-permute-start | bytes 1769480 | tf_op jit(solution)/shard_map/ppermute | solution.py:887
  66.0 160.0 %all-gather.11.cloned.1.call-start = ((), (), s32[]{:S(2)}) async-start(), calls=%async_computation.6 | async-start | bytes 4456448 | tf_op jit(solution)/shard_map/all_gather | solution.py:894
  67.8 158.2 %all-gather.9.cloned.1.call-start = ((), (), s32[]{:S(2)}) async-start(), calls=%async_computation.5 | async-start | bytes 4456448 | tf_op jit(solution)/shard_map/all_gather | solution.py:894
  68.7 307.1 %reduce-scatter.3.cloned.1.call-start = ((), (), s32[]{:S(2)}) async-start(), calls=%async_computation.7 | async-start | bytes 8912896 | tf_op jit(solution)/shard_map/reduce_scatter | solution.py:985
  69.2 23.2 %collective-permute-start.1 = (bf16[1,512,1024]{2,1,0:T(8,128)(2,1)S(1)}, bf16[1,512,1024]{2,1,0:T(8,128)(2,1)}, u32[]{:S(2)}, u32[]{:S(2)}) collective-permute-start(bf16[1,512,1024]{2,1,0:T(8,128)(2,1)S(1)} %get-tuple-element.90), channel_id=1, source_target_pairs={{0,1},{1,0},{2,3},{3,2},{4,5},{5,4},{6,7},{7,6},{8,9},{9,8},{10,11... | collective-permute-start | bytes 3145736 | tf_op jit(solution)/shard_map/ppermute | solution.py:887
  92.4 69.3 %collective-permute-start.4 = (bf16[2,512,1024]{2,1,0:T(8,128)(2,1)}, bf16[2,512,1024]{2,1,0:T(8,128)(2,1)}, u32[]{:S(2)}, u32[]{:S(2)}) collective-permute-start(bf16[2,512,1024]{2,1,0:T(8,128)(2,1)} %pad_maximum_fusion), channel_id=1, source_target_pairs={{0,1},{1,0},{2,3},{3,2},{4,5},{5,4},{6,7},{7,6},{8,9},{9,8},{10,11... | collective-permute-start | bytes 6291464 | tf_op jit(solution)/shard_map/ppermute | solution.py:887
  226.0 238.8 %reduce-scatter.5.cloned.1.call-start = ((), (), s32[]{:S(2)}) async-start(), calls=%async_computation.8 | async-start | bytes 8912896 | tf_op jit(solution)/shard_map/reduce_scatter | solution.py:985
  320.3 19.2 %collective-permute-start.5 = (bf16[2,8,1,64,512]{4,3,1,0,2:T(8,128)(2,1)S(1)}, bf16[2,8,1,64,512]{4,3,1,0,2:T(8,128)(2,1)}, u32[]{:S(2)}, u32[]{:S(2)}) collective-permute-start(bf16[2,8,1,64,512]{4,3,1,0,2:T(8,128)(2,1)S(1)} %dynamic-slice_bitcast_fusion), channel_id=1, source_target_pairs={{0,2},{2,0},{4,6},{6,4},{8,10},{10,8},{12,14},{14,12},{16,18},{18,... | collective-permute-start | bytes 3145736 | tf_op jit(solution)/shard_map/ppermute | solution.py:949
  341.5 13.7 %collective-permute-start.6 = (bf16[2,4,1,64,512]{4,3,0,2,1:T(8,128)(2,1)S(1)}, bf16[2,4,1,64,512]{4,3,0,2,1:T(8,128)(2,1)S(1)}, u32[]{:S(2)}, u32[]{:S(2)}) collective-permute-start(bf16[2,4,1,64,512]{4,3,0,2,1:T(8,128)(2,1)S(1)} %bitcast.262), channel_id=1, source_target_pairs={{0,4},{2,6},{4,0},{6,2},{8,12},{10,14},{12,8},{14,10},{16,20},{18,... | collective-permute-start | bytes 1572872 | tf_op jit(solution)/shard_map/ppermute | solution.py:949
  367.8 27.3 %collective-permute-start.7 = (bf16[3,512,512]{2,1,0:T(8,128)(2,1)}, bf16[3,512,512]{2,1,0:T(8,128)(2,1)}, u32[]{:S(2)}, u32[]{:S(2)}) collective-permute-start(bf16[3,512,512]{2,1,0:T(8,128)(2,1)} %get-tuple-element.124), channel_id=1, source_target_pairs={{0,2},{2,0},{4,6},{6,4},{8,10},{10,8},{12,14},{14,12},{16,18},{18,... | collective-permute-start | bytes 4718600 | tf_op jit(solution)/shard_map/ppermute | solution.py:959
  375.8 34.6 %collective-permute-start.9 = (bf16[1,512,1024]{2,1,0:T(8,128)(2,1)}, bf16[1,512,1024]{2,1,0:T(8,128)(2,1)}, u32[]{:S(2)}, u32[]{:S(2)}) collective-permute-start(bf16[1,512,1024]{2,1,0:T(8,128)(2,1)} %get-tuple-element.130), channel_id=1, source_target_pairs={{0,1},{1,0},{2,3},{3,2},{4,5},{5,4},{6,7},{7,6},{8,9},{9,8},{10,11... | collective-permute-start | bytes 3145736 | tf_op jit(solution)/shard_map/ppermute | solution.py:887
  398.5 28.2 %collective-permute-start.8 = (bf16[3,4,1,64,512]{4,3,0,2,1:T(8,128)(2,1)}, bf16[3,4,1,64,512]{4,3,0,2,1:T(8,128)(2,1)}, u32[]{:S(2)}, u32[]{:S(2)}) collective-permute-start(bf16[3,4,1,64,512]{4,3,0,2,1:T(8,128)(2,1)} %bitcast.194), channel_id=1, source_target_pairs={{0,4},{2,6},{4,0},{6,2},{8,12},{10,14},{12,8},{14,10},{16,20},{18,... | collective-permute-start | bytes 2359304 | tf_op jit(solution)/shard_map/ppermute | solution.py:949
  398.9 29.1 %collective-permute-start.10 = (bf16[1,512,1024]{2,1,0:T(8,128)(2,1)}, bf16[1,512,1024]{2,1,0:T(8,128)(2,1)}, u32[]{:S(2)}, u32[]{:S(2)}) collective-permute-start(bf16[1,512,1024]{2,1,0:T(8,128)(2,1)} %get-tuple-element.133), channel_id=1, source_target_pairs={{0,1},{1,0},{2,3},{3,2},{4,5},{5,4},{6,7},{7,6},{8,9},{9,8},{10,11... | collective-permute-start | bytes 3145736 | tf_op jit(solution)/shard_map/ppermute | solution.py:887
  399.0 23.9 %collective-permute-start.13 = (bf16[2,64,512]{2,1,0:T(8,128)(2,1)S(1)}, bf16[2,64,512]{2,1,0:T(8,128)(2,1)S(1)}, u32[]{:S(2)}, u32[]{:S(2)}) collective-permute-start(bf16[2,64,512]{2,1,0:T(8,128)(2,1)S(1)} %get-tuple-element.245), channel_id=1, source_target_pairs={{0,24},{2,26},{4,28},{6,30},{8,16},{10,18},{12,20},{14,22},{16,8},... | collective-permute-start | bytes 393224 | tf_op jit(solution)/shard_map/ppermute | solution.py:975
  399.4 23.5 %collective-permute-start.12 = (bf16[2,64,512]{2,1,0:T(8,128)(2,1)S(1)}, bf16[2,64,512]{2,1,0:T(8,128)(2,1)S(1)}, u32[]{:S(2)}, u32[]{:S(2)}) collective-permute-start(bf16[2,64,512]{2,1,0:T(8,128)(2,1)S(1)} %get-tuple-element.246), channel_id=1, source_target_pairs={{0,16},{2,18},{4,20},{6,22},{8,24},{10,26},{12,28},{14,30},{16,0},... | collective-permute-start | bytes 393224 | tf_op jit(solution)/shard_map/ppermute | solution.py:975
  410.3 12.5 %collective-permute-start.11 = (bf16[2,64,512]{2,1,0:T(8,128)(2,1)S(1)}, bf16[2,64,512]{2,1,0:T(8,128)(2,1)}, u32[]{:S(2)}, u32[]{:S(2)}) collective-permute-start(bf16[2,64,512]{2,1,0:T(8,128)(2,1)S(1)} %get-tuple-element.244), channel_id=1, source_target_pairs={{0,8},{2,10},{4,12},{6,14},{8,0},{10,2},{12,4},{14,6},{16,24},{18,... | collective-permute-start | bytes 393224 | tf_op jit(solution)/shard_map/ppermute | solution.py:975
  428.1 13.8 %copy-start.6 = (f32[2,1024]{1,0:T(2,128)S(1)}, f32[2,1024]{1,0:T(2,128)}, u32[]{:S(2)}) copy-start(f32[2,1024]{1,0:T(2,128)} %param.13) | copy-start | bytes 24580
  428.1 13.8 %copy-start.9 = (f32[2,128]{1,0:T(2,128)S(1)}, f32[2,128]{1,0:T(2,128)}, u32[]{:S(2)}) copy-start(f32[2,128]{1,0:T(2,128)} %copy-done.8) | copy-start | bytes 3076
  428.1 13.8 %copy-start.11 = (f32[2,128]{1,0:T(2,128)S(1)}, f32[2,128]{1,0:T(2,128)}, u32[]{:S(2)}) copy-start(f32[2,128]{1,0:T(2,128)} %copy-done.10) | copy-start | bytes 3076
  428.1 13.9 %copy-start.7 = (f32[2,1,1024]{2,1,0:T(1,128)S(1)}, f32[2,1,1024]{2,1,0:T(1,128)}, u32[]{:S(2)}) copy-start(f32[2,1,1024]{2,1,0:T(1,128)} %get-tuple-element.165) | copy-start | bytes 24580
  440.4 17.2 %collective-permute-start.14 = (bf16[3,512,512]{2,1,0:T(8,128)(2,1)}, bf16[3,512,512]{2,1,0:T(8,128)(2,1)}, u32[]{:S(2)}, u32[]{:S(2)}) collective-permute-start(bf16[3,512,512]{2,1,0:T(8,128)(2,1)} %get-tuple-element.140), channel_id=1, source_target_pairs={{0,2},{2,0},{4,6},{6,4},{8,10},{10,8},{12,14},{14,12},{16,18},{18,... | collective-permute-start | bytes 4718600 | tf_op jit(solution)/shard_map/ppermute | solution.py:959
  443.0 31.9 %collective-permute-start.16 = (bf16[3,64,512]{2,1,0:T(8,128)(2,1)}, bf16[3,64,512]{2,1,0:T(8,128)(2,1)S(1)}, u32[]{:S(2)}, u32[]{:S(2)}) collective-permute-start(bf16[3,64,512]{2,1,0:T(8,128)(2,1)} %get-tuple-element.239), channel_id=1, source_target_pairs={{0,8},{2,10},{4,12},{6,14},{8,0},{10,2},{12,4},{14,6},{16,24},{18,... | collective-permute-start | bytes 589832 | tf_op jit(solution)/shard_map/ppermute | solution.py:975
  443.0 31.8 %collective-permute-start.18 = (bf16[3,64,512]{2,1,0:T(8,128)(2,1)}, bf16[3,64,512]{2,1,0:T(8,128)(2,1)}, u32[]{:S(2)}, u32[]{:S(2)}) collective-permute-start(bf16[3,64,512]{2,1,0:T(8,128)(2,1)} %get-tuple-element.240), channel_id=1, source_target_pairs={{0,24},{2,26},{4,28},{6,30},{8,16},{10,18},{12,20},{14,22},{16,8},... | collective-permute-start | bytes 589832 | tf_op jit(solution)/shard_map/ppermute | solution.py:975
  445.8 29.1 %collective-permute-start.17 = (bf16[3,64,512]{2,1,0:T(8,128)(2,1)}, bf16[3,64,512]{2,1,0:T(8,128)(2,1)}, u32[]{:S(2)}, u32[]{:S(2)}) collective-permute-start(bf16[3,64,512]{2,1,0:T(8,128)(2,1)} %get-tuple-element.241), channel_id=1, source_target_pairs={{0,16},{2,18},{4,20},{6,22},{8,24},{10,26},{12,28},{14,30},{16,0},... | collective-permute-start | bytes 589832 | tf_op jit(solution)/shard_map/ppermute | solution.py:975
  456.5 51.0 %collective-permute-start.19 = (bf16[1,512,1024]{2,1,0:T(8,128)(2,1)}, bf16[1,512,1024]{2,1,0:T(8,128)(2,1)}, u32[]{:S(2)}, u32[]{:S(2)}) collective-permute-start(bf16[1,512,1024]{2,1,0:T(8,128)(2,1)} %get-tuple-element.143), channel_id=1, source_target_pairs={{0,1},{1,0},{2,3},{3,2},{4,5},{5,4},{6,7},{7,6},{8,9},{9,8},{10,11... | collective-permute-start | bytes 3145736 | tf_op jit(solution)/shard_map/ppermute | solution.py:887
  461.0 33.7 %collective-permute-start.15 = (bf16[3,4,1,64,512]{4,3,0,2,1:T(8,128)(2,1)}, bf16[3,4,1,64,512]{4,3,0,2,1:T(8,128)(2,1)}, u32[]{:S(2)}, u32[]{:S(2)}) collective-permute-start(bf16[3,4,1,64,512]{4,3,0,2,1:T(8,128)(2,1)} %bitcast.193), channel_id=1, source_target_pairs={{0,4},{2,6},{4,0},{6,2},{8,12},{10,14},{12,8},{14,10},{16,20},{18,... | collective-permute-start | bytes 2359304 | tf_op jit(solution)/shard_map/ppermute | solution.py:949
  474.8 32.7 %collective-permute-start.20 = (bf16[1,512,1024]{2,1,0:T(8,128)(2,1)}, bf16[1,512,1024]{2,1,0:T(8,128)(2,1)}, u32[]{:S(2)}, u32[]{:S(2)}) collective-permute-start(bf16[1,512,1024]{2,1,0:T(8,128)(2,1)} %get-tuple-element.148), channel_id=1, source_target_pairs={{0,1},{1,0},{2,3},{3,2},{4,5},{5,4},{6,7},{7,6},{8,9},{9,8},{10,11... | collective-permute-start | bytes 3145736 | tf_op jit(solution)/shard_map/ppermute | solution.py:887
  482.1 12.0 %copy-start.12 = (f32[1,1,1024]{2,1,0:T(1,128)S(1)}, f32[1,1,1024]{2,1,0:T(1,128)}, u32[]{:S(2)}) copy-start(f32[1,1,1024]{2,1,0:T(1,128)} %get-tuple-element.161) | copy-start | bytes 12292
  482.1 42.7 %collective-permute-start.24 = (bf16[64,6144]{1,0:T(8,128)(2,1)}, bf16[64,6144]{1,0:T(8,128)(2,1)}, u32[]{:S(2)}, u32[]{:S(2)}) collective-permute-start(bf16[64,6144]{1,0:T(8,128)(2,1)} %fusion.20), channel_id=1, source_target_pairs={{0,1},{1,0},{2,3},{3,2},{4,5},{5,4},{6,7},{7,6},{8,9},{9,8},{10,11... | collective-permute-start | bytes 2359304 | tf_op jit(solution)/shard_map/ppermute | solution.py:887
  496.1 10.2 %copy-start.13 = (f32[1,1,1024]{2,1,0:T(1,128)S(1)}, f32[1,1,1024]{2,1,0:T(1,128)}, u32[]{:S(2)}) copy-start(f32[1,1,1024]{2,1,0:T(1,128)} %get-tuple-element.163) | copy-start | bytes 12292
  496.1 11.1 %copy-start.4 = (f32[2,2048]{1,0:T(2,128)S(1)}, f32[2,2048]{1,0:T(2,128)}, u32[]{:S(2)}) copy-start(f32[2,2048]{1,0:T(2,128)} %copy-done.3) | copy-start | bytes 49156
  508.3 16.4 %all-to-all-start = ((f32[32,1,704]{2,1,0:T(1,128)}), f32[32,1,704]{2,1,0:T(1,128)S(1)}, u32[]{:S(2)}, u32[]{:S(2)}) async-start(f32[32,1,704]{2,1,0:T(1,128)} %all_to_all.8), calls=%async_computation.2 | async-start | bytes 196608 | tf_op jit(solution)/shard_map/all_to_all | solution.py:1075
  513.9 11.6 %collective-permute-start.21 = (bf16[3,64,512]{2,1,0:T(8,128)(2,1)}, bf16[3,64,512]{2,1,0:T(8,128)(2,1)S(1)}, u32[]{:S(2)}, u32[]{:S(2)}) collective-permute-start(bf16[3,64,512]{2,1,0:T(8,128)(2,1)} %get-tuple-element.236), channel_id=1, source_target_pairs={{0,8},{2,10},{4,12},{6,14},{8,0},{10,2},{12,4},{14,6},{16,24},{18,... | collective-permute-start | bytes 589832 | tf_op jit(solution)/shard_map/ppermute | solution.py:975
  515.7 12.8 %collective-permute-start.23 = (bf16[3,64,512]{2,1,0:T(8,128)(2,1)}, bf16[3,64,512]{2,1,0:T(8,128)(2,1)}, u32[]{:S(2)}, u32[]{:S(2)}) collective-permute-start(bf16[3,64,512]{2,1,0:T(8,128)(2,1)} %get-tuple-element.237), channel_id=1, source_target_pairs={{0,24},{2,26},{4,28},{6,30},{8,16},{10,18},{12,20},{14,22},{16,8},... | collective-permute-start | bytes 589832 | tf_op jit(solution)/shard_map/ppermute | solution.py:975
  518.0 18.2 %collective-permute-start.22 = (bf16[3,64,512]{2,1,0:T(8,128)(2,1)}, bf16[3,64,512]{2,1,0:T(8,128)(2,1)}, u32[]{:S(2)}, u32[]{:S(2)}) collective-permute-start(bf16[3,64,512]{2,1,0:T(8,128)(2,1)} %get-tuple-element.238), channel_id=1, source_target_pairs={{0,16},{2,18},{4,20},{6,22},{8,24},{10,26},{12,28},{14,30},{16,0},... | collective-permute-start | bytes 589832 | tf_op jit(solution)/shard_map/ppermute | solution.py:975
  523.1 17.6 %copy-start.1 = (bf16[2,64,2048]{2,1,0:T(8,128)(2,1)S(1)}, bf16[2,64,2048]{2,1,0:T(8,128)(2,1)}, u32[]{:S(2)}) copy-start(bf16[2,64,2048]{2,1,0:T(8,128)(2,1)} %reduce-scatter.3.cloned.1.call-done) | copy-start | bytes 1572868
Sparse Core Ops, SparseCore 0:
  25.9 46.9 all-gather.4
  75.6 36.7 all-gather.6
  115.2 49.6 all-gather.10
  167.5 49.1 all-gather.8
  226.1 107.1 reduce-scatter.2
  337.2 118.8 reduce-scatter.4
